TPU v7x, 128 devices: a whole 4x4x4 slice. The times are simulated.
128 devices in a mesh: lat: 4 (over y_lo, core), lon: 32 (over z, x, y_hi).
Axes of the slice: x: 4, y: 4 (y_hi: 2, y_lo: 2; y = y_hi * 2 + y_lo), z: 4, core: 2. Of those that a mesh axis runs over, the one named last changes fastest.
Arguments:
- observation_residual: bfloat16 [128, 262144], P(None, ('lat', 'lon')), may hold values from -6 to 6
- obs_index: int32 [2, 262144], P(None, ('lat', 'lon')), may hold values from 0 to 8191, as said below
- obs_count: int32 [1, 16384], P(None, ('lat', 'lon')), may hold values from 12 to 16, as said below
- obs_weight: float32 [128], replicated, may hold values from 0.3 to 3
- jacobian: bfloat16 [128, 8, 137], replicated, may hold values from -0.5 to 0.5
- decoder: bfloat16 [137, 128], replicated, may hold values from -0.5 to 0.5
- conv_weight: bfloat16 [4, 3, 128, 128], replicated, may hold values from -0.3125 to 0.3125
- gates: bfloat16 [4, 128, 2048, 512], P(None, None, 'lon', 'lat'), may hold values from 0.049804688 to 1.09375
- encoder: bfloat16 [128, 137], replicated, may hold values from -0.5 to 0.5
Outputs:
- state_grad: float32 [137, 2048, 512], P(None, 'lon', 'lat')
Inputs may be any that keep to these rules, and one draw needn't show every extreme that they name: `obs_index`: row 0 is a column within the destination tile, longitude offset * 128 + latitude offset, up to 8191; row 1 is a Jacobian block below 8. `obs_count`: slots of a pair at or after its count are unused. In every draw some tiles receive 16 from every sender.
All inputs are finite; a program needn't handle non-finite values.
Results may differ from a plain program's by a relative error of at most 0.0056.
Values may be sent and summed in bfloat16 or wider, within the bound.
No kernel may reach another device: no remote copies, remote signals or barrier semaphores. Data moves between devices by JAX's collectives and lax.ppermute only.
A program may use at most 128 MiB of HBM per device.

v0:
```python
import jax
import jax.numpy as jnp
from jax import lax
from jax.sharding import PartitionSpec as P


def with_halo(block, sides, width):
    for axis, dim in sides:
        count = lax.axis_size(axis)
        forward = [(i, i + 1) for i in range(count - 1)]
        forward.append((count - 1, 0))
        backward = [(target, source) for source, target in forward]
        low = lax.ppermute(
            lax.slice_in_dim(block, block.shape[dim] - width, None, axis=dim), axis, forward
        )
        high = lax.ppermute(lax.slice_in_dim(block, 0, width, axis=dim), axis, backward)
        block = jnp.concatenate([low, block, high], axis=dim)
    return block


def project(resid, kinds, counts, obs_weight, jacobian, slot_index):
    channels, kind_count, vertical_levels = jacobian.shape
    senders = counts.shape[0]
    slot_grid = (
        jnp.arange(senders * slot_index, dtype=jnp.int32).reshape(senders, slot_index) % slot_index
    )
    valid = (slot_grid < counts[:, None]).reshape(-1)
    weighted = jnp.where(
        valid[None, :], obs_weight[:, None] * resid.astype(jnp.float32), 0.0
    ).astype(jnp.bfloat16)
    jac_flat = jacobian.reshape(channels, kind_count * vertical_levels)
    every_kind = lax.dot_general(
        jac_flat, weighted, (((0,), (0,)), ((), ())), preferred_element_type=jnp.float32
    )
    every_kind = every_kind.reshape(kind_count, vertical_levels, -1)
    picked = (kinds[None, :] == jnp.arange(kind_count, dtype=jnp.int32)[:, None]).astype(
        jnp.float32
    )
    return jnp.sum(every_kind * picked[:, None, :], axis=0).astype(jnp.bfloat16)


def per_device(
    observation_residual,
    obs_index,
    obs_count,
    obs_weight,
    jacobian,
    decoder,
    conv_weight,
    gates,
    encoder,
):
    lat_count = lax.axis_size("lat")
    lon_count = lax.axis_size("lon")
    device_count = lat_count * lon_count
    slot_count = observation_residual.shape[1]
    slot_index = slot_count // device_count
    vertical_levels = jacobian.shape[2]
    layers_n, width, tile_lon, tile_lat = gates.shape
    cell_total = tile_lon * tile_lat
    resid_in, index_in, count_in = (
        lax.all_to_all(
            observation_residual, ("lat", "lon"), split_axis=1, concat_axis=1, tiled=True
        ),
        lax.all_to_all(obs_index, ("lat", "lon"), split_axis=1, concat_axis=1, tiled=True),
        lax.all_to_all(obs_count, ("lat", "lon"), split_axis=1, concat_axis=1, tiled=True),
    )
    incr_in = project(resid_in, index_in[1], count_in[0], obs_weight, jacobian, slot_index)
    cells_in = index_in[0:1]
    block_tensor = 512
    cell_ids = jnp.arange(cell_total, dtype=jnp.int32)

    def accumulate_block(step, total):
        incr_part = lax.dynamic_slice_in_dim(incr_in, step * block_tensor, block_tensor, 1)
        cell_part = lax.dynamic_slice_in_dim(cells_in[0], step * block_tensor, block_tensor, 0)
        onehot = (cell_part[:, None] == cell_ids[None, :]).astype(jnp.bfloat16)
        return total + jnp.dot(incr_part, onehot, preferred_element_type=jnp.float32)

    column_grad = lax.fori_loop(
        0,
        slot_count // block_tensor,
        accumulate_block,
        jnp.zeros((vertical_levels, cell_total), jnp.float32),
    )
    hidden = lax.dot_general(
        decoder,
        column_grad.astype(jnp.bfloat16),
        (((0,), (0,)), ((), ())),
        preferred_element_type=jnp.float32,
    )
    for layer in reversed(range(layers_n)):
        field = hidden.astype(jnp.bfloat16).reshape(width, tile_lon, tile_lat)
        padded = with_halo(field, (("lon", 1),), 4)
        back = jnp.zeros((width, cell_total), jnp.float32)
        for tap in range(3):
            offset = 8 - 4 * tap
            window = padded[:, offset : offset + tile_lon, :].reshape(width, cell_total)
            back = back + lax.dot_general(
                conv_weight[layer, tap],
                window,
                (((0,), (0,)), ((), ())),
                preferred_element_type=jnp.float32,
            )
        hidden = hidden + gates[layer].reshape(width, cell_total) * back
    state_grad = column_grad + lax.dot_general(
        encoder,
        hidden.astype(jnp.bfloat16),
        (((0,), (0,)), ((), ())),
        preferred_element_type=jnp.float32,
    )
    return state_grad.reshape(vertical_levels, tile_lon, tile_lat)


def solution(mesh):
    return jax.shard_map(
        per_device,
        mesh=mesh,
        in_specs=(
            P(None, ("lat", "lon")),
            P(None, ("lat", "lon")),
            P(None, ("lat", "lon")),
            P(),
            P(),
            P(),
            P(),
            P(None, None, "lon", "lat"),
            P(),
        ),
        out_specs=P(None, "lon", "lat"),
        check_vma=False,
    )
```

profile of v0, /device:TPU:0, one launch (start us, length us, event | category | flops | bytes accessed | tf_op | source)
XLA Modules:
  0.0 219.7 jit_solution(14997991868617479300)
XLA Ops:
  0.0 1.4 copy.28
  1.4 11.2 %all-to-all-start = ((s32[1,128,1]{2,0,1:T(1,128)}), s32[1,128,1]{2,0,1:T(1,128)S(1)}, u32[]{:S(2)}, u32[]{:S(2)}) async-start(s32[1,128,1]{2,0,1:T(1,128)} %copy.28), calls=%async_computation | async-start | bytes 131072 | tf_op jit(solution)/shard_map/all_to_all | solution.py:66
  12.6 2.1 copy.29
  14.7 1.0 copy.30
  15.8 10.2 %slice_convert_fusion = (f32[1,128,64,128]{3,2,1,0:T(8,128)}, f32[1,128,64,128]{3,2,1,0:T(8,128)}, f32[1,128,64,128]{3,2,1,0:T(8,128)}, f32[1,128,64,128]{3,2,1,0:T(8,128)}) fusion(bf16[4,128,64,128]{3,2,1,0:T(8,128)(2,1)} %param.18), kind=kLoop, calls=%fused_computation.43 | loop fusion | flops 4194304 | bytes 25165824 | tf_op jit(solution)/shard_map/convert_element_type | solution.py:104
  26.1 0.8 copy.31
  26.9 5.4 %copy.32 = f32[1,128,64,128]{1,3,2,0:T(8,128)} copy(f32[1,128,64,128]{3,2,1,0:T(8,128)} %get-tuple-element.129) | data formatting | bytes 8388608 | tf_op jit(solution)/shard_map/convert_element_type | solution.py:104
  32.3 5.4 %copy.33 = f32[1,128,64,128]{1,3,2,0:T(8,128)} copy(f32[1,128,64,128]{3,2,1,0:T(8,128)} %get-tuple-element.128) | data formatting | bytes 8388608 | tf_op jit(solution)/shard_map/convert_element_type | solution.py:104
  37.7 5.4 %copy.34 = f32[1,128,64,128]{1,3,2,0:T(8,128)} copy(f32[1,128,64,128]{3,2,1,0:T(8,128)} %get-tuple-element.130) | data formatting | bytes 8388608 | tf_op jit(solution)/shard_map/convert_element_type | solution.py:104
  43.1 5.4 %copy.35 = f32[1,128,64,128]{1,3,2,0:T(8,128)} copy(f32[1,128,64,128]{3,2,1,0:T(8,128)} %get-tuple-element.127) | data formatting | bytes 8388608 | tf_op jit(solution)/shard_map/convert_element_type | solution.py:104
  48.6 9.8 %all-to-all-start.2 = ((s32[2,128,16]{2,0,1:T(2,128)}), s32[2,128,16]{2,0,1:T(2,128)S(1)}, u32[]{:S(2)}, u32[]{:S(2)}) async-start(s32[2,128,16]{2,0,1:T(2,128)} %copy.31), calls=%async_computation.2 | async-start | bytes 262144 | tf_op jit(solution)/shard_map/all_to_all | solution.py:65
  58.3 2.4 %reduce = s32[128]{0:T(128)S(1)} reduce(s32[1,128,1]{2,0,1:T(1,128)S(1)} %all-to-all-done, s32[]{:T(128)} %constant.47.clone.1), dimensions={0,2}, to_apply=%all_to_all.19.reduce_sub_computation | reduce | bytes 1028 | tf_op jit(solution)/shard_map/all_to_all | solution.py:66
  60.8 6.8 %all-to-all-done.2 = s32[2,128,16]{2,0,1:T(2,128)S(1)} async-done(((s32[2,128,16]{2,0,1:T(2,128)}), s32[2,128,16]{2,0,1:T(2,128)S(1)}, u32[]{:S(2)}, u32[]{:S(2)}) %all-to-all-start.2) | async-done | bytes 16416 | tf_op jit(solution)/shard_map/all_to_all | solution.py:65
  67.6 5.2 %all-to-all-start.1 = ((bf16[128,128,16]{0,2,1:T(8,128)(2,1)}), bf16[128,128,16]{0,2,1:T(8,128)(2,1)S(1)}, u32[]{:S(2)}, u32[]{:S(2)}) async-start(bf16[128,128,16]{0,2,1:T(8,128)(2,1)} %bitcast.1), calls=%async_computation.1 | async-start | bytes 1048576 | tf_op jit(solution)/shard_map/all_to_all | solution.py:62
  73.3 12.2 %all-to-all-done.1 = bf16[128,128,16]{0,2,1:T(8,128)(2,1)S(1)} async-done(((bf16[128,128,16]{0,2,1:T(8,128)(2,1)}), bf16[128,128,16]{0,2,1:T(8,128)(2,1)S(1)}, u32[]{:S(2)}, u32[]{:S(2)}) %all-to-all-start.1) | async-done | bytes 524320 | tf_op jit(solution)/shard_map/all_to_all | solution.py:62
  85.9 4.9 %convolution_bitcast_fusion.2 = f32[1096,2048]{1,0:T(8,128)} fusion(bf16[128,2048]{0,1:T(8,128)(2,1)S(1)} %bitcast.144, bf16[128,1096]{0,1:T(8,128)(2,1)S(1)} %reshape.139), kind=kOutput, calls=%fused_computation.33 | convolution fusion | flops 574619648 | bytes 9783296 | tf_op jit(solution)/shard_map/dot_general | solution.py:32
  90.8 8.3 %reshape.140 = f32[8,137,2048]{2,1,0:T(8,128)} reshape(f32[1096,2048]{1,0:T(8,128)} %convolution_bitcast_fusion.2) | data formatting | bytes 17956864 | tf_op jit(solution)/shard_map/reshape | solution.py:35
  99.1 4.9 %multiply_reduce_fusion = bf16[137,2048]{1,0:T(8,128)(2,1)S(1)} fusion(f32[8,137,2048]{2,1,0:T(8,128)} %reshape.140, f32[8,2048]{1,0:T(8,128)S(1)} %fusion.28), kind=kLoop, calls=%fused_computation.32 | loop fusion | flops 4208640 | bytes 9605120 | tf_op jit(solution)/shard_map/reduce_sum | solution.py:39
  104.0 31.8 %while.14 = (s32[]{:T(128)}, f32[137,8192]{1,0:T(8,128)}, bf16[137,2048]{1,0:T(8,128)(2,1)S(1)}, s32[1,2048]{1,0:T(1,128)S(1)}, s32[]{:T(128)}, /*index=5*/s32[]{:T(128)}, s32[]{:T(128)}, s32[]{:T(128)}) while((s32[]{:T(128)}, f32[137,8192]{1,0:T(8,128)}, bf16[137,2048]{1,0:T(8,128)(2,1)S(1)}, s32[1,2048]{1,0:T(1,128)S(1)}, ...), condition=%wide.region_2.3_spmd.clone, body=%wide.region_1.2_spmd.clone.sunk | while | flops 1155678208 | bytes 9132189 | solution.py:79
  104.1 6.2 %fusion.90 = f32[137,8192]{1,0:T(8,128)} fusion(s32[512]{0:T(512)S(1)} %bitcast.145, f32[137,8192]{1,0:T(8,128)} %get-tuple-element.189, pred[]{:T(512)S(6)} %compare.7, bf16[137,2048]{1,0:T(8,128)(2,1)S(1)} %get-tuple-element.198, s32[]{:T(128)S(6)} %select_n.32), kind=kOutput, calls=%fused_computation.3.clone.1 | convolution fusion | flops 1155678208 | bytes 9127941 | tf_op jit(solution)/shard_map/while/body/eval_jaxpr/dot_general | solution.py:77
  110.3 8.5 %fusion.90 = f32[137,8192]{1,0:T(8,128)} fusion(s32[512]{0:T(512)S(1)} %bitcast.145, f32[137,8192]{1,0:T(8,128)} %get-tuple-element.189, pred[]{:T(512)S(6)} %compare.7, bf16[137,2048]{1,0:T(8,128)(2,1)S(1)} %get-tuple-element.198, s32[]{:T(128)S(6)} %select_n.32), kind=kOutput, calls=%fused_computation.3.clone.1 | convolution fusion | flops 1155678208 | bytes 9127941 | tf_op jit(solution)/shard_map/while/body/eval_jaxpr/dot_general | solution.py:77
  118.8 8.5 %fusion.90 = f32[137,8192]{1,0:T(8,128)} fusion(s32[512]{0:T(512)S(1)} %bitcast.145, f32[137,8192]{1,0:T(8,128)} %get-tuple-element.189, pred[]{:T(512)S(6)} %compare.7, bf16[137,2048]{1,0:T(8,128)(2,1)S(1)} %get-tuple-element.198, s32[]{:T(128)S(6)} %select_n.32), kind=kOutput, calls=%fused_computation.3.clone.1 | convolution fusion | flops 1155678208 | bytes 9127941 | tf_op jit(solution)/shard_map/while/body/eval_jaxpr/dot_general | solution.py:77
  127.4 8.5 %fusion.90 = f32[137,8192]{1,0:T(8,128)} fusion(s32[512]{0:T(512)S(1)} %bitcast.145, f32[137,8192]{1,0:T(8,128)} %get-tuple-element.189, pred[]{:T(512)S(6)} %compare.7, bf16[137,2048]{1,0:T(8,128)(2,1)S(1)} %get-tuple-element.198, s32[]{:T(128)S(6)} %select_n.32), kind=kOutput, calls=%fused_computation.3.clone.1 | convolution fusion | flops 1155678208 | bytes 9127941 | tf_op jit(solution)/shard_map/while/body/eval_jaxpr/dot_general | solution.py:77
  135.9 3.7 %fusion.67 = (bf16[128,8192]{0,1:T(8,128)(2,1)S(1)}, f32[128,8192]{0,1:T(8,128)S(1)}) fusion(bf16[137,128]{1,0:T(8,128)(2,1)S(1)} %copy-done, f32[137,8192]{1,0:T(8,128)} %get-tuple-element.99), kind=kOutput, calls=%fused_computation.93 | convolution fusion | flops 289480704 | bytes 10815744 | tf_op jit(solution)/shard_map/dot_general | solution.py:85
  139.7 2.0 collective-permute-start
  141.6 1.6 collective-permute-start.1
  143.9 3.0 %collective-permute-done = bf16[128,4,128]{0,2,1:T(8,128)(2,1)S(1)} collective-permute-done((bf16[128,4,128]{0,2,1:T(8,128)(2,1)S(1)}, bf16[128,4,128]{0,2,1:T(8,128)(2,1)S(1)}, u32[]{:S(2)}, u32[]{:S(2)}) %collective-permute-start) | collective-permute-done | bytes 131104 | tf_op jit(solution)/shard_map/ppermute | solution.py:16
  147.0 5.8 %collective-permute-done.1 = bf16[128,4,128]{0,2,1:T(8,128)(2,1)S(1)} collective-permute-done((bf16[128,4,128]{0,2,1:T(8,128)(2,1)S(1)}, bf16[128,4,128]{0,2,1:T(8,128)(2,1)S(1)}, u32[]{:S(2)}, u32[]{:S(2)}) %collective-permute-start.1) | collective-permute-done | bytes 131104 | tf_op jit(solution)/shard_map/ppermute | solution.py:13
  153.8 1.5 copy-done.4
  155.3 1.3 fusion.68
  157.2 3.0 %collective-permute-start.3 = (bf16[128,4,128]{0,2,1:T(8,128)(2,1)S(1)}, bf16[128,4,128]{0,2,1:T(8,128)(2,1)S(1)}, u32[]{:S(2)}, u32[]{:S(2)}) collective-permute-start(bf16[128,4,128]{0,2,1:T(8,128)(2,1)S(1)} %get-tuple-element.142), channel_id=1, source_target_pairs={{0,1},{1,2},{2,3},{3,4},{4,5},{5,6},{6,7},{7,8},{8,9},{9,10},{10,1... | collective-permute-start | bytes 393224 | tf_op jit(solution)/shard_map/ppermute | solution.py:13
  160.9 3.7 %collective-permute-done.2 = bf16[128,4,128]{0,2,1:T(8,128)(2,1)S(1)} collective-permute-done((bf16[128,4,128]{0,2,1:T(8,128)(2,1)S(1)}, bf16[128,4,128]{0,2,1:T(8,128)(2,1)S(1)}, u32[]{:S(2)}, u32[]{:S(2)}) %collective-permute-start.2) | collective-permute-done | bytes 131104 | tf_op jit(solution)/shard_map/ppermute | solution.py:16
  164.6 3.3 %collective-permute-done.3 = bf16[128,4,128]{0,2,1:T(8,128)(2,1)S(1)} collective-permute-done((bf16[128,4,128]{0,2,1:T(8,128)(2,1)S(1)}, bf16[128,4,128]{0,2,1:T(8,128)(2,1)S(1)}, u32[]{:S(2)}, u32[]{:S(2)}) %collective-permute-start.3) | collective-permute-done | bytes 131104 | tf_op jit(solution)/shard_map/ppermute | solution.py:13
  169.0 1.5 copy-done.3
  170.5 1.3 fusion.69
  171.9 3.5 %collective-permute-start.5 = (bf16[128,4,128]{0,2,1:T(8,128)(2,1)S(1)}, bf16[128,4,128]{0,2,1:T(8,128)(2,1)S(1)}, u32[]{:S(2)}, u32[]{:S(2)}) collective-permute-start(bf16[128,4,128]{0,2,1:T(8,128)(2,1)S(1)} %get-tuple-element.138), channel_id=1, source_target_pairs={{0,1},{1,2},{2,3},{3,4},{4,5},{5,6},{6,7},{7,8},{8,9},{9,10},{10,1... | collective-permute-start | bytes 393224 | tf_op jit(solution)/shard_map/ppermute | solution.py:13
  176.1 2.3 %collective-permute-done.4 = bf16[128,4,128]{0,2,1:T(8,128)(2,1)S(1)} collective-permute-done((bf16[128,4,128]{0,2,1:T(8,128)(2,1)S(1)}, bf16[128,4,128]{0,2,1:T(8,128)(2,1)S(1)}, u32[]{:S(2)}, u32[]{:S(2)}) %collective-permute-start.4) | collective-permute-done | bytes 131104 | tf_op jit(solution)/shard_map/ppermute | solution.py:16
  178.3 4.3 %collective-permute-done.5 = bf16[128,4,128]{0,2,1:T(8,128)(2,1)S(1)} collective-permute-done((bf16[128,4,128]{0,2,1:T(8,128)(2,1)S(1)}, bf16[128,4,128]{0,2,1:T(8,128)(2,1)S(1)}, u32[]{:S(2)}, u32[]{:S(2)}) %collective-permute-start.5) | collective-permute-done | bytes 131104 | tf_op jit(solution)/shard_map/ppermute | solution.py:13
  183.7 1.5 copy-done.2
  185.2 3.3 %fusion.70 = (bf16[128,8192]{0,1:T(8,128)(2,1)S(1)}, f32[128,8192]{0,1:T(8,128)}) fusion(f32[128,8192]{0,1:T(8,128)S(1)} %get-tuple-element.152, f32[128,8192]{0,1:T(8,128)S(1)} %bitcast.132, f32[8192,128]{1,0:T(8,128)S(1)} %fusion.35, f32[8192,128]{1,0:T(8,128)S(1)} %fusion.37, bf16[128,8192]{0,1:T(8,128)(2,1)S(1)} %bitcast.142, ...), kind=kOutput, calls=%fused_computation.96 | convolution fusion | flops 273678336 | bytes 25198592 | tf_op jit(solution)/shard_map/dot_general | solution.py:98
  188.6 3.5 %collective-permute-start.7 = (bf16[128,4,128]{0,2,1:T(8,128)(2,1)S(1)}, bf16[128,4,128]{0,2,1:T(8,128)(2,1)S(1)}, u32[]{:S(2)}, u32[]{:S(2)}) collective-permute-start(bf16[128,4,128]{0,2,1:T(8,128)(2,1)S(1)} %get-tuple-element.134), channel_id=1, source_target_pairs={{0,1},{1,2},{2,3},{3,4},{4,5},{5,6},{6,7},{7,8},{8,9},{9,10},{10,1... | collective-permute-start | bytes 393224 | tf_op jit(solution)/shard_map/ppermute | solution.py:13
  192.1 2.7 %fusion.31 = f32[8192,128]{1,0:T(8,128)} fusion(bf16[128,8192]{0,1:T(8,128)(2,1)S(1)} %get-tuple-element.153, bf16[4,3,128,128]{3,2,1,0:T(8,128)(2,1)S(1)} %copy-done.5), kind=kOutput, calls=%fused_computation.59 | convolution fusion | flops 268435456 | bytes 6324224 | tf_op jit(solution)/shard_map/dot_general | solution.py:98
  194.8 1.7 collective-permute-done.6
  196.5 3.2 %collective-permute-done.7 = bf16[128,4,128]{0,2,1:T(8,128)(2,1)S(1)} collective-permute-done((bf16[128,4,128]{0,2,1:T(8,128)(2,1)S(1)}, bf16[128,4,128]{0,2,1:T(8,128)(2,1)S(1)}, u32[]{:S(2)}, u32[]{:S(2)}) %collective-permute-start.7) | collective-permute-done | bytes 131104 | tf_op jit(solution)/shard_map/ppermute | solution.py:13
  200.0 2.8 %fusion.29 = f32[8192,128]{1,0:T(8,128)} fusion(bf16[128,8192]{0,1:T(8,128)(2,1)S(1)} %bitcast.139, bf16[4,3,128,128]{3,2,1,0:T(8,128)(2,1)S(1)} %copy-done.5), kind=kOutput, calls=%fused_computation.57 | convolution fusion | flops 268435456 | bytes 6324224 | tf_op jit(solution)/shard_map/dot_general | solution.py:98
  202.8 11.0 %fusion.7 = f32[137,8192]{1,0:T(8,128)} fusion(f32[137,8192]{1,0:T(8,128)} %get-tuple-element.99, bf16[128,137]{0,1:T(8,128)(2,1)S(1)} %copy-done.6, f32[128,8192]{0,1:T(8,128)} %get-tuple-element.154, f32[128,8192]{0,1:T(8,128)} %bitcast.135, f32[8192,128]{1,0:T(8,128)} %fusion.29, f32[8192,128]{1,0:T(8,128)} %fusion.31, ...), kind=kOutput, calls=%fused_computation.9 | convolution fusion | flops 562110464 | bytes 27922432 | tf_op jit(solution)/shard_map/dot_general | solution.py:105
  213.8 3.2 %copy.36 = f32[18,8,64,128]{3,2,1,0:T(8,128)S(1)} copy(f32[18,8,64,128]{3,1,2,0:T(8,128)} %bitcast.130) | data formatting | bytes 9437184
  216.9 2.8 %slice.159 = f32[137,64,128]{2,1,0:T(8,128)} slice(f32[144,64,128]{2,1,0:T(8,128)S(1)} %bitcast.131), slice={[0:137], [0:64], [0:128]} | slice | bytes 8978432 | tf_op jit(solution)/shard_map/reshape | solution.py:111
  (46 shorter events, 7.6 us)
Async XLA Ops:
  0.0 135.9 %copy-start = (bf16[137,128]{1,0:T(8,128)(2,1)S(1)}, bf16[137,128]{1,0:T(8,128)(2,1)}, u32[]{:S(2)}) copy-start(bf16[137,128]{1,0:T(8,128)(2,1)} %param.16) | copy-start | bytes 105220
  1.4 47.2 %all-to-all-start = ((s32[1,128,1]{2,0,1:T(1,128)}), s32[1,128,1]{2,0,1:T(1,128)S(1)}, u32[]{:S(2)}, u32[]{:S(2)}) async-start(s32[1,128,1]{2,0,1:T(1,128)} %copy.28), calls=%async_computation | async-start | bytes 131072 | tf_op jit(solution)/shard_map/all_to_all | solution.py:66
  15.8 10.2 %copy-start.7 = (s32[2,2048]{1,0:T(2,128)S(1)}, s32[2,2048]{1,0:T(2,128)}, u32[]{:S(2)}) copy-start(s32[2,2048]{1,0:T(2,128)} %param.12) | copy-start | bytes 49156
  43.1 42.5 %copy-start.8 = (f32[128]{0:T(128)S(1)}, f32[128]{0:T(128)}, u32[]{:S(2)}) copy-start(f32[128]{0:T(128)} %param.14) | copy-start | bytes 1540
  48.6 19.0 %all-to-all-start.2 = ((s32[2,128,16]{2,0,1:T(2,128)}), s32[2,128,16]{2,0,1:T(2,128)S(1)}, u32[]{:S(2)}, u32[]{:S(2)}) async-start(s32[2,128,16]{2,0,1:T(2,128)} %copy.31), calls=%async_computation.2 | async-start | bytes 262144 | tf_op jit(solution)/shard_map/all_to_all | solution.py:65
  67.6 18.0 %all-to-all-start.1 = ((bf16[128,128,16]{0,2,1:T(8,128)(2,1)}), bf16[128,128,16]{0,2,1:T(8,128)(2,1)S(1)}, u32[]{:S(2)}, u32[]{:S(2)}) async-start(bf16[128,128,16]{0,2,1:T(8,128)(2,1)} %bitcast.1), calls=%async_computation.1 | async-start | bytes 1048576 | tf_op jit(solution)/shard_map/all_to_all | solution.py:62
  135.9 7.4 %copy-start.5 = (bf16[4,3,128,128]{3,2,1,0:T(8,128)(2,1)S(1)}, bf16[4,3,128,128]{3,2,1,0:T(8,128)(2,1)}, u32[]{:S(2)}) copy-start(bf16[4,3,128,128]{3,2,1,0:T(8,128)(2,1)} %param.17) | copy-start | bytes 1179652
  139.7 7.3 %collective-permute-start = (bf16[128,4,128]{0,2,1:T(8,128)(2,1)S(1)}, bf16[128,4,128]{0,2,1:T(8,128)(2,1)S(1)}, u32[]{:S(2)}, u32[]{:S(2)}) collective-permute-start(bf16[128,4,128]{0,2,1:T(8,128)(2,1)S(1)} %get-tuple-element.145), channel_id=1, source_target_pairs={{1,0},{2,1},{3,2},{4,3},{5,4},{6,5},{7,6},{8,7},{9,8},{10,9},{11,1... | collective-permute-start | bytes 393224 | tf_op jit(solution)/shard_map/ppermute | solution.py:16
  141.6 11.2 %collective-permute-start.1 = (bf16[128,4,128]{0,2,1:T(8,128)(2,1)S(1)}, bf16[128,4,128]{0,2,1:T(8,128)(2,1)S(1)}, u32[]{:S(2)}, u32[]{:S(2)}) collective-permute-start(bf16[128,4,128]{0,2,1:T(8,128)(2,1)S(1)} %get-tuple-element.146), channel_id=1, source_target_pairs={{0,1},{1,2},{2,3},{3,4},{4,5},{5,6},{6,7},{7,8},{8,9},{9,10},{10,1... | collective-permute-start | bytes 393224 | tf_op jit(solution)/shard_map/ppermute | solution.py:13
  153.2 2.2 copy-start.4
  156.7 7.9 %collective-permute-start.2 = (bf16[128,4,128]{0,2,1:T(8,128)(2,1)S(1)}, bf16[128,4,128]{0,2,1:T(8,128)(2,1)S(1)}, u32[]{:S(2)}, u32[]{:S(2)}) collective-permute-start(bf16[128,4,128]{0,2,1:T(8,128)(2,1)S(1)} %get-tuple-element.141), channel_id=1, source_target_pairs={{1,0},{2,1},{3,2},{4,3},{5,4},{6,5},{7,6},{8,7},{9,8},{10,9},{11,1... | collective-permute-start | bytes 393224 | tf_op jit(solution)/shard_map/ppermute | solution.py:16
  157.2 10.7 %collective-permute-start.3 = (bf16[128,4,128]{0,2,1:T(8,128)(2,1)S(1)}, bf16[128,4,128]{0,2,1:T(8,128)(2,1)S(1)}, u32[]{:S(2)}, u32[]{:S(2)}) collective-permute-start(bf16[128,4,128]{0,2,1:T(8,128)(2,1)S(1)} %get-tuple-element.142), channel_id=1, source_target_pairs={{0,1},{1,2},{2,3},{3,4},{4,5},{5,6},{6,7},{7,8},{8,9},{9,10},{10,1... | collective-permute-start | bytes 393224 | tf_op jit(solution)/shard_map/ppermute | solution.py:13
  168.3 2.2 copy-start.3
  171.8 6.5 %collective-permute-start.4 = (bf16[128,4,128]{0,2,1:T(8,128)(2,1)S(1)}, bf16[128,4,128]{0,2,1:T(8,128)(2,1)S(1)}, u32[]{:S(2)}, u32[]{:S(2)}) collective-permute-start(bf16[128,4,128]{0,2,1:T(8,128)(2,1)S(1)} %get-tuple-element.137), channel_id=1, source_target_pairs={{1,0},{2,1},{3,2},{4,3},{5,4},{6,5},{7,6},{8,7},{9,8},{10,9},{11,1... | collective-permute-start | bytes 393224 | tf_op jit(solution)/shard_map/ppermute | solution.py:16
  171.9 10.8 %collective-permute-start.5 = (bf16[128,4,128]{0,2,1:T(8,128)(2,1)S(1)}, bf16[128,4,128]{0,2,1:T(8,128)(2,1)S(1)}, u32[]{:S(2)}, u32[]{:S(2)}) collective-permute-start(bf16[128,4,128]{0,2,1:T(8,128)(2,1)S(1)} %get-tuple-element.138), channel_id=1, source_target_pairs={{0,1},{1,2},{2,3},{3,4},{4,5},{5,6},{6,7},{7,8},{8,9},{9,10},{10,1... | collective-permute-start | bytes 393224 | tf_op jit(solution)/shard_map/ppermute | solution.py:13
  183.0 2.2 copy-start.2
  188.5 7.9 %collective-permute-start.6 = (bf16[128,4,128]{0,2,1:T(8,128)(2,1)S(1)}, bf16[128,4,128]{0,2,1:T(8,128)(2,1)S(1)}, u32[]{:S(2)}, u32[]{:S(2)}) collective-permute-start(bf16[128,4,128]{0,2,1:T(8,128)(2,1)S(1)} %get-tuple-element.133), channel_id=1, source_target_pairs={{1,0},{2,1},{3,2},{4,3},{5,4},{6,5},{7,6},{8,7},{9,8},{10,9},{11,1... | collective-permute-start | bytes 393224 | tf_op jit(solution)/shard_map/ppermute | solution.py:16
  188.6 11.0 %collective-permute-start.7 = (bf16[128,4,128]{0,2,1:T(8,128)(2,1)S(1)}, bf16[128,4,128]{0,2,1:T(8,128)(2,1)S(1)}, u32[]{:S(2)}, u32[]{:S(2)}) collective-permute-start(bf16[128,4,128]{0,2,1:T(8,128)(2,1)S(1)} %get-tuple-element.134), channel_id=1, source_target_pairs={{0,1},{1,2},{2,3},{3,4},{4,5},{5,6},{6,7},{7,8},{8,9},{9,10},{10,1... | collective-permute-start | bytes 393224 | tf_op jit(solution)/shard_map/ppermute | solution.py:13
  200.0 2.8 %copy-start.6 = (bf16[128,137]{0,1:T(8,128)(2,1)S(1)}, bf16[128,137]{0,1:T(8,128)(2,1)}, u32[]{:S(2)}) copy-start(bf16[128,137]{0,1:T(8,128)(2,1)} %param.19) | copy-start | bytes 105220
  216.9 2.8 %copy-start.1 = (bf16[137,128]{1,0:T(8,128)(2,1)S(1)}, bf16[137,128]{1,0:T(8,128)(2,1)}, u32[]{:S(2)}) copy-start(bf16[137,128]{1,0:T(8,128)(2,1)} %param.16) | copy-start | bytes 105220
where the time goes:
time: 221 us; the launch traced here: 220 us
  matrix products  66.8 us (30%)
  local copies, waits for them, and re-layouts  46.5 us (21%)
  waiting for transfers between devices  46.2 us (21%)
  starting transfers between devices  40.5 us (18%)
  other arithmetic  19.4 us (9%)
    dot_general x4, matrix products, accumulate_block(): jnp.dot(incr_part, onehot, preferred_element_type=jnp.float32)  31.8 us
    convert_element_type x4, local copies, waits for them, and re-layouts, per_device(): hidden = hidden + gates[layer].reshape(width, cell_total) * back  21.7 us
    ppermute x4, waiting for transfers between devices, with_halo(): lax.ppermute(lax.slice_in_dim(block, block.shape[dim] - width, None, axis...  16.6 us
    dot_general x11, matrix products, per_device(): lax.dot_general(conv_weight[layer, tap], window, (((0,), (0,)), ((), ()))...  15.4 us
    all_to_all x1, waiting for transfers between devices, per_device(): lax.all_to_all(observation_residual, ('lat', 'lon'), split_axis=1, concat...  12.2 us
    ppermute x4, starting transfers between devices, with_halo(): lax.ppermute(lax.slice_in_dim(block, block.shape[dim] - width, None, axis...  11.7 us
    all_to_all x1, starting transfers between devices, per_device(): lax.all_to_all(obs_count, ('lat', 'lon'), split_axis=1, concat_axis=1, ti...  11.2 us
    dot_general x1, matrix products, per_device(): lax.dot_general(encoder, hidden.astype(jnp.bfloat16), (((0,), (0,)), ((),...  11 us
  transfers between devices with their start and end apart: 11, of which 10 were waited for; matrix products, arithmetic and copies ran while one was open for 20% of the time, Pallas kernels for 0%

commit v1 on v0

v1 whole, which is shorter than its diff:
```python
import functools

import jax
import jax.numpy as jnp
from jax import lax
from jax.experimental import pallas as pl
from jax.experimental.pallas import tpu as pltpu
from jax.sharding import PartitionSpec as P

F32 = jnp.float32
BF16 = jnp.bfloat16
LANES = 128
CHUNK = 8
DIL = 4
UNUSED = 255.0


def params(mib):
    return pltpu.CompilerParams(vmem_limit_bytes=mib << 20)


def iota(shape, dim):
    return lax.broadcasted_iota(jnp.int32, shape, dim)


def dot(a, b):
    return jnp.dot(a, b, preferred_element_type=F32)


def pack_kernel(resid, index, count, weight, out):
    dests = out.shape[0]
    slots = resid.shape[1]
    per = slots // dests
    weighted = weight[...] * resid[...].astype(F32)
    out[:, 0:per, :] = weighted.astype(BF16).T.reshape(dests, per, LANES)
    spread = (iota((dests, slots), 1) // per == iota((dests, slots), 0)).astype(F32).astype(BF16)
    counts = jnp.broadcast_to(count[...].astype(F32), (8, dests)).astype(BF16)
    used = dot(counts, spread)[0:1]
    cell = index[0:1, :]
    kind = index[1:2, :]
    valid = (iota((1, slots), 1) % per).astype(F32) < used
    low = ((cell >> 7) & (CHUNK - 1)).astype(F32)
    lat = (cell & (LANES - 1)).astype(F32)
    group = jnp.where(valid, (cell >> 10).astype(F32), UNUSED)
    row = iota((LANES, slots), 0) & 63
    meta = jnp.where(
        row == 0, low, jnp.where(row == 1, lat, jnp.where(row == 2, group, kind.astype(F32)))
    )
    meta = meta.astype(BF16).T.reshape(dests, 2, 8, LANES)
    first = meta[:, 0].astype(F32)
    second = meta[:, 1].astype(F32)
    lane = iota((dests, 8, LANES), 2)
    out[:, per : per + 8, :] = jnp.where(lane < 64, first, second).astype(BF16)


def pack(resid, index, count, weight, dests):
    per = resid.shape[1] // dests
    return pl.pallas_call(
        pack_kernel,
        out_shape=jax.ShapeDtypeStruct((dests, per + 8, LANES), BF16),
        compiler_params=params(40),
        name="pack",
    )(resid, index, count, weight)


def gates_kernel(src, out, wide):
    channels, lons, lats = src.shape[1:]

    def widen(c, carry):
        wide[pl.ds(pl.multiple_of(c * lons, lons), lons), :] = src[0, c].astype(F32)
        return carry

    lax.fori_loop(0, channels, widen, 0, unroll=8)

    def gather(lon, carry):
        at = pl.ds(pl.multiple_of(lon * lats, lats), lats)
        for c in range(0, channels, 16):
            a = wide[pl.ds(c * lons + lon, 8, stride=lons), :]
            b = wide[pl.ds((c + 8) * lons + lon, 8, stride=lons), :]
            out[0, c : c + 16, at] = jnp.concatenate([a, b], axis=0).astype(BF16)
        return carry

    lax.fori_loop(0, lons, gather, 0, unroll=2)


def flat_gates(gates):
    layers, channels, lons, lats = gates.shape
    return pl.pallas_call(
        gates_kernel,
        grid=(layers,),
        in_specs=[pl.BlockSpec((1, channels, lons, lats), lambda i: (i, 0, 0, 0))],
        out_specs=pl.BlockSpec((1, channels, lons * lats), lambda i: (i, 0, 0)),
        out_shape=jax.ShapeDtypeStruct((layers, channels, lons * lats), BF16),
        scratch_shapes=[pltpu.VMEM((channels * lons, lats), F32)],
        compiler_params=params(40),
        name="flat_gates",
    )(gates)


def front_kernel(packed, jac, dec, incr_out, key_out, group_out, grad_out, hid_out, lo_out, hi_out):
    senders = packed.shape[0]
    half = senders * 8
    slots = 2 * half
    levels = jac.shape[0]
    kinds = jac.shape[1] // LANES
    x = jnp.concatenate(
        [packed[:, 0:8, :].reshape(half, LANES).T, packed[:, 8:16, :].reshape(half, LANES).T],
        axis=1,
    )
    meta = packed[:, 16:24, :].reshape(half, LANES)
    meta_t = meta.astype(F32).T

    def line(q):
        return jnp.concatenate([meta_t[q : q + 1], meta_t[64 + q : 65 + q]], axis=1)

    def column(q):
        pick = iota((LANES, LANES), 0)
        a = dot(meta, (pick == q).astype(F32).astype(BF16))
        b = dot(meta, (pick == 64 + q).astype(F32).astype(BF16))
        return jnp.concatenate([a, b], axis=0)

    group = line(2)
    kind = line(3)
    group_out[...] = jnp.broadcast_to(group, (8, slots))
    spread = jnp.concatenate(
        [x * (kind == k).astype(F32).astype(BF16) for k in range(kinds)], axis=0
    )
    incr = dot(jac[...], spread).astype(BF16)
    incr_out[...] = incr
    key = column(0) * LANES + column(1) - iota((slots, LANES), 1).astype(F32)
    key_out[...] = key
    onehot = hot(key)
    last = CHUNK - 1
    lhs = jnp.concatenate(
        [incr * (group == g).astype(F32).astype(BF16) for g in (0, last)], axis=0
    )
    grad = dot(lhs, onehot)
    grad_out[...] = grad
    for side in range(2):
        part = grad[side * levels : (side + 1) * levels].astype(BF16)
        hidden = dot(dec[...], part)
        hid_out[side] = hidden
        (lo_out, hi_out)[side][...] = hidden.astype(BF16)


def hot(key):
    return jnp.concatenate(
        [jnp.where(key == float(r * LANES), 1.0, 0.0).astype(BF16) for r in range(CHUNK)], axis=1
    )


def front(packed, jac, dec):
    slots = packed.shape[0] * 16
    levels = jac.shape[0]
    cols = CHUNK * LANES
    sd = jax.ShapeDtypeStruct
    return pl.pallas_call(
        front_kernel,
        out_shape=(
            sd((levels, slots), BF16),
            sd((slots, LANES), F32),
            sd((8, slots), F32),
            sd((2 * levels, cols), F32),
            sd((2, LANES, cols), F32),
            sd((LANES, cols), BF16),
            sd((LANES, cols), BF16),
        ),
        compiler_params=params(56),
        name="front",
    )(packed, jac, dec)


def conv(weight, taps):
    return dot(weight, jnp.concatenate(taps, axis=0))


def inner_layers(hid, ga, gb, gate_a, gate_b, wa, wb, near_out, finish):
    cols = CHUNK * LANES
    step = DIL * LANES
    total = hid.shape[1]
    for i in range(total // cols - 1):
        o = step + i * cols
        at = slice(o, o + cols)
        back = conv(wa[...], [ga[:, o + d : o + d + cols] for d in (step, 0, -step)])
        new = hid[:, at] + gate_a[0, :, at].astype(F32) * back
        hid[:, at] = new
        gb[:, at] = new.astype(BF16)
    near_out[0] = hid[:, step : step + cols]
    near_out[1] = hid[:, total - step - cols : total - step]
    for i in range(1, total // cols - 1):
        o = i * cols
        at = slice(o, o + cols)
        back = conv(wb[...], [gb[:, o + d : o + d + cols] for d in (step, 0, -step)])
        finish(i, hid[:, at] + gate_b[0, :, at].astype(F32) * back)


def mid_kernel(
    incr, key, group, hid_edge, g_lo, g_hi, dec, gate_a, gate_b, wa, wb,
    grad_out, hid_out, near_out, hid, ga, gb, lhs, onehot,
):
    cols = CHUNK * LANES
    levels = incr.shape[0]
    total = hid.shape[1]
    inner = total // cols - 2
    onehot[...] = hot(key[...])
    for g in range(inner):
        mask = (group[0:1, :] == float(g + 1)).astype(F32).astype(BF16)
        lhs[g * levels : (g + 1) * levels, :] = incr[...] * mask
    hid[:, 0:cols] = hid_edge[0]
    hid[:, total - cols : total] = hid_edge[1]
    ga[:, 0:cols] = g_lo[...]
    ga[:, total - cols : total] = g_hi[...]
    for n in range(0, cols, 256):
        grad_out[:, n : n + 256] = dot(lhs[...], onehot[:, n : n + 256])
    for g in range(inner):
        at = slice((g + 1) * cols, (g + 2) * cols)
        new = dot(dec[...], grad_out[g * levels : (g + 1) * levels, :].astype(BF16))
        hid[:, at] = new
        ga[:, at] = new.astype(BF16)

    def finish(i, value):
        hid_out[:, (i - 1) * cols : i * cols] = value

    inner_layers(hid, ga, gb, gate_a, gate_b, wa, wb, near_out, finish)


def whole(shape):
    return pl.BlockSpec(shape, lambda i: (0,) * len(shape))


def mid(incr, key, group, hid_edge, g_lo, g_hi, dec, gates, layer, wa, wb):
    levels, slots = incr.shape
    _, channels, total = gates.shape
    cols = CHUNK * LANES
    inner = total // cols - 2
    sd = jax.ShapeDtypeStruct
    outs = (
        sd((inner * levels, cols), F32),
        sd((channels, inner * cols), F32),
        sd((2, channels, cols), F32),
    )
    return pl.pallas_call(
        mid_kernel,
        grid=(1,),
        in_specs=[
            whole(incr.shape),
            whole(key.shape),
            whole(group.shape),
            whole(hid_edge.shape),
            whole(g_lo.shape),
            whole(g_hi.shape),
            whole(dec.shape),
            pl.BlockSpec((1, channels, total), lambda i: (layer, 0, 0)),
            pl.BlockSpec((1, channels, total), lambda i: (layer - 1, 0, 0)),
            whole(wa.shape),
            whole(wb.shape),
        ],
        out_specs=tuple(whole(o.shape) for o in outs),
        out_shape=outs,
        scratch_shapes=[
            pltpu.VMEM((channels, total), F32),
            pltpu.VMEM((channels, total), BF16),
            pltpu.VMEM((channels, total), BF16),
            pltpu.VMEM((inner * levels, slots), BF16),
            pltpu.VMEM((slots, cols), BF16),
        ],
        compiler_params=params(58),
        name="mid",
    )(incr, key, group, hid_edge, g_lo, g_hi, dec, gates, gates, wa, wb)


def emit(enc, grad, value, tile):
    full = grad + dot(enc, value.astype(BF16))
    for r in range(CHUNK):
        for l in range(0, full.shape[0], 8):
            tile[pl.ds(l * CHUNK + r, 8, stride=CHUNK), :] = full[
                l : l + 8, r * LANES : (r + 1) * LANES
            ]


def send_tile(tile, out, chunk, sem):
    levels = out.shape[0]
    src = tile.reshape(tile.shape[0] // CHUNK, CHUNK, LANES)
    return pltpu.make_async_copy(
        src.at[0:levels], out.at[:, CHUNK * chunk : CHUNK * (chunk + 1), :], sem
    )


def last_kernel(
    hid_in, hid_edge, g_lo, g_hi, grad, enc, gate_a, gate_b, wa, wb,
    out, near_out, hid, ga, gb, tiles, sems,
):
    cols = CHUNK * LANES
    total = hid.shape[1]
    levels = enc.shape[0]
    hid[:, 0:cols] = hid_edge[0]
    hid[:, total - cols : total] = hid_edge[1]
    hid[:, cols : total - cols] = hid_in[...]
    ga[:, 0:cols] = g_lo[...]
    ga[:, total - cols : total] = g_hi[...]
    ga[:, cols : total - cols] = hid_in[...].astype(BF16)
    copies = []

    def finish(i, value):
        slot = (i - 1) % 2
        if i > 2:
            copies[i - 3].wait()
        emit(enc[...], grad[(i - 1) * levels : i * levels, :], value, tiles.at[slot])
        copy = send_tile(tiles.at[slot], out, i, sems.at[slot])
        copy.start()
        copies.append(copy)

    inner_layers(hid, ga, gb, gate_a, gate_b, wa, wb, near_out, finish)
    copies[-2].wait()
    copies[-1].wait()


def last(hid_in, hid_edge, g_lo, g_hi, grad, enc, gates, layer, wa, wb, out_shape):
    _, channels, total = gates.shape
    cols = CHUNK * LANES
    levels = enc.shape[0]
    sd = jax.ShapeDtypeStruct
    near = sd((2, channels, cols), F32)
    return pl.pallas_call(
        last_kernel,
        grid=(1,),
        in_specs=[
            whole(hid_in.shape),
            whole(hid_edge.shape),
            whole(g_lo.shape),
            whole(g_hi.shape),
            whole(grad.shape),
            whole(enc.shape),
            pl.BlockSpec((1, channels, total), lambda i: (layer, 0, 0)),
            pl.BlockSpec((1, channels, total), lambda i: (layer - 1, 0, 0)),
            whole(wa.shape),
            whole(wb.shape),
        ],
        out_specs=(pl.BlockSpec(memory_space=pl.ANY), whole(near.shape)),
        out_shape=(sd(out_shape, F32), near),
        scratch_shapes=[
            pltpu.VMEM((channels, total), F32),
            pltpu.VMEM((channels, total), BF16),
            pltpu.VMEM((channels, total), BF16),
            pltpu.VMEM((2, levels * CHUNK, LANES), F32),
            pltpu.SemaphoreType.DMA((2,)),
        ],
        compiler_params=params(58),
        name="last",
    )(hid_in, hid_edge, g_lo, g_hi, grad, enc, gates, gates, wa, wb)


def edge_values(hid, g_lo, g_hi, halo_lo, halo_hi, near, a_lo, a_hi, ah_lo, ah_hi, b_lo, b_hi, wa, wb):
    cols = CHUNK * LANES
    step = DIL * LANES
    result = []
    for side in range(2):
        if side == 0:
            field = jnp.concatenate([halo_lo[...], g_lo[...]], axis=1)
            old = jnp.concatenate([halo_lo[:, step:].astype(F32), hid[0, :, :step]], axis=1)
            gate = jnp.concatenate([ah_lo[0], a_lo[0, :, :step]], axis=1)
        else:
            field = jnp.concatenate([g_hi[...], halo_hi[...]], axis=1)
            old = jnp.concatenate([hid[1, :, step:], halo_hi[:, :step].astype(F32)], axis=1)
            gate = jnp.concatenate([a_hi[0, :, step:], ah_hi[0]], axis=1)
        back = conv(wa[...], [field[:, d : d + cols] for d in (2 * step, step, 0)])
        new = old + gate.astype(F32) * back
        pieces = (new, near[0]) if side == 0 else (near[1], new)
        joined = jnp.concatenate(pieces, axis=1)
        field = joined.astype(BF16)
        back = conv(wb[...], [field[:, d : d + cols] for d in (2 * step, step, 0)])
        gate = (b_lo, b_hi)[side][0]
        result.append(joined[:, step : step + cols] + gate.astype(F32) * back)
    return result


def edge_kernel(*refs):
    ins, (hid_out, lo_out, hi_out) = refs[:14], refs[14:]
    lo, hi = edge_values(*ins)
    hid_out[0] = lo
    hid_out[1] = hi
    lo_out[...] = lo.astype(BF16)
    hi_out[...] = hi.astype(BF16)


def edge_last_kernel(*refs):
    ins, (grad, enc, _), (out, tiles, sems) = refs[:14], refs[14:17], refs[17:]
    levels = enc.shape[0]
    values = edge_values(*ins)
    chunks = out.shape[1] // CHUNK
    copies = []
    for side in range(2):
        part = grad[side * levels : (side + 1) * levels, :]
        emit(enc[...], part, values[side], tiles.at[side])
        copy = send_tile(tiles.at[side], out, side * (chunks - 1), sems.at[side])
        copy.start()
        copies.append(copy)
    for copy in copies:
        copy.wait()


def edge_call(hid, g_lo, g_hi, halo_lo, halo_hi, near, gates, layer, ah_lo, ah_hi, which, wa, wb, tail=None):
    _, channels, total = gates.shape
    cols = CHUNK * LANES
    step = DIL * LANES
    end = total // cols - 1
    sd = jax.ShapeDtypeStruct

    def gate_at(k, c):
        return pl.BlockSpec((1, channels, cols), lambda i: (k, 0, c))

    halo_at = pl.BlockSpec((1, channels, step), lambda i: (which, 0, 0))
    specs = [
        whole(hid.shape),
        whole(g_lo.shape),
        whole(g_hi.shape),
        whole(halo_lo.shape),
        whole(halo_hi.shape),
        whole(near.shape),
        gate_at(layer, 0),
        gate_at(layer, end),
        halo_at,
        halo_at,
        gate_at(layer - 1, 0),
        gate_at(layer - 1, end),
        whole(wa.shape),
        whole(wb.shape),
    ]
    args = [hid, g_lo, g_hi, halo_lo, halo_hi, near, gates, gates, ah_lo, ah_hi, gates, gates, wa, wb]
    if tail is None:
        outs = (sd(hid.shape, F32), sd(g_lo.shape, BF16), sd(g_hi.shape, BF16))
        return pl.pallas_call(
            edge_kernel,
            grid=(1,),
            in_specs=specs,
            out_specs=tuple(whole(o.shape) for o in outs),
            out_shape=outs,
            compiler_params=params(40),
            name="edge",
        )(*args)
    grad, enc, state = tail
    return pl.pallas_call(
        edge_last_kernel,
        grid=(1,),
        in_specs=specs + [whole(grad.shape), whole(enc.shape), pl.BlockSpec(memory_space=pl.ANY)],
        out_specs=pl.BlockSpec(memory_space=pl.ANY),
        out_shape=sd(state.shape, F32),
        scratch_shapes=[
            pltpu.VMEM((2, enc.shape[0] * CHUNK, LANES), F32),
            pltpu.SemaphoreType.DMA((2,)),
        ],
        input_output_aliases={len(specs) + 2: 0},
        compiler_params=params(40),
        name="edge_last",
    )(*args, grad, enc, state)


def halos(lo, hi):
    count = lax.axis_size("lon")
    up = [(i, (i + 1) % count) for i in range(count)]
    down = [(b, a) for a, b in up]
    return lax.ppermute(hi, "lon", up), lax.ppermute(lo, "lon", down)


def per_device(resid, index, count, weight, jacobian, decoder, conv_weight, gates, encoder):
    dests = lax.axis_size("lat") * lax.axis_size("lon")
    channels, kinds, levels = jacobian.shape
    pad = -levels % 16
    packed = pack(resid, index, count, weight.reshape(-1, 1), dests)
    packed = lax.all_to_all(packed, ("lat", "lon"), split_axis=0, concat_axis=0, tiled=True)
    flat = flat_gates(gates)
    step = DIL * LANES
    gate_lo = jnp.stack([flat[1, :, :step], flat[3, :, :step]])
    gate_hi = jnp.stack([flat[1, :, -step:], flat[3, :, -step:]])
    gh_lo, gh_hi = halos(gate_lo, gate_hi)
    jac = jnp.pad(jacobian.transpose(2, 1, 0).reshape(levels, kinds * channels), ((0, pad), (0, 0)))
    dec = jnp.pad(decoder.T, ((0, 0), (0, pad)))
    enc = jnp.pad(encoder.T, ((0, pad), (0, 0)))
    layers = conv_weight.shape[0]
    w = conv_weight.reshape(layers, -1, channels).transpose(0, 2, 1)

    incr, key, group, grad_e, hid_e, g_lo, g_hi = front(packed, jac, dec)
    halo_lo, halo_hi = halos(g_lo, g_hi)
    grad_i, hid_i, near = mid(incr, key, group, hid_e, g_lo, g_hi, dec, flat, 3, w[3], w[2])
    hid_e, g_lo, g_hi = edge_call(
        hid_e, g_lo, g_hi, halo_lo, halo_hi, near, flat, 3, gh_lo, gh_hi, 1, w[3], w[2]
    )
    halo_lo, halo_hi = halos(g_lo, g_hi)
    out_shape = (levels,) + gates.shape[2:]
    state, near = last(hid_i, hid_e, g_lo, g_hi, grad_i, enc, flat, 1, w[1], w[0], out_shape)
    return edge_call(
        hid_e, g_lo, g_hi, halo_lo, halo_hi, near, flat, 1, gh_lo, gh_hi, 0, w[1], w[0],
        tail=(grad_e, enc, state),
    )


def solution(mesh):
    return jax.shard_map(
        per_device,
        mesh=mesh,
        in_specs=(
            P(None, ("lat", "lon")),
            P(None, ("lat", "lon")),
            P(None, ("lat", "lon")),
            P(),
            P(),
            P(),
            P(),
            P(None, None, "lon", "lat"),
            P(),
        ),
        out_specs=P(None, "lon", "lat"),
        check_vma=False,
    )
```

time: 221 us -> 106 us (0.48)
  matrix products: 66.8 us -> 0 us
  Pallas kernels: 0 us -> 50.6 us
  waiting for transfers between devices: 46.2 us -> 2.08 us
  local copies, waits for them, and re-layouts: 46.5 us -> 22.8 us
  other arithmetic: 19.4 us -> 0.05 us
  starting transfers between devices: 40.5 us -> 29.4 us
    dot_general x18 -> x0, matrix products: 66.8 us -> none  [the longest x4 31.8 us: accumulate_block(): jnp.dot(incr_part, onehot, preferred_element_type=jnp.float32)]
    pallas_call x0 -> x7, Pallas kernels: none -> 50.6 us  [the longest x1 19.1 us: flat_gates(): pl.pallas_call(gates_kernel, grid=(layers,), in_specs=[pl.BlockSpec((1, c...]
    ppermute x8 -> x6, waiting for transfers between devices: 27.2 us -> 2.08 us  [halos(): return (lax.ppermute(hi, 'lon', up), lax.ppermute(lo, 'lon', down))]
    convert_element_type x4 -> x0, local copies, waits for them, and re-layouts: 21.7 us -> none  [per_device(): hidden = hidden + gates[layer].reshape(width, cell_total) * back]
    all_to_all x3 -> x1, waiting for transfers between devices: 19 us -> 0.01 us  [per_device(): lax.all_to_all(packed, ('lat', 'lon'), split_axis=0, concat_axis=0, tiled...]
    all_to_all x3 -> x1, starting transfers between devices: 26.1 us -> 11.2 us  [per_device(): lax.all_to_all(packed, ('lat', 'lon'), split_axis=0, concat_axis=0, tiled...]
    convert_element_type x3 -> x0, other arithmetic: 10.6 us -> none  [the longest x1 10.2 us: per_device(): hidden = hidden + gates[layer].reshape(width, cell_total) * back]
    reshape x3 -> x2, local copies, waits for them, and re-layouts: 11.2 us -> 0.98 us  [the longest x1 0.76 us: per_device(): packed = pack(resid, index, count, weight.reshape(-1, 1), dests)]
  transfers between devices with their start and end apart: 11 -> 7, of which waited for: 10 -> 2; matrix products, arithmetic and copies ran while one was open for 20% -> 3% of each run, Pallas kernels for 0% -> 44%
where the time goes in v1:
time: 106 us; the launch traced here: 105 us
  Pallas kernels  50.6 us (48%)
  starting transfers between devices  29.4 us (28%)
  local copies, waits for them, and re-layouts  22.8 us (22%)
  waiting for transfers between devices  2.08 us (2%)
    pallas_call x1, Pallas kernels, flat_gates(): pl.pallas_call(gates_kernel, grid=(layers,), in_specs=[pl.BlockSpec((1, c...  19.1 us
    unnamed x59, local copies, waits for them, and re-layouts  19 us
    ppermute x6, starting transfers between devices, halos(): return (lax.ppermute(hi, 'lon', up), lax.ppermute(lo, 'lon', down))  18.2 us
    pallas_call x1, Pallas kernels, mid(): pl.pallas_call(mid_kernel, grid=(1,), in_specs=[whole(incr.shape), whole(...  11.4 us
    all_to_all x1, starting transfers between devices, per_device(): lax.all_to_all(packed, ('lat', 'lon'), split_axis=0, concat_axis=0, tiled...  11.2 us
    pallas_call x1, Pallas kernels, last(): pl.pallas_call(last_kernel, grid=(1,), in_specs=[whole(hid_in.shape), who...  10.7 us
    pallas_call x1, Pallas kernels, front(): pl.pallas_call(front_kernel, out_shape=(sd((levels, slots), BF16), sd((sl...  5.15 us
  transfers between devices with their start and end apart: 7, of which 2 were waited for; matrix products, arithmetic and copies ran while one was open for 3% of the time, Pallas kernels for 44%

profile of v1, /device:TPU:0, one launch (start us, length us, event | category | flops | bytes accessed | tf_op | source)
XLA Modules:
  0.0 105.4 jit_solution(1741419782284172901)
XLA Ops:
  0.0 0.8 copy.14.weight
  0.8 1.0 copy-done.19
  1.8 0.7 copy-done.21
  2.5 0.7 copy-done.22
  3.2 1.3 %pack.1 = bf16[128,24,128]{2,1,0:T(8,128)(2,1)} custom-call(bf16[128,2048]{1,0:T(8,128)(2,1)S(1)} %copy-done.19, s32[2,2048]{1,0:T(2,128)S(1)} %copy-done.21, s32[1,128]{1,0:T(1,128)S(1)} %copy-done.22, f32[128,1]{1,0:T(8,128)S(1)} %copy.14.weight), custom_call_target="tpu_custom_call" | custom-call | tf_op jit(solution)/shard_map/pack/pallas_call | solution.py:58
  4.5 11.2 %all-to-all-start = ((bf16[128,24,128]{2,1,0:T(8,128)(2,1)}), bf16[128,24,128]{2,1,0:T(8,128)(2,1)S(1)}, u32[]{:S(2)}, u32[]{:S(2)}) async-start(bf16[128,24,128]{2,1,0:T(8,128)(2,1)} %pack.1), calls=%async_computation | async-start | bytes 1572864 | tf_op jit(solution)/shard_map/all_to_all | solution.py:470
  15.6 0.0 copy-start.26
  15.6 0.0 copy-start.25
  15.7 19.1 %flat_gates.1.gate_a.gate_b.refs_6_.refs_7_.refs_10_.refs_11_ = bf16[4,128,8192]{2,1,0:T(8,128)(2,1)S(1)} custom-call(bf16[4,128,64,128]{3,2,1,0:T(8,128)(2,1)} %src.1), custom_call_target="tpu_custom_call" | custom-call | tf_op jit(solution)/shard_map/flat_gates/pallas_call | solution.py:88
  34.8 3.3 %copy-done = bf16[4,128,8192]{2,1,0:T(8,128)(2,1)} copy-done((bf16[4,128,8192]{2,1,0:T(8,128)(2,1)}, bf16[4,128,8192]{2,1,0:T(8,128)(2,1)S(1)}, u32[]{:S(2)}) %copy-start) | copy-done | bytes 8388632
  38.1 2.5 %collective-permute-start.2 = (bf16[2,128,512]{2,1,0:T(8,128)(2,1)S(1)}, bf16[2,128,512]{2,1,0:T(8,128)(2,1)S(1)}, u32[]{:S(2)}, u32[]{:S(2)}) collective-permute-start(bf16[2,128,512]{2,1,0:T(8,128)(2,1)S(1)} %pad_maximum_fusion), channel_id=1, source_target_pairs={{0,1},{1,2},{2,3},{3,4},{4,5},{5,6},{6,7},{7,8},{8,9},{9,10},{10,1... | collective-permute-start | bytes 786440 | tf_op jit(solution)/shard_map/ppermute | solution.py:462
  40.7 5.3 %collective-permute-start.3 = (bf16[2,128,512]{2,1,0:T(8,128)(2,1)S(1)}, bf16[2,128,512]{2,1,0:T(8,128)(2,1)S(1)}, u32[]{:S(2)}, u32[]{:S(2)}) collective-permute-start(bf16[2,128,512]{2,1,0:T(8,128)(2,1)S(1)} %pad_maximum_fusion.1), channel_id=1, source_target_pairs={{1,0},{2,1},{3,2},{4,3},{5,4},{6,5},{7,6},{8,7},{9,8},{10,9},{11,1... | collective-permute-start | bytes 786440 | tf_op jit(solution)/shard_map/ppermute | solution.py:462
  46.1 0.1 copy.15
  46.2 0.6 pad.13.dec
  46.8 0.0 copy-done.25
  46.9 0.8 pad.12.jac
  47.6 0.0 all-to-all-done.packed
  47.7 0.9 copy-done.23
  48.6 5.1 %front.1 = (bf16[144,2048]{1,0:T(8,128)(2,1)}, f32[2048,128]{1,0:T(8,128)}, f32[8,2048]{1,0:T(8,128)}, f32[288,1024]{1,0:T(8,128)}, f32[2,128,1024]{2,1,0:T(8,12...) custom-call(bf16[128,24,128]{2,1,0:T(8,128)(2,1)} %copy-done.23, bf16[144,1024]{1,0:T(8,128)(2,1)} %pad.12.jac, ...), custom_call_target="tpu_custom_call" | custom-call | tf_op jit(solution)/shard_map/front/pallas_call | solution.py:157
  53.7 3.3 %collective-permute-start.1 = (bf16[128,1024]{1,0:T(8,128)(2,1)}, bf16[128,1024]{1,0:T(8,128)(2,1)S(1)}, u32[]{:S(2)}, u32[]{:S(2)}) collective-permute-start(bf16[128,1024]{1,0:T(8,128)(2,1)} %get-tuple-element.21.g_lo.refs_1_), channel_id=1, source_target_pairs={{1,0},{2,1},{3,2},{4,3},{5,4},{6,5},{7,6},{8,7},{9,8},{10,9},{11,1... | collective-permute-start | bytes 786440 | tf_op jit(solution)/shard_map/ppermute | solution.py:462
  57.1 0.2 collective-permute-start
  57.3 0.0 copy-done.24
  57.3 0.2 copy.16
  57.5 0.8 slice_bitcast_fusion
  58.3 0.0 copy-start.16
  58.3 11.4 %mid.1 = (f32[864,1024]{1,0:T(8,128)}, f32[128,6144]{1,0:T(8,128)}, f32[2,128,1024]{2,1,0:T(8,128)}) custom-call(bf16[144,2048]{1,0:T(8,128)(2,1)} %get-tuple-element.23.incr, f32[2048,128]{1,0:T(8,128)} %get-tuple-element.24.key, f32[8,2048]{1,0:T(8,128)} %get-tuple-element.25.group, f32[2,128,1024]{2,1,0:T(8,128)} %get-tuple-element.20.hid_edge.refs_0_, ...), custom_call_target="tpu_custom_call" | custom-call | tf_op jit(solution)/shard_map/mid/pallas_call | solution.py:242
  69.7 0.0 collective-permute-done.2.refs_8_
  69.7 0.0 collective-permute-done.3.refs_9_
  69.7 0.0 collective-permute-done.1.refs_4_
  69.7 0.7 collective-permute-done.refs_3_
  70.5 0.0 copy-done.7
  70.5 3.4 %copy-done.1 = bf16[4,128,8192]{2,1,0:T(8,128)(2,1)S(1)} copy-done((bf16[4,128,8192]{2,1,0:T(8,128)(2,1)S(1)}, bf16[4,128,8192]{2,1,0:T(8,128)(2,1)}, u32[]{:S(2)}) %copy-start.1) | copy-done | bytes 8388632
  73.9 1.2 %copy-done.13 = f32[2,128,1024]{2,1,0:T(8,128)S(1)} copy-done((f32[2,128,1024]{2,1,0:T(8,128)S(1)}, f32[2,128,1024]{2,1,0:T(8,128)}, u32[]{:S(2)}) %copy-start.13) | copy-done | bytes 1048600
  75.1 1.0 edge.1
  76.1 0.0 copy-start.4
  76.1 1.0 copy-done.4
  77.1 6.8 %collective-permute-start.5 = (bf16[128,1024]{1,0:T(8,128)(2,1)S(1)}, bf16[128,1024]{1,0:T(8,128)(2,1)S(1)}, u32[]{:S(2)}, u32[]{:S(2)}) collective-permute-start(bf16[128,1024]{1,0:T(8,128)(2,1)S(1)} %get-tuple-element.28.g_lo.refs_1_), channel_id=1, source_target_pairs={{1,0},{2,1},{3,2},{4,3},{5,4},{6,5},{7,6},{8,7},{9,8},{10,9},{11,1... | collective-permute-start | bytes 786440 | tf_op jit(solution)/shard_map/ppermute | solution.py:462
  83.9 0.0 collective-permute-start.4
  83.9 0.6 pad.14.enc.refs_15_
  84.5 0.0 copy-done.9
  84.6 10.7 %last.1 = (f32[137,64,128]{2,1,0:T(8,128)}, f32[2,128,1024]{2,1,0:T(8,128)}) custom-call(f32[128,6144]{1,0:T(8,128)} %get-tuple-element.30.hid_in, f32[2,128,1024]{2,1,0:T(8,128)} %copy-done.4, bf16[128,1024]{1,0:T(8,128)(2,1)} %copy-done.9, bf16[128,1024]{1,0:T(8,128)(2,1)} %copy-done.11, f32[864,1024]{1,0:T(8,128)} %get-tuple-element.31.grad, ...), custom_call_target="tpu_custom_call" | custom-call | tf_op jit(solution)/shard_map/last/pallas_call | solution.py:324
  95.2 0.0 collective-permute-done.5.refs_4_
  95.3 1.3 %collective-permute-done.4.refs_3_ = bf16[128,1024]{1,0:T(8,128)(2,1)S(1)} collective-permute-done((bf16[128,1024]{1,0:T(8,128)(2,1)S(1)}, bf16[128,1024]{1,0:T(8,128)(2,1)S(1)}, u32[]{:S(2)}, u32[]{:S(2)}) %collective-permute-start.4) | collective-permute-done | bytes 262176 | tf_op jit(solution)/shard_map/ppermute | solution.py:462
  96.6 3.4 %copy-done.2 = bf16[4,128,8192]{2,1,0:T(8,128)(2,1)S(1)} copy-done((bf16[4,128,8192]{2,1,0:T(8,128)(2,1)S(1)}, bf16[4,128,8192]{2,1,0:T(8,128)(2,1)}, u32[]{:S(2)}) %copy-start.2) | copy-done | bytes 8388632
  100.0 0.9 copy-done.10
  100.9 0.9 copy-done.12
  101.9 1.2 %copy-done.14 = f32[2,128,1024]{2,1,0:T(8,128)S(1)} copy-done((f32[2,128,1024]{2,1,0:T(8,128)S(1)}, f32[2,128,1024]{2,1,0:T(8,128)}, u32[]{:S(2)}) %copy-start.14) | copy-done | bytes 1048600
  103.1 2.1 %edge_last.1 = f32[137,64,128]{2,1,0:T(8,128)} custom-call(f32[2,128,1024]{2,1,0:T(8,128)S(1)} %copy-done.5, bf16[128,1024]{1,0:T(8,128)(2,1)S(1)} %copy-done.10, bf16[128,1024]{1,0:T(8,128)(2,1)S(1)} %copy-done.12, bf16[128,1024]{1,0:T(8,128)(2,1)S(1)} %collective-permute-done.4.refs_3_, ...), custom_call_target="tpu_custom_call", output_to_operand_aliasing={{}: (16, {})} | custom-call | tf_op jit(solution)/shard_map/edge_last/pallas_call | solution.py:442
  (41 shorter events, 0.2 us)
Async XLA Ops:
  0.8 1.0 copy-start.19
  1.8 0.7 copy-start.21
  2.5 0.7 copy-start.22
  4.5 43.2 %all-to-all-start = ((bf16[128,24,128]{2,1,0:T(8,128)(2,1)}), bf16[128,24,128]{2,1,0:T(8,128)(2,1)S(1)}, u32[]{:S(2)}, u32[]{:S(2)}) async-start(bf16[128,24,128]{2,1,0:T(8,128)(2,1)} %pack.1), calls=%async_computation | async-start | bytes 1572864 | tf_op jit(solution)/shard_map/all_to_all | solution.py:470
  15.6 30.4 %copy-start.26 = (bf16[137,128]{1,0:T(8,128)(2,1)S(1)}, bf16[137,128]{1,0:T(8,128)(2,1)}, u32[]{:S(2)}) copy-start(bf16[137,128]{1,0:T(8,128)(2,1)} %param.14) | copy-start | bytes 105220
  15.6 31.2 %copy-start.25 = (bf16[128,8,137]{0,1,2:T(8,128)(2,1)S(1)}, bf16[128,8,137]{0,1,2:T(8,128)(2,1)}, u32[]{:S(2)}) copy-start(bf16[128,8,137]{0,1,2:T(8,128)(2,1)} %param.13) | copy-start | bytes 841732
  34.8 3.3 %copy-start = (bf16[4,128,8192]{2,1,0:T(8,128)(2,1)}, bf16[4,128,8192]{2,1,0:T(8,128)(2,1)S(1)}, u32[]{:S(2)}) copy-start(bf16[4,128,8192]{2,1,0:T(8,128)(2,1)S(1)} %flat_gates.1.gate_a.gate_b.refs_6_.refs_7_.refs_10_.refs_11_) | copy-start | bytes 25165828
  38.1 19.2 %copy-start.24 = (bf16[4,3,128,128]{3,2,1,0:T(8,128)(2,1)S(1)}, bf16[4,3,128,128]{3,2,1,0:T(8,128)(2,1)}, u32[]{:S(2)}) copy-start(bf16[4,3,128,128]{3,2,1,0:T(8,128)(2,1)} %param.15) | copy-start | bytes 1179652
  38.1 31.6 %collective-permute-start.2 = (bf16[2,128,512]{2,1,0:T(8,128)(2,1)S(1)}, bf16[2,128,512]{2,1,0:T(8,128)(2,1)S(1)}, u32[]{:S(2)}, u32[]{:S(2)}) collective-permute-start(bf16[2,128,512]{2,1,0:T(8,128)(2,1)S(1)} %pad_maximum_fusion), channel_id=1, source_target_pairs={{0,1},{1,2},{2,3},{3,4},{4,5},{5,6},{6,7},{7,8},{8,9},{9,10},{10,1... | collective-permute-start | bytes 786440 | tf_op jit(solution)/shard_map/ppermute | solution.py:462
  40.7 29.0 %collective-permute-start.3 = (bf16[2,128,512]{2,1,0:T(8,128)(2,1)S(1)}, bf16[2,128,512]{2,1,0:T(8,128)(2,1)S(1)}, u32[]{:S(2)}, u32[]{:S(2)}) collective-permute-start(bf16[2,128,512]{2,1,0:T(8,128)(2,1)S(1)} %pad_maximum_fusion.1), channel_id=1, source_target_pairs={{1,0},{2,1},{3,2},{4,3},{5,4},{6,5},{7,6},{8,7},{9,8},{10,9},{11,1... | collective-permute-start | bytes 786440 | tf_op jit(solution)/shard_map/ppermute | solution.py:462
  47.6 0.9 copy-start.23
  53.7 16.0 %collective-permute-start.1 = (bf16[128,1024]{1,0:T(8,128)(2,1)}, bf16[128,1024]{1,0:T(8,128)(2,1)S(1)}, u32[]{:S(2)}, u32[]{:S(2)}) collective-permute-start(bf16[128,1024]{1,0:T(8,128)(2,1)} %get-tuple-element.21.g_lo.refs_1_), channel_id=1, source_target_pairs={{1,0},{2,1},{3,2},{4,3},{5,4},{6,5},{7,6},{8,7},{9,8},{10,9},{11,1... | collective-permute-start | bytes 786440 | tf_op jit(solution)/shard_map/ppermute | solution.py:462
  57.1 13.4 %collective-permute-start = (bf16[128,1024]{1,0:T(8,128)(2,1)}, bf16[128,1024]{1,0:T(8,128)(2,1)S(1)}, u32[]{:S(2)}, u32[]{:S(2)}) collective-permute-start(bf16[128,1024]{1,0:T(8,128)(2,1)} %get-tuple-element.22.g_hi.refs_2_), channel_id=1, source_target_pairs={{0,1},{1,2},{2,3},{3,4},{4,5},{5,6},{6,7},{7,8},{8,9},{9,10},{10,1... | collective-permute-start | bytes 786440 | tf_op jit(solution)/shard_map/ppermute | solution.py:462
  58.3 12.2 %copy-start.3 = (f32[2,128,1024]{2,1,0:T(8,128)S(1)}, f32[2,128,1024]{2,1,0:T(8,128)}, u32[]{:S(2)}) copy-start(f32[2,128,1024]{2,1,0:T(8,128)} %get-tuple-element.20.hid_edge.refs_0_) | copy-start | bytes 3145732
  58.3 12.2 %copy-start.7 = (bf16[128,1024]{1,0:T(8,128)(2,1)S(1)}, bf16[128,1024]{1,0:T(8,128)(2,1)}, u32[]{:S(2)}) copy-start(bf16[128,1024]{1,0:T(8,128)(2,1)} %get-tuple-element.21.g_lo.refs_1_) | copy-start | bytes 786436
  58.3 12.2 %copy-start.8 = (bf16[128,1024]{1,0:T(8,128)(2,1)S(1)}, bf16[128,1024]{1,0:T(8,128)(2,1)}, u32[]{:S(2)}) copy-start(bf16[128,1024]{1,0:T(8,128)(2,1)} %get-tuple-element.22.g_hi.refs_2_) | copy-start | bytes 786436
  58.3 12.2 %copy-start.15 = (bf16[128,384]{1,0:T(8,128)(2,1)S(1)}, bf16[128,384]{1,0:T(8,128)(2,1)}, u32[]{:S(2)}) copy-start(bf16[128,384]{1,0:T(8,128)(2,1)} %get-tuple-element.41.wb.refs_13_) | copy-start | bytes 294916
  58.3 12.2 %copy-start.16 = (bf16[128,384]{1,0:T(8,128)(2,1)S(1)}, bf16[128,384]{1,0:T(8,128)(2,1)}, u32[]{:S(2)}) copy-start(bf16[128,384]{1,0:T(8,128)(2,1)} %get-tuple-element.42.wa.refs_12_) | copy-start | bytes 294916
  70.5 3.4 %copy-start.1 = (bf16[4,128,8192]{2,1,0:T(8,128)(2,1)S(1)}, bf16[4,128,8192]{2,1,0:T(8,128)(2,1)}, u32[]{:S(2)}) copy-start(bf16[4,128,8192]{2,1,0:T(8,128)(2,1)} %copy-done) | copy-start | bytes 25165828
  73.9 1.2 %copy-start.13 = (f32[2,128,1024]{2,1,0:T(8,128)S(1)}, f32[2,128,1024]{2,1,0:T(8,128)}, u32[]{:S(2)}) copy-start(f32[2,128,1024]{2,1,0:T(8,128)} %get-tuple-element.26.refs_5_) | copy-start | bytes 3145732
  75.1 8.8 %copy-start.27 = (bf16[128,137]{0,1:T(8,128)(2,1)S(1)}, bf16[128,137]{0,1:T(8,128)(2,1)}, u32[]{:S(2)}) copy-start(bf16[128,137]{0,1:T(8,128)(2,1)} %param.17) | copy-start | bytes 105220
  76.1 1.0 copy-start.4
  77.1 7.4 %copy-start.9 = (bf16[128,1024]{1,0:T(8,128)(2,1)}, bf16[128,1024]{1,0:T(8,128)(2,1)S(1)}, u32[]{:S(2)}) copy-start(bf16[128,1024]{1,0:T(8,128)(2,1)S(1)} %get-tuple-element.28.g_lo.refs_1_) | copy-start | bytes 786436
  77.1 7.4 %copy-start.11 = (bf16[128,1024]{1,0:T(8,128)(2,1)}, bf16[128,1024]{1,0:T(8,128)(2,1)S(1)}, u32[]{:S(2)}) copy-start(bf16[128,1024]{1,0:T(8,128)(2,1)S(1)} %get-tuple-element.29.g_hi.refs_2_) | copy-start | bytes 786436
  77.1 18.1 %collective-permute-start.5 = (bf16[128,1024]{1,0:T(8,128)(2,1)S(1)}, bf16[128,1024]{1,0:T(8,128)(2,1)S(1)}, u32[]{:S(2)}, u32[]{:S(2)}) collective-permute-start(bf16[128,1024]{1,0:T(8,128)(2,1)S(1)} %get-tuple-element.28.g_lo.refs_1_), channel_id=1, source_target_pairs={{1,0},{2,1},{3,2},{4,3},{5,4},{6,5},{7,6},{8,7},{9,8},{10,9},{11,1... | collective-permute-start | bytes 786440 | tf_op jit(solution)/shard_map/ppermute | solution.py:462
  83.9 12.7 %collective-permute-start.4 = (bf16[128,1024]{1,0:T(8,128)(2,1)S(1)}, bf16[128,1024]{1,0:T(8,128)(2,1)S(1)}, u32[]{:S(2)}, u32[]{:S(2)}) collective-permute-start(bf16[128,1024]{1,0:T(8,128)(2,1)S(1)} %get-tuple-element.29.g_hi.refs_2_), channel_id=1, source_target_pairs={{0,1},{1,2},{2,3},{3,4},{4,5},{5,6},{6,7},{7,8},{8,9},{9,10},{10,1... | collective-permute-start | bytes 786440 | tf_op jit(solution)/shard_map/ppermute | solution.py:462
  84.6 12.0 %copy-start.5 = (f32[2,128,1024]{2,1,0:T(8,128)S(1)}, f32[2,128,1024]{2,1,0:T(8,128)}, u32[]{:S(2)}) copy-start(f32[2,128,1024]{2,1,0:T(8,128)} %copy-done.4) | copy-start | bytes 3145732
  84.6 12.0 %copy-start.6 = (f32[288,1024]{1,0:T(8,128)S(1)}, f32[288,1024]{1,0:T(8,128)}, u32[]{:S(2)}) copy-start(f32[288,1024]{1,0:T(8,128)} %get-tuple-element.33.refs_14_) | copy-start | bytes 3538948
  84.6 12.0 %copy-start.17 = (bf16[128,384]{1,0:T(8,128)(2,1)S(1)}, bf16[128,384]{1,0:T(8,128)(2,1)}, u32[]{:S(2)}) copy-start(bf16[128,384]{1,0:T(8,128)(2,1)} %get-tuple-element.39.wb.refs_13_) | copy-start | bytes 294916
  84.6 12.0 %copy-start.18 = (bf16[128,384]{1,0:T(8,128)(2,1)S(1)}, bf16[128,384]{1,0:T(8,128)(2,1)}, u32[]{:S(2)}) copy-start(bf16[128,384]{1,0:T(8,128)(2,1)} %get-tuple-element.40.wa.refs_12_) | copy-start | bytes 294916
  84.6 12.0 %copy-start.20 = (bf16[144,128]{1,0:T(8,128)(2,1)S(1)}, bf16[144,128]{1,0:T(8,128)(2,1)}, u32[]{:S(2)}) copy-start(bf16[144,128]{1,0:T(8,128)(2,1)} %pad.14.enc.refs_15_) | copy-start | bytes 110596
  96.6 3.4 %copy-start.2 = (bf16[4,128,8192]{2,1,0:T(8,128)(2,1)S(1)}, bf16[4,128,8192]{2,1,0:T(8,128)(2,1)}, u32[]{:S(2)}) copy-start(bf16[4,128,8192]{2,1,0:T(8,128)(2,1)} %copy-done) | copy-start | bytes 25165828
  100.0 0.9 copy-start.10
  100.9 0.9 copy-start.12
  101.9 1.2 %copy-start.14 = (f32[2,128,1024]{2,1,0:T(8,128)S(1)}, f32[2,128,1024]{2,1,0:T(8,128)}, u32[]{:S(2)}) copy-start(f32[2,128,1024]{2,1,0:T(8,128)} %get-tuple-element.32.refs_5_) | copy-start | bytes 3145732

commit v2 on v1

v2 whole, which is shorter than its diff:
```python
import functools

import jax
import jax.numpy as jnp
from jax import lax
from jax.experimental import pallas as pl
from jax.experimental.pallas import tpu as pltpu
from jax.sharding import PartitionSpec as P

F32 = jnp.float32
BF16 = jnp.bfloat16
LANES = 128
CHUNK = 8
DIL = 4
UNUSED = 255.0


def params(mib):
    return pltpu.CompilerParams(vmem_limit_bytes=mib << 20)


def iota(shape, dim):
    return lax.broadcasted_iota(jnp.int32, shape, dim)


def dot(a, b):
    return jnp.dot(a, b, preferred_element_type=F32)


def pack_kernel(resid_hbm, index_hbm, count_hbm, weight_hbm, out_hbm, resid, index, count, weight, out, in_sems, out_sems):
    parts, dests = out.shape[:2]
    slots = resid.shape[2]
    per = slots // dests
    small = [
        pltpu.make_async_copy(index_hbm, index, in_sems.at[parts]),
        pltpu.make_async_copy(count_hbm, count, in_sems.at[parts + 1]),
        pltpu.make_async_copy(weight_hbm, weight, in_sems.at[parts + 2]),
    ]
    for copy in small:
        copy.start()
    large = []
    for p in range(parts):
        src = resid_hbm.at[:, p * slots : (p + 1) * slots]
        large.append(pltpu.make_async_copy(src, resid.at[p], in_sems.at[p]))
        large[-1].start()
    for copy in small:
        copy.wait()
    scale = jnp.broadcast_to(weight[...], (LANES, LANES)).T
    scale = jnp.concatenate([scale] * (slots // LANES), axis=1)
    total = dests * parts
    counts = jnp.broadcast_to(count[...].astype(F32), (8, total)).astype(BF16)
    row = iota((LANES, slots), 0) & 63
    lane = iota((dests, 8, LANES), 2)
    sends = []
    for p in range(parts):
        at = slice(p * slots, (p + 1) * slots)
        spread = iota((total, slots), 1) // per + p * dests == iota((total, slots), 0)
        used = dot(counts, spread.astype(F32).astype(BF16))[0:1]
        cell = index[0:1, at]
        kind = index[1:2, at].astype(F32)
        valid = (iota((1, slots), 1) % per).astype(F32) < used
        low = ((cell >> 7) & (CHUNK - 1)).astype(F32)
        lat = (cell & (LANES - 1)).astype(F32)
        group = jnp.where(valid, (cell >> 10).astype(F32), UNUSED)
        meta = jnp.where(row == 0, low, jnp.where(row == 1, lat, jnp.where(row == 2, group, kind)))
        meta = meta.astype(BF16).T.reshape(dests, 2, 8, LANES)
        first = meta[:, 0].astype(F32)
        second = meta[:, 1].astype(F32)
        out[p, :, per : per + 8, :] = jnp.where(lane < 64, first, second).astype(BF16)
        large[p].wait()
        weighted = scale * resid[p].astype(F32)
        out[p, :, 0:per, :] = weighted.astype(BF16).T.reshape(dests, per, LANES)
        dst = out_hbm.at[p * dests : (p + 1) * dests]
        sends.append(pltpu.make_async_copy(out.at[p], dst, out_sems.at[p]))
        sends[-1].start()
    for copy in sends:
        copy.wait()


HBM = pl.BlockSpec(memory_space=pltpu.HBM)
VMEM = pl.BlockSpec(memory_space=pltpu.VMEM)
ANY = pl.BlockSpec(memory_space=pl.ANY)


def pack(resid, index, count, weight, dests):
    channels, slots = resid.shape
    per = slots // dests
    parts = 4
    return pl.pallas_call(
        pack_kernel,
        in_specs=[HBM] * 4,
        out_specs=HBM,
        out_shape=jax.ShapeDtypeStruct((dests, per + 8, LANES), BF16),
        scratch_shapes=[
            pltpu.VMEM((parts, channels, slots // parts), BF16),
            pltpu.VMEM(index.shape, jnp.int32),
            pltpu.VMEM(count.shape, jnp.int32),
            pltpu.VMEM(weight.shape, F32),
            pltpu.VMEM((parts, dests // parts, per + 8, LANES), BF16),
            pltpu.SemaphoreType.DMA((parts + 3,)),
            pltpu.SemaphoreType.DMA((parts,)),
        ],
        compiler_params=params(63),
        name="pack",
    )(resid, index, count, weight)


def by_channel(wide, lon, pitch, c):
    a = wide[pl.ds(c * pitch + lon, 8, stride=pitch), :]
    b = wide[pl.ds((c + 8) * pitch + lon, 8, stride=pitch), :]
    return jnp.concatenate([a, b], axis=0).astype(BF16)


def flatten(src, order, outs, buf, wide, sems):
    channels, lons, lats = src.shape[1:]
    pitch = wide.shape[0] // channels
    copies = [
        pltpu.make_async_copy(src.at[k], buf.at[i], sems.at[i]) for i, k in enumerate(order)
    ]
    for copy in copies:
        copy.start()
    for i, out in enumerate(outs):
        copies[i].wait()

        def widen(c, carry):
            wide[pl.ds(pl.multiple_of(c * pitch, 8), lons), :] = buf[i, c].astype(F32)
            return carry

        lax.fori_loop(0, channels, widen, 0, unroll=8)

        def gather(lon, carry):
            at = pl.ds(pl.multiple_of(lon * lats, lats), lats)
            for c in range(0, channels, 16):
                out[c : c + 16, at] = by_channel(wide, lon, pitch, c)
            return carry

        lax.fori_loop(0, lons, gather, 0, unroll=4)


def gates_scratch(gates):
    layers, channels, lons, lats = gates.shape
    return [
        pltpu.VMEM((2, channels, lons, lats), BF16),
        pltpu.VMEM((channels * (lons + 8), lats), F32),
        pltpu.SemaphoreType.DMA((2,)),
    ]


def prepare_kernel(src, jac, dec, enc, conv_w, f3, f2, jac_out, dec_out, enc_out, w_out, buf, wide, sems, rows, tall):
    levels, kinds = jac.shape[:2]
    padded = enc_out.shape[0]
    rows[...] = jnp.zeros_like(rows)
    rows[0 : levels * kinds, :] = jac[...].astype(F32).reshape(levels * kinds, LANES)
    for k in range(kinds):
        for l in range(0, padded, 16):
            jac_out[l : l + 16, k * LANES : (k + 1) * LANES] = by_channel(rows, k, kinds, l)
    tall[...] = jnp.zeros_like(tall)
    tall[0:levels, :] = enc[...].astype(F32)
    enc_out[...] = tall[0:padded, :].astype(BF16)
    tall[0:levels, :] = dec[...].astype(F32)
    dec_out[...] = tall[...].T[:, 0:padded].astype(BF16)
    for layer in range(conv_w.shape[0]):
        w_out[layer] = conv_w[layer].T
    flatten(src, (3, 2), (f3, f2), buf, wide, sems)


def prepare(gates, jacobian, decoder, encoder, conv_weight):
    layers, channels, lons, lats = gates.shape
    kinds, levels = jacobian.shape[1:]
    padded = levels + -levels % 16
    conv_w = conv_weight.reshape(layers, -1, channels)
    sd = jax.ShapeDtypeStruct
    flat = sd((channels, lons * lats), BF16)
    return pl.pallas_call(
        prepare_kernel,
        in_specs=[HBM] + [VMEM] * 4,
        out_specs=(VMEM,) * 6,
        out_shape=(
            flat,
            flat,
            sd((padded, kinds * channels), BF16),
            sd((channels, padded), BF16),
            sd((padded, channels), BF16),
            sd((layers, channels, conv_w.shape[1]), BF16),
        ),
        scratch_shapes=gates_scratch(gates)
        + [pltpu.VMEM((padded * kinds, channels), F32), pltpu.VMEM((256, channels), F32)],
        compiler_params=params(52),
        name="prepare",
    )(gates, jacobian.transpose(2, 1, 0), decoder, encoder.T, conv_w)


def later_gates_kernel(src, after, f1, f0, buf, wide, sems):
    del after
    flatten(src, (1, 0), (f1, f0), buf, wide, sems)


def later_gates(gates, after):
    layers, channels, lons, lats = gates.shape
    flat = jax.ShapeDtypeStruct((channels, lons * lats), BF16)
    return pl.pallas_call(
        later_gates_kernel,
        in_specs=[HBM, ANY],
        out_specs=(VMEM,) * 2,
        out_shape=(flat,) * 2,
        scratch_shapes=gates_scratch(gates),
        compiler_params=params(46),
        name="later_gates",
    )(gates, after)


def gate_edges_kernel(src, lo, hi, buf, wide, sems):
    channels, lons, lats = src.shape[1:]
    copies = []
    for k in range(2):
        for side in range(2):
            at = side * (lons - CHUNK)
            part = src.at[2 * k + 1, :, at : at + CHUNK, :]
            copies.append(pltpu.make_async_copy(part, buf.at[k, side], sems.at[k, side]))
            copies[-1].start()
    for k in range(2):
        for side, out in enumerate((lo, hi)):
            copies[2 * k + side].wait()
            wide[k, side] = buf[k, side].astype(F32).reshape(channels * CHUNK, lats)
            for r in range(DIL):
                for c in range(0, channels, 16):
                    value = by_channel(wide.at[k, side], side * DIL + r, CHUNK, c)
                    out[k, c : c + 16, r * lats : (r + 1) * lats] = value


def gate_edges(gates):
    layers, channels, lons, lats = gates.shape
    send = jax.ShapeDtypeStruct((2, channels, DIL * lats), BF16)
    return pl.pallas_call(
        gate_edges_kernel,
        in_specs=[HBM],
        out_specs=(VMEM,) * 2,
        out_shape=(send,) * 2,
        scratch_shapes=[
            pltpu.VMEM((2, 2, channels, CHUNK, lats), BF16),
            pltpu.VMEM((2, 2, channels * CHUNK, lats), F32),
            pltpu.SemaphoreType.DMA((2, 2)),
        ],
        compiler_params=params(58),
        name="gate_edges",
    )(gates)


def front_kernel(packed, jac, dec, incr_out, key_out, group_out, grad_out, hid_out, lo_out, hi_out):
    senders = packed.shape[0]
    half = senders * 8
    slots = 2 * half
    levels = jac.shape[0]
    kinds = jac.shape[1] // LANES
    x = jnp.concatenate(
        [packed[:, 0:8, :].reshape(half, LANES).T, packed[:, 8:16, :].reshape(half, LANES).T],
        axis=1,
    )
    meta = packed[:, 16:24, :].reshape(half, LANES)
    meta_t = meta.astype(F32).T

    def line(q):
        return jnp.concatenate([meta_t[q : q + 1], meta_t[64 + q : 65 + q]], axis=1)

    def column(q):
        pick = iota((LANES, LANES), 0)
        a = dot(meta, (pick == q).astype(F32).astype(BF16))
        b = dot(meta, (pick == 64 + q).astype(F32).astype(BF16))
        return jnp.concatenate([a, b], axis=0)

    group = line(2)
    kind = line(3)
    group_out[...] = jnp.broadcast_to(group, (8, slots))
    spread = jnp.concatenate(
        [x * (kind == k).astype(F32).astype(BF16) for k in range(kinds)], axis=0
    )
    incr = dot(jac[...], spread).astype(BF16)
    incr_out[...] = incr
    key = column(0) * LANES + column(1) - iota((slots, LANES), 1).astype(F32)
    key_out[...] = key
    onehot = hot(key)
    last = CHUNK - 1
    lhs = jnp.concatenate(
        [incr * (group == g).astype(F32).astype(BF16) for g in (0, last)], axis=0
    )
    grad = dot(lhs, onehot)
    grad_out[...] = grad
    for side in range(2):
        part = grad[side * levels : (side + 1) * levels].astype(BF16)
        hidden = dot(dec[...], part)
        hid_out[side] = hidden
        (lo_out, hi_out)[side][...] = hidden.astype(BF16)


def hot(key):
    return jnp.concatenate(
        [jnp.where(key == float(r * LANES), 1.0, 0.0).astype(BF16) for r in range(CHUNK)], axis=1
    )


def front(packed, jac, dec):
    slots = packed.shape[0] * 16
    levels = jac.shape[0]
    cols = CHUNK * LANES
    sd = jax.ShapeDtypeStruct
    return pl.pallas_call(
        front_kernel,
        in_specs=[VMEM] * 3,
        out_specs=(VMEM,) * 7,
        out_shape=(
            sd((levels, slots), BF16),
            sd((slots, LANES), F32),
            sd((8, slots), F32),
            sd((2 * levels, cols), F32),
            sd((2, LANES, cols), F32),
            sd((LANES, cols), BF16),
            sd((LANES, cols), BF16),
        ),
        compiler_params=params(28),
        name="front",
    )(packed, jac, dec)


def conv(weight, taps):
    return dot(weight[...], jnp.concatenate(taps, axis=0))


def inner_layers(hid, ga, gb, gate_a, gate_b, wa, wb, near_out, finish):
    cols = CHUNK * LANES
    step = DIL * LANES
    total = hid.shape[1]
    for i in range(total // cols - 1):
        o = step + i * cols
        at = slice(o, o + cols)
        back = conv(wa, [ga[:, o + d : o + d + cols] for d in (step, 0, -step)])
        new = hid[:, at] + gate_a[:, at].astype(F32) * back
        hid[:, at] = new
        gb[:, at] = new.astype(BF16)
    near_out[0] = hid[:, step : step + cols]
    near_out[1] = hid[:, total - step - cols : total - step]
    for i in range(1, total // cols - 1):
        o = i * cols
        at = slice(o, o + cols)
        back = conv(wb, [gb[:, o + d : o + d + cols] for d in (step, 0, -step)])
        finish(i, hid[:, at] + gate_b[:, at].astype(F32) * back)


def mid_kernel(
    incr, key, group, hid_edge, g_lo, g_hi, dec, gate_a, gate_b, w,
    grad_out, hid_out, near_out, hid, ga, gb, lhs, onehot,
):
    cols = CHUNK * LANES
    levels = incr.shape[0]
    total = hid.shape[1]
    inner = total // cols - 2
    onehot[...] = hot(key[...])
    for g in range(inner):
        mask = (group[0:1, :] == float(g + 1)).astype(F32).astype(BF16)
        lhs[g * levels : (g + 1) * levels, :] = incr[...] * mask
    hid[:, 0:cols] = hid_edge[0]
    hid[:, total - cols : total] = hid_edge[1]
    ga[:, 0:cols] = g_lo[...]
    ga[:, total - cols : total] = g_hi[...]
    for n in range(0, cols, 256):
        grad_out[:, n : n + 256] = dot(lhs[...], onehot[:, n : n + 256])
    for g in range(inner):
        at = slice((g + 1) * cols, (g + 2) * cols)
        new = dot(dec[...], grad_out[g * levels : (g + 1) * levels, :].astype(BF16))
        hid[:, at] = new
        ga[:, at] = new.astype(BF16)

    def finish(i, value):
        hid_out[:, (i - 1) * cols : i * cols] = value

    inner_layers(hid, ga, gb, gate_a, gate_b, w.at[3], w.at[2], near_out, finish)


def mid(incr, key, group, hid_edge, g_lo, g_hi, dec, gate_a, gate_b, w):
    levels, slots = incr.shape
    channels, total = gate_a.shape
    cols = CHUNK * LANES
    inner = total // cols - 2
    sd = jax.ShapeDtypeStruct
    outs = (
        sd((inner * levels, cols), F32),
        sd((channels, inner * cols), F32),
        sd((2, channels, cols), F32),
    )
    return pl.pallas_call(
        mid_kernel,
        in_specs=[VMEM] * 10,
        out_specs=(VMEM,) * 3,
        out_shape=outs,
        scratch_shapes=[
            pltpu.VMEM((channels, total), F32),
            pltpu.VMEM((channels, total), BF16),
            pltpu.VMEM((channels, total), BF16),
            pltpu.VMEM((inner * levels, slots), BF16),
            pltpu.VMEM((slots, cols), BF16),
        ],
        compiler_params=params(24),
        name="mid",
    )(incr, key, group, hid_edge, g_lo, g_hi, dec, gate_a, gate_b, w)


def emit(enc, grad, value, tile):
    full = grad + dot(enc, value.astype(BF16))
    for r in range(CHUNK):
        for l in range(0, full.shape[0], 8):
            tile[pl.ds(l * CHUNK + r, 8, stride=CHUNK), :] = full[
                l : l + 8, r * LANES : (r + 1) * LANES
            ]


def send_tile(tile, out, chunk, sem):
    levels = out.shape[0]
    src = tile.reshape(tile.shape[0] // CHUNK, CHUNK, LANES)
    return pltpu.make_async_copy(
        src.at[0:levels], out.at[:, CHUNK * chunk : CHUNK * (chunk + 1), :], sem
    )


def last_kernel(
    hid_in, hid_edge, g_lo, g_hi, grad, enc, gate_a, gate_b, w,
    out, near_out, hid, ga, gb, tiles, sems,
):
    cols = CHUNK * LANES
    total = hid.shape[1]
    levels = enc.shape[0]
    hid[:, 0:cols] = hid_edge[0]
    hid[:, total - cols : total] = hid_edge[1]
    hid[:, cols : total - cols] = hid_in[...]
    ga[:, 0:cols] = g_lo[...]
    ga[:, total - cols : total] = g_hi[...]
    ga[:, cols : total - cols] = hid_in[...].astype(BF16)
    copies = []

    def finish(i, value):
        slot = (i - 1) % 2
        if i > 2:
            copies[i - 3].wait()
        emit(enc[...], grad[(i - 1) * levels : i * levels, :], value, tiles.at[slot])
        copy = send_tile(tiles.at[slot], out, i, sems.at[slot])
        copy.start()
        copies.append(copy)

    inner_layers(hid, ga, gb, gate_a, gate_b, w.at[1], w.at[0], near_out, finish)
    copies[-2].wait()
    copies[-1].wait()


def last(hid_in, hid_edge, g_lo, g_hi, grad, enc, gate_a, gate_b, w, out_shape):
    channels, total = gate_a.shape
    cols = CHUNK * LANES
    levels = enc.shape[0]
    sd = jax.ShapeDtypeStruct
    return pl.pallas_call(
        last_kernel,
        in_specs=[VMEM] * 9,
        out_specs=(HBM, VMEM),
        out_shape=(sd(out_shape, F32), sd((2, channels, cols), F32)),
        scratch_shapes=[
            pltpu.VMEM((channels, total), F32),
            pltpu.VMEM((channels, total), BF16),
            pltpu.VMEM((channels, total), BF16),
            pltpu.VMEM((2, levels * CHUNK, LANES), F32),
            pltpu.SemaphoreType.DMA((2,)),
        ],
        compiler_params=params(18),
        name="last",
    )(hid_in, hid_edge, g_lo, g_hi, grad, enc, gate_a, gate_b, w)


def edge_values(which, hid, g_lo, g_hi, halo_lo, halo_hi, near, gate_a, gate_b, ah_lo, ah_hi, w):
    cols = CHUNK * LANES
    step = DIL * LANES
    wa, wb = w.at[2 * which + 1], w.at[2 * which]
    total = gate_a.shape[1]
    result = []
    for side in range(2):
        if side == 0:
            field = jnp.concatenate([halo_lo[...], g_lo[...]], axis=1)
            old = jnp.concatenate([halo_lo[:, step:].astype(F32), hid[0, :, :step]], axis=1)
            gate = jnp.concatenate([ah_lo[which], gate_a[:, :step]], axis=1)
        else:
            field = jnp.concatenate([g_hi[...], halo_hi[...]], axis=1)
            old = jnp.concatenate([hid[1, :, step:], halo_hi[:, :step].astype(F32)], axis=1)
            gate = jnp.concatenate([gate_a[:, total - step :], ah_hi[which]], axis=1)
        back = conv(wa, [field[:, d : d + cols] for d in (2 * step, step, 0)])
        new = old + gate.astype(F32) * back
        own = slice(side * (total - cols), side * (total - cols) + cols)
        pieces = (new, near[0]) if side == 0 else (near[1], new)
        joined = jnp.concatenate(pieces, axis=1)
        field = joined.astype(BF16)
        back = conv(wb, [field[:, d : d + cols] for d in (2 * step, step, 0)])
        result.append(joined[:, step : step + cols] + gate_b[:, own].astype(F32) * back)
    return result


def edge_kernel(which, *refs):
    ins, (hid_out, lo_out, hi_out) = refs[:11], refs[12:]
    lo, hi = edge_values(which, *ins)
    hid_out[0] = lo
    hid_out[1] = hi
    lo_out[...] = lo.astype(BF16)
    hi_out[...] = hi.astype(BF16)


def edge_last_kernel(which, *refs):
    ins, (grad, enc, _), (out, tiles, sems) = refs[:11], refs[11:14], refs[14:]
    levels = enc.shape[0]
    values = edge_values(which, *ins)
    chunks = out.shape[1] // CHUNK
    copies = []
    for side in range(2):
        part = grad[side * levels : (side + 1) * levels, :]
        emit(enc[...], part, values[side], tiles.at[side])
        copy = send_tile(tiles.at[side], out, side * (chunks - 1), sems.at[side])
        copy.start()
        copies.append(copy)
    for copy in copies:
        copy.wait()


def edge(which, *args):
    sd = jax.ShapeDtypeStruct
    hid, g_lo = args[:2]
    return pl.pallas_call(
        functools.partial(edge_kernel, which),
        in_specs=[VMEM] * 11 + [ANY],
        out_specs=(VMEM,) * 3,
        out_shape=(sd(hid.shape, F32), sd(g_lo.shape, BF16), sd(g_lo.shape, BF16)),
        compiler_params=params(18),
        name="edge",
    )(*args)


def edge_last(which, *args):
    enc, state = args[12:]
    return pl.pallas_call(
        functools.partial(edge_last_kernel, which),
        in_specs=[VMEM] * 13 + [HBM],
        out_specs=HBM,
        out_shape=jax.ShapeDtypeStruct(state.shape, F32),
        scratch_shapes=[
            pltpu.VMEM((2, enc.shape[0] * CHUNK, LANES), F32),
            pltpu.SemaphoreType.DMA((2,)),
        ],
        input_output_aliases={13: 0},
        compiler_params=params(18),
        name="edge_last",
    )(*args)


def halos(lo, hi):
    count = lax.axis_size("lon")
    up = [(i, (i + 1) % count) for i in range(count)]
    down = [(b, a) for a, b in up]
    return lax.ppermute(hi, "lon", up), lax.ppermute(lo, "lon", down)


def per_device(resid, index, count, weight, jacobian, decoder, conv_weight, gates, encoder):
    dests = lax.axis_size("lat") * lax.axis_size("lon")
    packed = pack(resid, index, count, weight.reshape(1, -1), dests)
    packed = lax.all_to_all(packed, ("lat", "lon"), split_axis=0, concat_axis=0, tiled=True)
    gh_lo, gh_hi = halos(*gate_edges(gates))
    f3, f2, jac, dec, enc, w = prepare(gates, jacobian, decoder, encoder, conv_weight)
    incr, key, group, grad_e, hid_e, g_lo, g_hi = front(packed, jac, dec)
    halo_lo, halo_hi = halos(g_lo, g_hi)
    f1, f0 = later_gates(gates, group)
    grad_i, hid_i, near = mid(incr, key, group, hid_e, g_lo, g_hi, dec, f3, f2, w)
    hid_e, g_lo, g_hi = edge(
        1, hid_e, g_lo, g_hi, halo_lo, halo_hi, near, f3, f2, gh_lo, gh_hi, w, f1
    )
    halo_lo, halo_hi = halos(g_lo, g_hi)
    out_shape = (jacobian.shape[2],) + gates.shape[2:]
    state, near = last(hid_i, hid_e, g_lo, g_hi, grad_i, enc, f1, f0, w, out_shape)
    return edge_last(
        0, hid_e, g_lo, g_hi, halo_lo, halo_hi, near, f1, f0, gh_lo, gh_hi, w, grad_e, enc, state
    )


def solution(mesh):
    return jax.shard_map(
        per_device,
        mesh=mesh,
        in_specs=(
            P(None, ("lat", "lon")),
            P(None, ("lat", "lon")),
            P(None, ("lat", "lon")),
            P(),
            P(),
            P(),
            P(),
            P(None, None, "lon", "lat"),
            P(),
        ),
        out_specs=P(None, "lon", "lat"),
        check_vma=False,
    )
```

time: 106 us -> 70.5 us (0.67)
  local copies, waits for them, and re-layouts: 22.8 us -> 0.03 us
  Pallas kernels: 50.6 us -> 32.1 us
  starting transfers between devices: 29.4 us -> 34.8 us
    unnamed x59 -> x12, local copies, waits for them, and re-layouts: 19 us -> 0.03 us
    pallas_call x7 -> x9, Pallas kernels: 50.6 us -> 32.1 us  [the longest x1 6.24 us: prepare(): pl.pallas_call(prepare_kernel, in_specs=[HBM] + [VMEM] * 4, out_specs=(VM...]
    ppermute x6, starting transfers between devices: 18.2 us -> 23.6 us  [halos(): return (lax.ppermute(hi, 'lon', up), lax.ppermute(lo, 'lon', down))]
    pad x3 -> x0, local copies, waits for them, and re-layouts: 2 us -> none  [the longest x1 0.75 us: per_device(): jnp.pad(jacobian.transpose(2, 1, 0).reshape(levels, kinds * channels), ((...]
  transfers between devices with their start and end apart: 7 -> 7, of which waited for: 2 -> 3; matrix products, arithmetic and copies ran while one was open for 3% -> 0% of each run, Pallas kernels for 44% -> 38%
where the time goes in v2:
time: 70.5 us; the launch traced here: 69.4 us
  starting transfers between devices  34.8 us (49%)
  Pallas kernels  32.1 us (46%)
  waiting for transfers between devices  2.08 us (3%)
    ppermute x6, starting transfers between devices, halos(): return (lax.ppermute(hi, 'lon', up), lax.ppermute(lo, 'lon', down))  23.6 us
    all_to_all x1, starting transfers between devices, per_device(): lax.all_to_all(packed, ('lat', 'lon'), split_axis=0, concat_axis=0, tiled...  11.2 us
    pallas_call x1, Pallas kernels, prepare(): pl.pallas_call(prepare_kernel, in_specs=[HBM] + [VMEM] * 4, out_specs=(VM...  6.24 us
    pallas_call x1, Pallas kernels, mid(): pl.pallas_call(mid_kernel, in_specs=[VMEM] * 10, out_specs=(VMEM,) * 3, o...  6.18 us
    pallas_call x1, Pallas kernels, last(): pl.pallas_call(last_kernel, in_specs=[VMEM] * 9, out_specs=(HBM, VMEM), o...  5.22 us
    pallas_call x1, Pallas kernels, later_gates(): pl.pallas_call(later_gates_kernel, in_specs=[HBM, ANY], out_specs=(VMEM,)...  4.19 us
    pallas_call x1, Pallas kernels, front(): pl.pallas_call(front_kernel, in_specs=[VMEM] * 3, out_specs=(VMEM,) * 7,...  2.59 us
    pallas_call x1, Pallas kernels, pack(): pl.pallas_call(pack_kernel, in_specs=[HBM] * 4, out_specs=HBM, out_shape=...  2.53 us
  transfers between devices with their start and end apart: 7, of which 3 were waited for; matrix products, arithmetic and copies ran while one was open for 0% of the time, Pallas kernels for 38%

profile of v2, /device:TPU:0, one launch (start us, length us, event | category | flops | bytes accessed | tf_op | source)
XLA Modules:
  0.0 69.4 jit_solution(128924375683057419)
XLA Ops:
  0.0 2.5 %pack.1 = bf16[128,24,128]{2,1,0:T(8,128)(2,1)} custom-call(bf16[128,2048]{1,0:T(8,128)(2,1)} %resid_hbm.1, s32[2,2048]{1,0:T(2,128)} %index_hbm.1, s32[1,128]{1,0:T(1,128)} %count_hbm.1, f32[1,128]{1,0:T(1,128)} %bitcast.7), custom_call_target="tpu_custom_call" | custom-call | tf_op jit(solution)/shard_map/pack/pallas_call | solution.py:89
  2.5 11.2 %all-to-all-start = ((bf16[128,24,128]{2,1,0:T(8,128)(2,1)}), bf16[128,24,128]{2,1,0:T(8,128)(2,1)S(1)}, u32[]{:S(2)}, u32[]{:S(2)}) async-start(bf16[128,24,128]{2,1,0:T(8,128)(2,1)} %pack.1), calls=%async_computation | async-start | bytes 1572864 | tf_op jit(solution)/shard_map/all_to_all | solution.py:565
  13.7 0.0 copy-start.2
  13.7 0.0 copy-start.3
  13.7 0.0 copy-start.4
  13.8 0.0 copy-start.5
  13.8 2.1 %gate_edges.1 = (bf16[2,128,512]{2,1,0:T(8,128)(2,1)}, bf16[2,128,512]{2,1,0:T(8,128)(2,1)}) custom-call(bf16[4,128,64,128]{3,2,1,0:T(8,128)(2,1)} %src.5), custom_call_target="tpu_custom_call" | custom-call | tf_op jit(solution)/shard_map/gate_edges/pallas_call | solution.py:234
  15.9 2.5 %collective-permute-start.2 = (bf16[2,128,512]{2,1,0:T(8,128)(2,1)}, bf16[2,128,512]{2,1,0:T(8,128)(2,1)S(1)}, u32[]{:S(2)}, u32[]{:S(2)}) collective-permute-start(bf16[2,128,512]{2,1,0:T(8,128)(2,1)} %get-tuple-element.42), channel_id=1, source_target_pairs={{0,1},{1,2},{2,3},{3,4},{4,5},{5,6},{6,7},{7,8},{8,9},{9,10},{10,1... | collective-permute-start | bytes 786440 | tf_op jit(solution)/shard_map/ppermute | solution.py:559
  18.4 5.3 %collective-permute-start.3 = (bf16[2,128,512]{2,1,0:T(8,128)(2,1)}, bf16[2,128,512]{2,1,0:T(8,128)(2,1)S(1)}, u32[]{:S(2)}, u32[]{:S(2)}) collective-permute-start(bf16[2,128,512]{2,1,0:T(8,128)(2,1)} %get-tuple-element.43), channel_id=1, source_target_pairs={{1,0},{2,1},{3,2},{4,3},{5,4},{6,5},{7,6},{8,7},{9,8},{10,9},{11,1... | collective-permute-start | bytes 786440 | tf_op jit(solution)/shard_map/ppermute | solution.py:559
  23.7 0.0 copy-done.2
  23.7 0.0 copy-done.3
  23.7 0.0 copy-done.4
  23.7 0.0 copy-done.5
  23.7 6.2 %prepare.1 = (bf16[128,8192]{1,0:T(8,128)(2,1)}, bf16[128,8192]{1,0:T(8,128)(2,1)}, bf16[144,1024]{1,0:T(8,128)(2,1)S(1)}, bf16[128,144]{1,0:T(8,128)(2,1)S(1)},...) custom-call(bf16[4,128,64,128]{3,2,1,0:T(8,128)(2,1)} %src.5, bf16[137,8,128]{2,1,0:T(8,128)(2,1)S(1)} %bitcast.5, ...), custom_call_target="tpu_custom_call" | custom-call | tf_op jit(solution)/shard_map/prepare/pallas_call | solution.py:174
  30.0 0.3 all-to-all-done.packed
  30.3 2.6 %front.1 = (bf16[144,2048]{1,0:T(8,128)(2,1)S(1)}, f32[2048,128]{1,0:T(8,128)S(1)}, f32[8,2048]{1,0:T(8,128)S(1)}, f32[288,1024]{1,0:T(8,128)S(1)}, f32[2,128,10...) custom-call(bf16[128,24,128]{2,1,0:T(8,128)(2,1)S(1)} %all-to-all-done.packed, ...), custom_call_target="tpu_custom_call" | custom-call | tf_op jit(solution)/shard_map/front/pallas_call | solution.py:306
  32.9 1.4 %collective-permute-start = (bf16[128,1024]{1,0:T(8,128)(2,1)S(1)}, bf16[128,1024]{1,0:T(8,128)(2,1)S(1)}, u32[]{:S(2)}, u32[]{:S(2)}) collective-permute-start(bf16[128,1024]{1,0:T(8,128)(2,1)S(1)} %get-tuple-element.34.g_hi.refs_2_), channel_id=1, source_target_pairs={{0,1},{1,2},{2,3},{3,4},{4,5},{5,6},{6,7},{7,8},{8,9},{9,10},{10,1... | collective-permute-start | bytes 786440 | tf_op jit(solution)/shard_map/ppermute | solution.py:559
  34.3 6.4 %collective-permute-start.1 = (bf16[128,1024]{1,0:T(8,128)(2,1)S(1)}, bf16[128,1024]{1,0:T(8,128)(2,1)S(1)}, u32[]{:S(2)}, u32[]{:S(2)}) collective-permute-start(bf16[128,1024]{1,0:T(8,128)(2,1)S(1)} %get-tuple-element.33.g_lo.refs_1_), channel_id=1, source_target_pairs={{1,0},{2,1},{3,2},{4,3},{5,4},{6,5},{7,6},{8,7},{9,8},{10,9},{11,1... | collective-permute-start | bytes 786440 | tf_op jit(solution)/shard_map/ppermute | solution.py:559
  40.7 0.0 copy-start
  40.7 0.0 copy-start.1
  40.7 4.2 %later_gates.1 = (bf16[128,8192]{1,0:T(8,128)(2,1)S(1)}, bf16[128,8192]{1,0:T(8,128)(2,1)S(1)}) custom-call(bf16[4,128,64,128]{3,2,1,0:T(8,128)(2,1)} %src.5, f32[8,2048]{1,0:T(8,128)S(1)} %get-tuple-element.37.group.after), custom_call_target="tpu_custom_call" | custom-call | tf_op jit(solution)/shard_map/later_gates/pallas_call | solution.py:201
  44.9 0.0 copy-done
  44.9 0.0 copy-done.1
  44.9 6.2 %mid.1 = (f32[864,1024]{1,0:T(8,128)S(1)}, f32[128,6144]{1,0:T(8,128)S(1)}, f32[2,128,1024]{2,1,0:T(8,128)S(1)}) custom-call(bf16[144,2048]{1,0:T(8,128)(2,1)S(1)} %get-tuple-element.35.incr, f32[2048,128]{1,0:T(8,128)S(1)} %get-tuple-element.36.key, f32[8,2048]{1,0:T(8,128)S(1)} %get-tuple-element.37.group.after, ...), custom_call_target="tpu_custom_call" | custom-call | tf_op jit(solution)/shard_map/mid/pallas_call | solution.py:389
  51.1 0.0 collective-permute-done.2.refs_8_
  51.1 0.0 collective-permute-done.3.refs_9_
  51.1 0.0 collective-permute-done.refs_3_
  51.2 0.0 collective-permute-done.1.refs_4_
  51.2 1.0 %edge.1 = (f32[2,128,1024]{2,1,0:T(8,128)S(1)}, bf16[128,1024]{1,0:T(8,128)(2,1)S(1)}, bf16[128,1024]{1,0:T(8,128)(2,1)S(1)}) custom-call(f32[2,128,1024]{2,1,0:T(8,128)S(1)} %get-tuple-element.32.hid_edge.refs_0_, bf16[128,1024]{1,0:T(8,128)(2,1)S(1)} %get-tuple-element.33.g_lo.refs_1_, bf16[128,1024]{1,0:T(8,128)(2,1)S(1)} %get-tuple-element.34.g_hi.refs_2_, ...), custom_call_target="tpu_custom_call" | custom-call | tf_op jit(solution)/shard_map/edge/pallas_call | solution.py:528
  52.2 0.3 collective-permute-start.4
  52.4 7.7 %collective-permute-start.5 = (bf16[128,1024]{1,0:T(8,128)(2,1)S(1)}, bf16[128,1024]{1,0:T(8,128)(2,1)S(1)}, u32[]{:S(2)}, u32[]{:S(2)}) collective-permute-start(bf16[128,1024]{1,0:T(8,128)(2,1)S(1)} %get-tuple-element.46.g_lo.refs_1_), channel_id=1, source_target_pairs={{1,0},{2,1},{3,2},{4,3},{5,4},{6,5},{7,6},{8,7},{9,8},{10,9},{11,1... | collective-permute-start | bytes 786440 | tf_op jit(solution)/shard_map/ppermute | solution.py:559
  60.2 5.2 %last.1 = (f32[137,64,128]{2,1,0:T(8,128)}, f32[2,128,1024]{2,1,0:T(8,128)S(1)}) custom-call(f32[128,6144]{1,0:T(8,128)S(1)} %get-tuple-element.48.hid_in, f32[2,128,1024]{2,1,0:T(8,128)S(1)} %get-tuple-element.45.hid_edge.refs_0_, bf16[128,1024]{1,0:T(8,128)(2,1)S(1)} %get-tuple-element.46.g_lo.refs_1_, ...), custom_call_target="tpu_custom_call" | custom-call | tf_op jit(solution)/shard_map/last/pallas_call | solution.py:457
  65.4 0.5 collective-permute-done.4.refs_3_
  65.9 1.2 %collective-permute-done.5.refs_4_ = bf16[128,1024]{1,0:T(8,128)(2,1)S(1)} collective-permute-done((bf16[128,1024]{1,0:T(8,128)(2,1)S(1)}, bf16[128,1024]{1,0:T(8,128)(2,1)S(1)}, u32[]{:S(2)}, u32[]{:S(2)}) %collective-permute-start.5) | collective-permute-done | bytes 262176 | tf_op jit(solution)/shard_map/ppermute | solution.py:559
  67.1 2.1 %edge_last.1 = f32[137,64,128]{2,1,0:T(8,128)} custom-call(f32[2,128,1024]{2,1,0:T(8,128)S(1)} %get-tuple-element.45.hid_edge.refs_0_, bf16[128,1024]{1,0:T(8,128)(2,1)S(1)} %get-tuple-element.46.g_lo.refs_1_, bf16[128,1024]{1,0:T(8,128)(2,1)S(1)} %get-tuple-element.47.g_hi.refs_2_, ...), custom_call_target="tpu_custom_call", output_to_operand_aliasing={{}: (13, {})} | custom-call | tf_op jit(solution)/shard_map/edge_last/pallas_call | solution.py:540
Async XLA Ops:
  2.5 27.8 %all-to-all-start = ((bf16[128,24,128]{2,1,0:T(8,128)(2,1)}), bf16[128,24,128]{2,1,0:T(8,128)(2,1)S(1)}, u32[]{:S(2)}, u32[]{:S(2)}) async-start(bf16[128,24,128]{2,1,0:T(8,128)(2,1)} %pack.1), calls=%async_computation | async-start | bytes 1572864 | tf_op jit(solution)/shard_map/all_to_all | solution.py:565
  13.7 10.0 %copy-start.2 = (bf16[4,3,128,128]{3,2,1,0:T(8,128)(2,1)S(1)}, bf16[4,3,128,128]{3,2,1,0:T(8,128)(2,1)}, u32[]{:S(2)}) copy-start(bf16[4,3,128,128]{3,2,1,0:T(8,128)(2,1)} %param.15) | copy-start | bytes 1179652
  13.7 10.0 %copy-start.3 = (bf16[128,8,137]{0,1,2:T(8,128)(2,1)S(1)}, bf16[128,8,137]{0,1,2:T(8,128)(2,1)}, u32[]{:S(2)}) copy-start(bf16[128,8,137]{0,1,2:T(8,128)(2,1)} %param.13) | copy-start | bytes 841732
  13.7 10.0 %copy-start.4 = (bf16[137,128]{1,0:T(8,128)(2,1)S(1)}, bf16[137,128]{1,0:T(8,128)(2,1)}, u32[]{:S(2)}) copy-start(bf16[137,128]{1,0:T(8,128)(2,1)} %dec.1) | copy-start | bytes 105220
  13.8 9.9 %copy-start.5 = (bf16[128,137]{0,1:T(8,128)(2,1)S(1)}, bf16[128,137]{0,1:T(8,128)(2,1)}, u32[]{:S(2)}) copy-start(bf16[128,137]{0,1:T(8,128)(2,1)} %param.17) | copy-start | bytes 105220
  15.9 35.3 %collective-permute-start.2 = (bf16[2,128,512]{2,1,0:T(8,128)(2,1)}, bf16[2,128,512]{2,1,0:T(8,128)(2,1)S(1)}, u32[]{:S(2)}, u32[]{:S(2)}) collective-permute-start(bf16[2,128,512]{2,1,0:T(8,128)(2,1)} %get-tuple-element.42), channel_id=1, source_target_pairs={{0,1},{1,2},{2,3},{3,4},{4,5},{5,6},{6,7},{7,8},{8,9},{9,10},{10,1... | collective-permute-start | bytes 786440 | tf_op jit(solution)/shard_map/ppermute | solution.py:559
  18.4 32.7 %collective-permute-start.3 = (bf16[2,128,512]{2,1,0:T(8,128)(2,1)}, bf16[2,128,512]{2,1,0:T(8,128)(2,1)S(1)}, u32[]{:S(2)}, u32[]{:S(2)}) collective-permute-start(bf16[2,128,512]{2,1,0:T(8,128)(2,1)} %get-tuple-element.43), channel_id=1, source_target_pairs={{1,0},{2,1},{3,2},{4,3},{5,4},{6,5},{7,6},{8,7},{9,8},{10,9},{11,1... | collective-permute-start | bytes 786440 | tf_op jit(solution)/shard_map/ppermute | solution.py:559
  32.9 18.3 %collective-permute-start = (bf16[128,1024]{1,0:T(8,128)(2,1)S(1)}, bf16[128,1024]{1,0:T(8,128)(2,1)S(1)}, u32[]{:S(2)}, u32[]{:S(2)}) collective-permute-start(bf16[128,1024]{1,0:T(8,128)(2,1)S(1)} %get-tuple-element.34.g_hi.refs_2_), channel_id=1, source_target_pairs={{0,1},{1,2},{2,3},{3,4},{4,5},{5,6},{6,7},{7,8},{8,9},{9,10},{10,1... | collective-permute-start | bytes 786440 | tf_op jit(solution)/shard_map/ppermute | solution.py:559
  34.3 16.9 %collective-permute-start.1 = (bf16[128,1024]{1,0:T(8,128)(2,1)S(1)}, bf16[128,1024]{1,0:T(8,128)(2,1)S(1)}, u32[]{:S(2)}, u32[]{:S(2)}) collective-permute-start(bf16[128,1024]{1,0:T(8,128)(2,1)S(1)} %get-tuple-element.33.g_lo.refs_1_), channel_id=1, source_target_pairs={{1,0},{2,1},{3,2},{4,3},{5,4},{6,5},{7,6},{8,7},{9,8},{10,9},{11,1... | collective-permute-start | bytes 786440 | tf_op jit(solution)/shard_map/ppermute | solution.py:559
  40.7 4.2 %copy-start = (bf16[128,8192]{1,0:T(8,128)(2,1)S(1)}, bf16[128,8192]{1,0:T(8,128)(2,1)}, u32[]{:S(2)}) copy-start(bf16[128,8192]{1,0:T(8,128)(2,1)} %get-tuple-element.38.gate_a.refs_6_) | copy-start | bytes 6291460
  40.7 4.2 %copy-start.1 = (bf16[128,8192]{1,0:T(8,128)(2,1)S(1)}, bf16[128,8192]{1,0:T(8,128)(2,1)}, u32[]{:S(2)}) copy-start(bf16[128,8192]{1,0:T(8,128)(2,1)} %get-tuple-element.39.gate_b.refs_7_) | copy-start | bytes 6291460
  52.2 13.7 %collective-permute-start.4 = (bf16[128,1024]{1,0:T(8,128)(2,1)S(1)}, bf16[128,1024]{1,0:T(8,128)(2,1)S(1)}, u32[]{:S(2)}, u32[]{:S(2)}) collective-permute-start(bf16[128,1024]{1,0:T(8,128)(2,1)S(1)} %get-tuple-element.47.g_hi.refs_2_), channel_id=1, source_target_pairs={{0,1},{1,2},{2,3},{3,4},{4,5},{5,6},{6,7},{7,8},{8,9},{9,10},{10,1... | collective-permute-start | bytes 786440 | tf_op jit(solution)/shard_map/ppermute | solution.py:559
  52.4 14.7 %collective-permute-start.5 = (bf16[128,1024]{1,0:T(8,128)(2,1)S(1)}, bf16[128,1024]{1,0:T(8,128)(2,1)S(1)}, u32[]{:S(2)}, u32[]{:S(2)}) collective-permute-start(bf16[128,1024]{1,0:T(8,128)(2,1)S(1)} %get-tuple-element.46.g_lo.refs_1_), channel_id=1, source_target_pairs={{1,0},{2,1},{3,2},{4,3},{5,4},{6,5},{7,6},{8,7},{9,8},{10,9},{11,1... | collective-permute-start | bytes 786440 | tf_op jit(solution)/shard_map/ppermute | solution.py:559

commit v3 on v2

--- a/solution.py
+++ b/solution.py
@@ -111,42 +111,7 @@
     return jnp.concatenate([a, b], axis=0).astype(BF16)
 
 
-def flatten(src, order, outs, buf, wide, sems):
-    channels, lons, lats = src.shape[1:]
-    pitch = wide.shape[0] // channels
-    copies = [
-        pltpu.make_async_copy(src.at[k], buf.at[i], sems.at[i]) for i, k in enumerate(order)
-    ]
-    for copy in copies:
-        copy.start()
-    for i, out in enumerate(outs):
-        copies[i].wait()
-
-        def widen(c, carry):
-            wide[pl.ds(pl.multiple_of(c * pitch, 8), lons), :] = buf[i, c].astype(F32)
-            return carry
-
-        lax.fori_loop(0, channels, widen, 0, unroll=8)
-
-        def gather(lon, carry):
-            at = pl.ds(pl.multiple_of(lon * lats, lats), lats)
-            for c in range(0, channels, 16):
-                out[c : c + 16, at] = by_channel(wide, lon, pitch, c)
-            return carry
-
-        lax.fori_loop(0, lons, gather, 0, unroll=4)
-
-
-def gates_scratch(gates):
-    layers, channels, lons, lats = gates.shape
-    return [
-        pltpu.VMEM((2, channels, lons, lats), BF16),
-        pltpu.VMEM((channels * (lons + 8), lats), F32),
-        pltpu.SemaphoreType.DMA((2,)),
-    ]
-
-
-def prepare_kernel(src, jac, dec, enc, conv_w, f3, f2, jac_out, dec_out, enc_out, w_out, buf, wide, sems, rows, tall):
+def prepare_kernel(jac, dec, enc, conv_w, jac_out, dec_out, enc_out, w_out, rows, tall):
     levels, kinds = jac.shape[:2]
     padded = enc_out.shape[0]
     rows[...] = jnp.zeros_like(rows)
@@ -161,55 +126,35 @@
     dec_out[...] = tall[...].T[:, 0:padded].astype(BF16)
     for layer in range(conv_w.shape[0]):
         w_out[layer] = conv_w[layer].T
-    flatten(src, (3, 2), (f3, f2), buf, wide, sems)
-
-
-def prepare(gates, jacobian, decoder, encoder, conv_weight):
-    layers, channels, lons, lats = gates.shape
-    kinds, levels = jacobian.shape[1:]
+
+
+def prepare(jacobian, decoder, encoder, conv_weight):
+    channels, kinds, levels = jacobian.shape
+    layers = conv_weight.shape[0]
     padded = levels + -levels % 16
     conv_w = conv_weight.reshape(layers, -1, channels)
     sd = jax.ShapeDtypeStruct
-    flat = sd((channels, lons * lats), BF16)
     return pl.pallas_call(
         prepare_kernel,
-        in_specs=[HBM] + [VMEM] * 4,
-        out_specs=(VMEM,) * 6,
+        in_specs=[VMEM] * 4,
+        out_specs=(VMEM,) * 4,
         out_shape=(
-            flat,
-            flat,
             sd((padded, kinds * channels), BF16),
             sd((channels, padded), BF16),
             sd((padded, channels), BF16),
             sd((layers, channels, conv_w.shape[1]), BF16),
         ),
-        scratch_shapes=gates_scratch(gates)
-        + [pltpu.VMEM((padded * kinds, channels), F32), pltpu.VMEM((256, channels), F32)],
-        compiler_params=params(52),
+        scratch_shapes=[
+            pltpu.VMEM((padded * kinds, channels), F32),
+            pltpu.VMEM((256, channels), F32),
+        ],
+        compiler_params=params(12),
         name="prepare",
-    )(gates, jacobian.transpose(2, 1, 0), decoder, encoder.T, conv_w)
-
-
-def later_gates_kernel(src, after, f1, f0, buf, wide, sems):
+    )(jacobian.transpose(2, 1, 0), decoder, encoder.T, conv_w)
+
+
+def gate_edges_kernel(src, after, lo, hi, buf, wide, sems):
     del after
-    flatten(src, (1, 0), (f1, f0), buf, wide, sems)
-
-
-def later_gates(gates, after):
-    layers, channels, lons, lats = gates.shape
-    flat = jax.ShapeDtypeStruct((channels, lons * lats), BF16)
-    return pl.pallas_call(
-        later_gates_kernel,
-        in_specs=[HBM, ANY],
-        out_specs=(VMEM,) * 2,
-        out_shape=(flat,) * 2,
-        scratch_shapes=gates_scratch(gates),
-        compiler_params=params(46),
-        name="later_gates",
-    )(gates, after)
-
-
-def gate_edges_kernel(src, lo, hi, buf, wide, sems):
     channels, lons, lats = src.shape[1:]
     copies = []
     for k in range(2):
@@ -228,12 +173,12 @@
                     out[k, c : c + 16, r * lats : (r + 1) * lats] = value
 
 
-def gate_edges(gates):
+def gate_edges(gates, after):
     layers, channels, lons, lats = gates.shape
     send = jax.ShapeDtypeStruct((2, channels, DIL * lats), BF16)
     return pl.pallas_call(
         gate_edges_kernel,
-        in_specs=[HBM],
+        in_specs=[HBM, ANY],
         out_specs=(VMEM,) * 2,
         out_shape=(send,) * 2,
         scratch_shapes=[
@@ -243,7 +188,7 @@
         ],
         compiler_params=params(58),
         name="gate_edges",
-    )(gates)
+    )(gates, after)
 
 
 def front_kernel(packed, jac, dec, incr_out, key_out, group_out, grad_out, hid_out, lo_out, hi_out):
@@ -325,33 +270,87 @@
     return dot(weight[...], jnp.concatenate(taps, axis=0))
 
 
-def inner_layers(hid, ga, gb, gate_a, gate_b, wa, wb, near_out, finish):
+def pieces(low, inside, high, start, size):
+    parts = []
+    at = 0
+    for ref in (low, inside, high):
+        first, stop = max(start - at, 0), min(start + size - at, ref.shape[1])
+        if first < stop:
+            parts.append(ref[:, first:stop])
+        at += ref.shape[1]
+    return parts[0] if len(parts) == 1 else jnp.concatenate(parts, axis=1)
+
+
+def load_gates(gates, layer, bufs, sems):
+    copies = [
+        pltpu.make_async_copy(gates.at[layer - i], bufs.at[i], sems.at[i]) for i in range(2)
+    ]
+    for copy in copies:
+        copy.start()
+    return copies
+
+
+def widen(copy, buf, wide):
+    channels, lons = buf.shape[:2]
+    pitch = wide.shape[0] // channels
+    copy.wait()
+
+    def body(c, carry):
+        wide[pl.ds(pl.multiple_of(c * pitch, 8), lons), :] = buf[c].astype(F32)
+        return carry
+
+    lax.fori_loop(0, channels, body, 0, unroll=8)
+
+
+def gate_rows(wide, lon, count, channels):
+    pitch = wide.shape[0] // channels
+    columns = [
+        jnp.concatenate(
+            [wide[pl.ds(c * pitch + r, 8, stride=pitch), :] for c in range(0, channels, 8)], axis=0
+        )
+        for r in range(lon, lon + count)
+    ]
+    return jnp.concatenate(columns, axis=1)
+
+
+def inner_layers(low, inside, high, old, hid, gb, load, bufs, wide, wa, wb, near_out, finish, ends=None):
     cols = CHUNK * LANES
     step = DIL * LANES
-    total = hid.shape[1]
-    for i in range(total // cols - 1):
+    channels, total = hid.shape
+    count = total // cols
+    widen(load[0], bufs.at[0], wide)
+    for i in range(count - 1):
         o = step + i * cols
         at = slice(o, o + cols)
-        back = conv(wa, [ga[:, o + d : o + d + cols] for d in (step, 0, -step)])
-        new = hid[:, at] + gate_a[:, at].astype(F32) * back
+        taps = [pieces(low, inside, high, o + d, cols) for d in (step, 0, -step)]
+        back = conv(wa, taps)
+        new = old(o, cols) + gate_rows(wide, o // LANES, CHUNK, channels) * back
         hid[:, at] = new
         gb[:, at] = new.astype(BF16)
     near_out[0] = hid[:, step : step + cols]
     near_out[1] = hid[:, total - step - cols : total - step]
-    for i in range(1, total // cols - 1):
+    lons = total // LANES
+    if ends is not None:
+        ends[0] = gate_rows(wide, 0, DIL, channels).astype(BF16)
+        ends[1] = gate_rows(wide, lons - DIL, DIL, channels).astype(BF16)
+    widen(load[1], bufs.at[1], wide)
+    for i in range(1, count - 1):
         o = i * cols
         at = slice(o, o + cols)
         back = conv(wb, [gb[:, o + d : o + d + cols] for d in (step, 0, -step)])
-        finish(i, hid[:, at] + gate_b[:, at].astype(F32) * back)
+        finish(i, hid[:, at] + gate_rows(wide, o // LANES, CHUNK, channels) * back)
 
 
 def mid_kernel(
-    incr, key, group, hid_edge, g_lo, g_hi, dec, gate_a, gate_b, w,
-    grad_out, hid_out, near_out, hid, ga, gb, lhs, onehot,
+    incr, key, group, hid_edge, g_lo, g_hi, dec, gates, w,
+    grad_out, hid_out, field_out, near_out, ends_a, ends_b,
+    hid, ga, gb, lhs, onehot, bufs, wide, sems,
 ):
+    load = load_gates(gates, 3, bufs, sems)
     cols = CHUNK * LANES
+    step = DIL * LANES
     levels = incr.shape[0]
-    total = hid.shape[1]
+    channels, total = hid.shape
     inner = total // cols - 2
     onehot[...] = hot(key[...])
     for g in range(inner):
@@ -359,48 +358,68 @@
         lhs[g * levels : (g + 1) * levels, :] = incr[...] * mask
     hid[:, 0:cols] = hid_edge[0]
     hid[:, total - cols : total] = hid_edge[1]
-    ga[:, 0:cols] = g_lo[...]
-    ga[:, total - cols : total] = g_hi[...]
     for n in range(0, cols, 256):
         grad_out[:, n : n + 256] = dot(lhs[...], onehot[:, n : n + 256])
     for g in range(inner):
-        at = slice((g + 1) * cols, (g + 2) * cols)
         new = dot(dec[...], grad_out[g * levels : (g + 1) * levels, :].astype(BF16))
-        hid[:, at] = new
-        ga[:, at] = new.astype(BF16)
+        hid[:, (g + 1) * cols : (g + 2) * cols] = new
+        ga[:, g * cols : (g + 1) * cols] = new.astype(BF16)
+
+    def old(o, size):
+        return hid[:, o : o + size]
 
     def finish(i, value):
         hid_out[:, (i - 1) * cols : i * cols] = value
-
-    inner_layers(hid, ga, gb, gate_a, gate_b, w.at[3], w.at[2], near_out, finish)
-
-
-def mid(incr, key, group, hid_edge, g_lo, g_hi, dec, gate_a, gate_b, w):
+        field_out[:, (i - 1) * cols : i * cols] = value.astype(BF16)
+
+    inner_layers(
+        g_lo, ga, g_hi, old, hid, gb, load, bufs, wide, w.at[3], w.at[2], near_out, finish, ends_a
+    )
+    lons = total // LANES
+    ends_b[0] = gate_rows(wide, 0, CHUNK, channels).astype(BF16)
+    ends_b[1] = gate_rows(wide, lons - CHUNK, CHUNK, channels).astype(BF16)
+
+
+def gates_scratch(gates):
+    channels, lons, lats = gates.shape[1:]
+    return [
+        pltpu.VMEM((2, channels, lons, lats), BF16),
+        pltpu.VMEM((channels * (lons + 8), lats), F32),
+        pltpu.SemaphoreType.DMA((2,)),
+    ]
+
+
+def mid(incr, key, group, hid_edge, g_lo, g_hi, dec, gates, w):
     levels, slots = incr.shape
-    channels, total = gate_a.shape
+    channels, lons, lats = gates.shape[1:]
+    total = lons * lats
     cols = CHUNK * LANES
     inner = total // cols - 2
     sd = jax.ShapeDtypeStruct
     outs = (
         sd((inner * levels, cols), F32),
         sd((channels, inner * cols), F32),
+        sd((channels, inner * cols), BF16),
         sd((2, channels, cols), F32),
+        sd((2, channels, DIL * LANES), BF16),
+        sd((2, channels, cols), BF16),
     )
     return pl.pallas_call(
         mid_kernel,
-        in_specs=[VMEM] * 10,
-        out_specs=(VMEM,) * 3,
+        in_specs=[VMEM] * 7 + [HBM, VMEM],
+        out_specs=(VMEM,) * 6,
         out_shape=outs,
         scratch_shapes=[
             pltpu.VMEM((channels, total), F32),
-            pltpu.VMEM((channels, total), BF16),
+            pltpu.VMEM((channels, inner * cols), BF16),
             pltpu.VMEM((channels, total), BF16),
             pltpu.VMEM((inner * levels, slots), BF16),
             pltpu.VMEM((slots, cols), BF16),
-        ],
-        compiler_params=params(24),
+        ]
+        + gates_scratch(gates),
+        compiler_params=params(44),
         name="mid",
-    )(incr, key, group, hid_edge, g_lo, g_hi, dec, gate_a, gate_b, w)
+    )(incr, key, group, hid_edge, g_lo, g_hi, dec, gates, w)
 
 
 def emit(enc, grad, value, tile):
@@ -421,19 +440,17 @@
 
 
 def last_kernel(
-    hid_in, hid_edge, g_lo, g_hi, grad, enc, gate_a, gate_b, w,
-    out, near_out, hid, ga, gb, tiles, sems,
+    hid_in, field_in, hid_edge, g_lo, g_hi, grad, enc, gates, w,
+    out, near_out, ends_a, ends_b, hid, gb, tiles, sems, bufs, wide, gate_sems,
 ):
+    load = load_gates(gates, 1, bufs, gate_sems)
     cols = CHUNK * LANES
-    total = hid.shape[1]
+    channels, total = hid.shape
     levels = enc.shape[0]
-    hid[:, 0:cols] = hid_edge[0]
-    hid[:, total - cols : total] = hid_edge[1]
-    hid[:, cols : total - cols] = hid_in[...]
-    ga[:, 0:cols] = g_lo[...]
-    ga[:, total - cols : total] = g_hi[...]
-    ga[:, cols : total - cols] = hid_in[...].astype(BF16)
     copies = []
+
+    def old(o, size):
+        return pieces(hid_edge.at[0], hid_in, hid_edge.at[1], o, size)
 
     def finish(i, value):
         slot = (i - 1) % 2
@@ -444,61 +461,70 @@
         copy.start()
         copies.append(copy)
 
-    inner_layers(hid, ga, gb, gate_a, gate_b, w.at[1], w.at[0], near_out, finish)
+    inner_layers(
+        g_lo, field_in, g_hi, old, hid, gb, load, bufs, wide, w.at[1], w.at[0], near_out, finish, ends_a
+    )
+    lons = total // LANES
+    ends_b[0] = gate_rows(wide, 0, CHUNK, channels).astype(BF16)
+    ends_b[1] = gate_rows(wide, lons - CHUNK, CHUNK, channels).astype(BF16)
     copies[-2].wait()
     copies[-1].wait()
 
 
-def last(hid_in, hid_edge, g_lo, g_hi, grad, enc, gate_a, gate_b, w, out_shape):
-    channels, total = gate_a.shape
+def last(hid_in, field_in, hid_edge, g_lo, g_hi, grad, enc, gates, w, out_shape):
+    channels, lons, lats = gates.shape[1:]
+    total = lons * lats
     cols = CHUNK * LANES
     levels = enc.shape[0]
     sd = jax.ShapeDtypeStruct
     return pl.pallas_call(
         last_kernel,
-        in_specs=[VMEM] * 9,
-        out_specs=(HBM, VMEM),
-        out_shape=(sd(out_shape, F32), sd((2, channels, cols), F32)),
+        in_specs=[VMEM] * 7 + [HBM, VMEM],
+        out_specs=(HBM, VMEM, VMEM, VMEM),
+        out_shape=(
+            sd(out_shape, F32),
+            sd((2, channels, cols), F32),
+            sd((2, channels, DIL * LANES), BF16),
+            sd((2, channels, cols), BF16),
+        ),
         scratch_shapes=[
             pltpu.VMEM((channels, total), F32),
             pltpu.VMEM((channels, total), BF16),
-            pltpu.VMEM((channels, total), BF16),
             pltpu.VMEM((2, levels * CHUNK, LANES), F32),
             pltpu.SemaphoreType.DMA((2,)),
-        ],
-        compiler_params=params(18),
+        ]
+        + gates_scratch(gates),
+        compiler_params=params(46),
         name="last",
-    )(hid_in, hid_edge, g_lo, g_hi, grad, enc, gate_a, gate_b, w)
+    )(hid_in, field_in, hid_edge, g_lo, g_hi, grad, enc, gates, w)
 
 
 def edge_values(which, hid, g_lo, g_hi, halo_lo, halo_hi, near, gate_a, gate_b, ah_lo, ah_hi, w):
     cols = CHUNK * LANES
     step = DIL * LANES
     wa, wb = w.at[2 * which + 1], w.at[2 * which]
-    total = gate_a.shape[1]
     result = []
     for side in range(2):
         if side == 0:
             field = jnp.concatenate([halo_lo[...], g_lo[...]], axis=1)
             old = jnp.concatenate([halo_lo[:, step:].astype(F32), hid[0, :, :step]], axis=1)
-            gate = jnp.concatenate([ah_lo[which], gate_a[:, :step]], axis=1)
+            gate = jnp.concatenate([ah_lo[which], gate_a[0]], axis=1)
         else:
             field = jnp.concatenate([g_hi[...], halo_hi[...]], axis=1)
             old = jnp.concatenate([hid[1, :, step:], halo_hi[:, :step].astype(F32)], axis=1)
-            gate = jnp.concatenate([gate_a[:, total - step :], ah_hi[which]], axis=1)
+            gate = jnp.concatenate([gate_a[1], ah_hi[which]], axis=1)
         back = conv(wa, [field[:, d : d + cols] for d in (2 * step, step, 0)])
         new = old + gate.astype(F32) * back
-        own = slice(side * (total - cols), side * (total - cols) + cols)
         pieces = (new, near[0]) if side == 0 else (near[1], new)
         joined = jnp.concatenate(pieces, axis=1)
         field = joined.astype(BF16)
         back = conv(wb, [field[:, d : d + cols] for d in (2 * step, step, 0)])
-        result.append(joined[:, step : step + cols] + gate_b[:, own].astype(F32) * back)
+        result.append(joined[:, step : step + cols] + gate_b[side].astype(F32) * back)
     return result
 
 
 def edge_kernel(which, *refs):
-    ins, (hid_out, lo_out, hi_out) = refs[:11], refs[12:]
+    ins, (hid_out, lo_out, hi_out) = refs[:11], refs[11:]
     lo, hi = edge_values(which, *ins)
     hid_out[0] = lo
     hid_out[1] = hi
@@ -527,7 +553,7 @@
     hid, g_lo = args[:2]
     return pl.pallas_call(
         functools.partial(edge_kernel, which),
-        in_specs=[VMEM] * 11 + [ANY],
+        in_specs=[VMEM] * 11,
         out_specs=(VMEM,) * 3,
         out_shape=(sd(hid.shape, F32), sd(g_lo.shape, BF16), sd(g_lo.shape, BF16)),
         compiler_params=params(18),
@@ -563,20 +589,24 @@
     dests = lax.axis_size("lat") * lax.axis_size("lon")
     packed = pack(resid, index, count, weight.reshape(1, -1), dests)
     packed = lax.all_to_all(packed, ("lat", "lon"), split_axis=0, concat_axis=0, tiled=True)
-    gh_lo, gh_hi = halos(*gate_edges(gates))
-    f3, f2, jac, dec, enc, w = prepare(gates, jacobian, decoder, encoder, conv_weight)
+    jac, dec, enc, w = prepare(jacobian, decoder, encoder, conv_weight)
+    gh_lo, gh_hi = halos(*gate_edges(gates, dec))
     incr, key, group, grad_e, hid_e, g_lo, g_hi = front(packed, jac, dec)
     halo_lo, halo_hi = halos(g_lo, g_hi)
-    f1, f0 = later_gates(gates, group)
-    grad_i, hid_i, near = mid(incr, key, group, hid_e, g_lo, g_hi, dec, f3, f2, w)
+    grad_i, hid_i, field_i, near, end_a, end_b = mid(
+        incr, key, group, hid_e, g_lo, g_hi, dec, gates, w
+    )
     hid_e, g_lo, g_hi = edge(
-        1, hid_e, g_lo, g_hi, halo_lo, halo_hi, near, f3, f2, gh_lo, gh_hi, w, f1
+        1, hid_e, g_lo, g_hi, halo_lo, halo_hi, near, end_a, end_b, gh_lo, gh_hi, w
     )
     halo_lo, halo_hi = halos(g_lo, g_hi)
     out_shape = (jacobian.shape[2],) + gates.shape[2:]
-    state, near = last(hid_i, hid_e, g_lo, g_hi, grad_i, enc, f1, f0, w, out_shape)
+    state, near, end_a, end_b = last(
+        hid_i, field_i, hid_e, g_lo, g_hi, grad_i, enc, gates, w, out_shape
+    )
     return edge_last(
-        0, hid_e, g_lo, g_hi, halo_lo, halo_hi, near, f1, f0, gh_lo, gh_hi, w, grad_e, enc, state
+        0, hid_e, g_lo, g_hi, halo_lo, halo_hi, near, end_a, end_b, gh_lo, gh_hi, w,
+        grad_e, enc, state,
     )
 
 

time: 70.5 us -> 71.3 us (1.011); the launches traced: 69.4 us -> 70.9 us
  starting transfers between devices: 34.8 us -> 27.9 us
  local copies, waits for them, and re-layouts: 0.03 us -> 5.78 us
  waiting for transfers between devices: 2.08 us -> 7.57 us
  Pallas kernels: 32.1 us -> 29.4 us
    ppermute x6, starting transfers between devices: 23.6 us -> 16.7 us  [halos(): return (lax.ppermute(hi, 'lon', up), lax.ppermute(lo, 'lon', down))]
    unnamed x12 -> x14, local copies, waits for them, and re-layouts: 0.03 us -> 5.78 us
    ppermute x6, waiting for transfers between devices: 1.74 us -> 6.07 us  [halos(): return (lax.ppermute(hi, 'lon', up), lax.ppermute(lo, 'lon', down))]
    pallas_call x5 -> x4, Pallas kernels: 23.9 us -> 21.3 us  [the longest x1 10.8 us: last(): pl.pallas_call(last_kernel, in_specs=[VMEM] * 7 + [HBM, VMEM], out_specs=...]
    all_to_all x1, waiting for transfers between devices: 0.34 us -> 1.5 us  [per_device(): lax.all_to_all(packed, ('lat', 'lon'), split_axis=0, concat_axis=0, tiled...]
  transfers between devices with their start and end apart: 7 -> 7, of which waited for: 3 -> 3; matrix products, arithmetic and copies ran while one was open for 0% -> 0% of each run, Pallas kernels for 38% -> 34%
where the time goes in v3:
time: 71.3 us; the launch traced here: 70.9 us
  Pallas kernels  29.4 us (41%)
  starting transfers between devices  27.9 us (39%)
  waiting for transfers between devices  7.57 us (11%)
  local copies, waits for them, and re-layouts  5.78 us (8%)
    ppermute x6, starting transfers between devices, halos(): return (lax.ppermute(hi, 'lon', up), lax.ppermute(lo, 'lon', down))  16.7 us
    all_to_all x1, starting transfers between devices, per_device(): lax.all_to_all(packed, ('lat', 'lon'), split_axis=0, concat_axis=0, tiled...  11.2 us
    pallas_call x1, Pallas kernels, last(): pl.pallas_call(last_kernel, in_specs=[VMEM] * 7 + [HBM, VMEM], out_specs=...  10.8 us
    pallas_call x1, Pallas kernels, mid(): pl.pallas_call(mid_kernel, in_specs=[VMEM] * 7 + [HBM, VMEM], out_specs=(...  8.15 us
    ppermute x6, waiting for transfers between devices, halos(): return (lax.ppermute(hi, 'lon', up), lax.ppermute(lo, 'lon', down))  6.07 us
    unnamed x14, local copies, waits for them, and re-layouts  5.78 us
    pallas_call x1, Pallas kernels, front(): pl.pallas_call(front_kernel, in_specs=[VMEM] * 3, out_specs=(VMEM,) * 7,...  2.6 us
    pallas_call x1, Pallas kernels, pack(): pl.pallas_call(pack_kernel, in_specs=[HBM] * 4, out_specs=HBM, out_shape=...  2.51 us
  transfers between devices with their start and end apart: 7, of which 3 were waited for; matrix products, arithmetic and copies ran while one was open for 0% of the time, Pallas kernels for 34%

profile of v3, /device:TPU:0, one launch (start us, length us, event | category | flops | bytes accessed | tf_op | source)
XLA Modules:
  0.0 70.9 jit_solution(10848506564141824435)
XLA Ops:
  0.0 2.5 %pack.1 = bf16[128,24,128]{2,1,0:T(8,128)(2,1)} custom-call(bf16[128,2048]{1,0:T(8,128)(2,1)} %resid_hbm.1, s32[2,2048]{1,0:T(2,128)} %index_hbm.1, s32[1,128]{1,0:T(1,128)} %count_hbm.1, f32[1,128]{1,0:T(1,128)} %bitcast.7), custom_call_target="tpu_custom_call" | custom-call | tf_op jit(solution)/shard_map/pack/pallas_call | solution.py:89
  2.5 11.2 %all-to-all-start = ((bf16[128,24,128]{2,1,0:T(8,128)(2,1)}), bf16[128,24,128]{2,1,0:T(8,128)(2,1)S(1)}, u32[]{:S(2)}, u32[]{:S(2)}) async-start(bf16[128,24,128]{2,1,0:T(8,128)(2,1)} %pack.1), calls=%async_computation | async-start | bytes 1572864 | tf_op jit(solution)/shard_map/all_to_all | solution.py:591
  13.7 0.0 copy-start.3
  13.7 1.0 %copy-done.3 = bf16[4,3,128,128]{3,2,1,0:T(8,128)(2,1)S(1)} copy-done((bf16[4,3,128,128]{3,2,1,0:T(8,128)(2,1)S(1)}, bf16[4,3,128,128]{3,2,1,0:T(8,128)(2,1)}, u32[]{:S(2)}) %copy-start.3) | copy-done | bytes 393240
  14.7 0.0 copy-start.4
  14.7 1.0 %copy-done.4 = bf16[128,8,137]{0,1,2:T(8,128)(2,1)S(1)} copy-done((bf16[128,8,137]{0,1,2:T(8,128)(2,1)S(1)}, bf16[128,8,137]{0,1,2:T(8,128)(2,1)}, u32[]{:S(2)}) %copy-start.4) | copy-done | bytes 280600
  15.7 0.0 copy-start.5
  15.7 0.8 %copy-done.5 = bf16[137,128]{1,0:T(8,128)(2,1)S(1)} copy-done((bf16[137,128]{1,0:T(8,128)(2,1)S(1)}, bf16[137,128]{1,0:T(8,128)(2,1)}, u32[]{:S(2)}) %copy-start.5) | copy-done | bytes 35096
  16.4 0.0 copy-start.6
  16.4 0.8 %copy-done.6 = bf16[128,137]{0,1:T(8,128)(2,1)S(1)} copy-done((bf16[128,137]{0,1:T(8,128)(2,1)S(1)}, bf16[128,137]{0,1:T(8,128)(2,1)}, u32[]{:S(2)}) %copy-start.6) | copy-done | bytes 35096
  17.2 0.3 prepare.1
  17.5 0.0 copy-start.1
  17.5 0.6 copy-done.1
  18.1 0.0 copy-start.2
  18.1 2.1 %gate_edges.1 = (bf16[2,128,512]{2,1,0:T(8,128)(2,1)}, bf16[2,128,512]{2,1,0:T(8,128)(2,1)}) custom-call(bf16[4,128,64,128]{3,2,1,0:T(8,128)(2,1)} %gates.3, bf16[128,144]{1,0:T(8,128)(2,1)} %copy-done.1), custom_call_target="tpu_custom_call" | custom-call | tf_op jit(solution)/shard_map/gate_edges/pallas_call | solution.py:179
  20.2 2.5 %collective-permute-start.2 = (bf16[2,128,512]{2,1,0:T(8,128)(2,1)}, bf16[2,128,512]{2,1,0:T(8,128)(2,1)S(1)}, u32[]{:S(2)}, u32[]{:S(2)}) collective-permute-start(bf16[2,128,512]{2,1,0:T(8,128)(2,1)} %get-tuple-element.43), channel_id=1, source_target_pairs={{0,1},{1,2},{2,3},{3,4},{4,5},{5,6},{6,7},{7,8},{8,9},{9,10},{10,1... | collective-permute-start | bytes 786440 | tf_op jit(solution)/shard_map/ppermute | solution.py:585
  22.7 5.3 %collective-permute-start.3 = (bf16[2,128,512]{2,1,0:T(8,128)(2,1)}, bf16[2,128,512]{2,1,0:T(8,128)(2,1)S(1)}, u32[]{:S(2)}, u32[]{:S(2)}) collective-permute-start(bf16[2,128,512]{2,1,0:T(8,128)(2,1)} %get-tuple-element.44), channel_id=1, source_target_pairs={{1,0},{2,1},{3,2},{4,3},{5,4},{6,5},{7,6},{8,7},{9,8},{10,9},{11,1... | collective-permute-start | bytes 786440 | tf_op jit(solution)/shard_map/ppermute | solution.py:585
  28.0 1.5 %all-to-all-done.packed = bf16[128,24,128]{2,1,0:T(8,128)(2,1)S(1)} async-done(((bf16[128,24,128]{2,1,0:T(8,128)(2,1)}), bf16[128,24,128]{2,1,0:T(8,128)(2,1)S(1)}, u32[]{:S(2)}, u32[]{:S(2)}) %all-to-all-start) | async-done | bytes 786464 | tf_op jit(solution)/shard_map/all_to_all | solution.py:591
  29.5 0.0 copy-done.2
  29.5 2.6 %front.1 = (bf16[144,2048]{1,0:T(8,128)(2,1)S(1)}, f32[2048,128]{1,0:T(8,128)S(1)}, f32[8,2048]{1,0:T(8,128)S(1)}, f32[288,1024]{1,0:T(8,128)S(1)}, f32[2,128,10...) custom-call(bf16[128,24,128]{2,1,0:T(8,128)(2,1)S(1)} %all-to-all-done.packed, ...), custom_call_target="tpu_custom_call" | custom-call | tf_op jit(solution)/shard_map/front/pallas_call | solution.py:251
  32.1 2.0 %collective-permute-start.1 = (bf16[128,1024]{1,0:T(8,128)(2,1)S(1)}, bf16[128,1024]{1,0:T(8,128)(2,1)S(1)}, u32[]{:S(2)}, u32[]{:S(2)}) collective-permute-start(bf16[128,1024]{1,0:T(8,128)(2,1)S(1)} %get-tuple-element.34.g_lo.refs_1_), channel_id=1, source_target_pairs={{1,0},{2,1},{3,2},{4,3},{5,4},{6,5},{7,6},{8,7},{9,8},{10,9},{11,1... | collective-permute-start | bytes 786440 | tf_op jit(solution)/shard_map/ppermute | solution.py:585
  34.1 1.6 %collective-permute-start = (bf16[128,1024]{1,0:T(8,128)(2,1)S(1)}, bf16[128,1024]{1,0:T(8,128)(2,1)S(1)}, u32[]{:S(2)}, u32[]{:S(2)}) collective-permute-start(bf16[128,1024]{1,0:T(8,128)(2,1)S(1)} %get-tuple-element.35.g_hi.refs_2_), channel_id=1, source_target_pairs={{0,1},{1,2},{2,3},{3,4},{4,5},{5,6},{6,7},{7,8},{8,9},{9,10},{10,1... | collective-permute-start | bytes 786440 | tf_op jit(solution)/shard_map/ppermute | solution.py:585
  35.7 8.2 %mid.1 = (f32[864,1024]{1,0:T(8,128)}, f32[128,6144]{1,0:T(8,128)S(1)}, bf16[128,6144]{1,0:T(8,128)(2,1)S(1)}, f32[2,128,1024]{2,1,0:T(8,128)S(1)}, bf16[2,128,5...) custom-call(bf16[144,2048]{1,0:T(8,128)(2,1)S(1)} %get-tuple-element.36.incr, ...), custom_call_target="tpu_custom_call" | custom-call | tf_op jit(solution)/shard_map/mid/pallas_call | solution.py:407
  43.9 0.0 copy-start
  43.9 1.7 %copy-done = f32[128,6144]{1,0:T(8,128)} copy-done((f32[128,6144]{1,0:T(8,128)}, f32[128,6144]{1,0:T(8,128)S(1)}, u32[]{:S(2)}) %copy-start) | copy-done | bytes 3145752
  45.6 0.0 collective-permute-done.2.refs_8_
  45.6 0.0 collective-permute-done.3.refs_9_
  45.6 3.9 %collective-permute-done.1.refs_4_ = bf16[128,1024]{1,0:T(8,128)(2,1)S(1)} collective-permute-done((bf16[128,1024]{1,0:T(8,128)(2,1)S(1)}, bf16[128,1024]{1,0:T(8,128)(2,1)S(1)}, u32[]{:S(2)}, u32[]{:S(2)}) %collective-permute-start.1) | collective-permute-done | bytes 262176 | tf_op jit(solution)/shard_map/ppermute | solution.py:585
  49.5 0.0 collective-permute-done.refs_3_
  49.5 1.0 %edge.1 = (f32[2,128,1024]{2,1,0:T(8,128)S(1)}, bf16[128,1024]{1,0:T(8,128)(2,1)S(1)}, bf16[128,1024]{1,0:T(8,128)(2,1)S(1)}) custom-call(f32[2,128,1024]{2,1,0:T(8,128)S(1)} %get-tuple-element.33.hid_edge.refs_0_, bf16[128,1024]{1,0:T(8,128)(2,1)S(1)} %get-tuple-element.34.g_lo.refs_1_, bf16[128,1024]{1,0:T(8,128)(2,1)S(1)} %get-tuple-element.35.g_hi.refs_2_, ...), custom_call_target="tpu_custom_call" | custom-call | tf_op jit(solution)/shard_map/edge/pallas_call | solution.py:554
  50.4 5.3 %collective-permute-start.5 = (bf16[128,1024]{1,0:T(8,128)(2,1)S(1)}, bf16[128,1024]{1,0:T(8,128)(2,1)S(1)}, u32[]{:S(2)}, u32[]{:S(2)}) collective-permute-start(bf16[128,1024]{1,0:T(8,128)(2,1)S(1)} %get-tuple-element.46.g_lo.refs_1_), channel_id=1, source_target_pairs={{1,0},{2,1},{3,2},{4,3},{5,4},{6,5},{7,6},{8,7},{9,8},{10,9},{11,1... | collective-permute-start | bytes 786440 | tf_op jit(solution)/shard_map/ppermute | solution.py:585
  55.7 0.0 collective-permute-start.4
  55.7 10.8 %last.1 = (f32[137,64,128]{2,1,0:T(8,128)}, f32[2,128,1024]{2,1,0:T(8,128)S(1)}, bf16[2,128,512]{2,1,0:T(8,128)(2,1)S(1)}, bf16[2,128,1024]{2,1,0:T(8,128)(2,1)S(1)}) custom-call(f32[128,6144]{1,0:T(8,128)} %copy-done, bf16[128,6144]{1,0:T(8,128)(2,1)S(1)} %get-tuple-element.49.field_in, f32[2,128,1024]{2,1,0:T(8,128)S(1)} %get-tuple-element.45.hid_edge.refs_0_, ...), custom_call_target="tpu_custom_call" | custom-call | tf_op jit(solution)/shard_map/last/pallas_call | solution.py:480
  66.5 0.0 collective-permute-done.5.refs_4_
  66.5 2.2 %collective-permute-done.4.refs_3_ = bf16[128,1024]{1,0:T(8,128)(2,1)S(1)} collective-permute-done((bf16[128,1024]{1,0:T(8,128)(2,1)S(1)}, bf16[128,1024]{1,0:T(8,128)(2,1)S(1)}, u32[]{:S(2)}, u32[]{:S(2)}) %collective-permute-start.4) | collective-permute-done | bytes 262176 | tf_op jit(solution)/shard_map/ppermute | solution.py:585
  68.7 2.1 %edge_last.1 = f32[137,64,128]{2,1,0:T(8,128)} custom-call(f32[2,128,1024]{2,1,0:T(8,128)S(1)} %get-tuple-element.45.hid_edge.refs_0_, bf16[128,1024]{1,0:T(8,128)(2,1)S(1)} %get-tuple-element.46.g_lo.refs_1_, bf16[128,1024]{1,0:T(8,128)(2,1)S(1)} %get-tuple-element.47.g_hi.refs_2_, ...), custom_call_target="tpu_custom_call", output_to_operand_aliasing={{}: (13, {})} | custom-call | tf_op jit(solution)/shard_map/edge_last/pallas_call | solution.py:566
Async XLA Ops:
  2.5 27.0 %all-to-all-start = ((bf16[128,24,128]{2,1,0:T(8,128)(2,1)}), bf16[128,24,128]{2,1,0:T(8,128)(2,1)S(1)}, u32[]{:S(2)}, u32[]{:S(2)}) async-start(bf16[128,24,128]{2,1,0:T(8,128)(2,1)} %pack.1), calls=%async_computation | async-start | bytes 1572864 | tf_op jit(solution)/shard_map/all_to_all | solution.py:591
  13.7 1.0 %copy-start.3 = (bf16[4,3,128,128]{3,2,1,0:T(8,128)(2,1)S(1)}, bf16[4,3,128,128]{3,2,1,0:T(8,128)(2,1)}, u32[]{:S(2)}) copy-start(bf16[4,3,128,128]{3,2,1,0:T(8,128)(2,1)} %param.15) | copy-start | bytes 1179652
  14.7 1.0 %copy-start.4 = (bf16[128,8,137]{0,1,2:T(8,128)(2,1)S(1)}, bf16[128,8,137]{0,1,2:T(8,128)(2,1)}, u32[]{:S(2)}) copy-start(bf16[128,8,137]{0,1,2:T(8,128)(2,1)} %param.13) | copy-start | bytes 841732
  15.7 0.8 %copy-start.5 = (bf16[137,128]{1,0:T(8,128)(2,1)S(1)}, bf16[137,128]{1,0:T(8,128)(2,1)}, u32[]{:S(2)}) copy-start(bf16[137,128]{1,0:T(8,128)(2,1)} %dec.1) | copy-start | bytes 105220
  16.4 0.8 %copy-start.6 = (bf16[128,137]{0,1:T(8,128)(2,1)S(1)}, bf16[128,137]{0,1:T(8,128)(2,1)}, u32[]{:S(2)}) copy-start(bf16[128,137]{0,1:T(8,128)(2,1)} %param.17) | copy-start | bytes 105220
  17.5 0.6 copy-start.1
  18.1 11.4 %copy-start.2 = (bf16[128,144]{1,0:T(8,128)(2,1)S(1)}, bf16[128,144]{1,0:T(8,128)(2,1)}, u32[]{:S(2)}) copy-start(bf16[128,144]{1,0:T(8,128)(2,1)} %copy-done.1) | copy-start | bytes 110596
  20.2 25.4 %collective-permute-start.2 = (bf16[2,128,512]{2,1,0:T(8,128)(2,1)}, bf16[2,128,512]{2,1,0:T(8,128)(2,1)S(1)}, u32[]{:S(2)}, u32[]{:S(2)}) collective-permute-start(bf16[2,128,512]{2,1,0:T(8,128)(2,1)} %get-tuple-element.43), channel_id=1, source_target_pairs={{0,1},{1,2},{2,3},{3,4},{4,5},{5,6},{6,7},{7,8},{8,9},{9,10},{10,1... | collective-permute-start | bytes 786440 | tf_op jit(solution)/shard_map/ppermute | solution.py:585
  22.7 22.8 %collective-permute-start.3 = (bf16[2,128,512]{2,1,0:T(8,128)(2,1)}, bf16[2,128,512]{2,1,0:T(8,128)(2,1)S(1)}, u32[]{:S(2)}, u32[]{:S(2)}) collective-permute-start(bf16[2,128,512]{2,1,0:T(8,128)(2,1)} %get-tuple-element.44), channel_id=1, source_target_pairs={{1,0},{2,1},{3,2},{4,3},{5,4},{6,5},{7,6},{8,7},{9,8},{10,9},{11,1... | collective-permute-start | bytes 786440 | tf_op jit(solution)/shard_map/ppermute | solution.py:585
  32.1 17.4 %collective-permute-start.1 = (bf16[128,1024]{1,0:T(8,128)(2,1)S(1)}, bf16[128,1024]{1,0:T(8,128)(2,1)S(1)}, u32[]{:S(2)}, u32[]{:S(2)}) collective-permute-start(bf16[128,1024]{1,0:T(8,128)(2,1)S(1)} %get-tuple-element.34.g_lo.refs_1_), channel_id=1, source_target_pairs={{1,0},{2,1},{3,2},{4,3},{5,4},{6,5},{7,6},{8,7},{9,8},{10,9},{11,1... | collective-permute-start | bytes 786440 | tf_op jit(solution)/shard_map/ppermute | solution.py:585
  34.1 15.4 %collective-permute-start = (bf16[128,1024]{1,0:T(8,128)(2,1)S(1)}, bf16[128,1024]{1,0:T(8,128)(2,1)S(1)}, u32[]{:S(2)}, u32[]{:S(2)}) collective-permute-start(bf16[128,1024]{1,0:T(8,128)(2,1)S(1)} %get-tuple-element.35.g_hi.refs_2_), channel_id=1, source_target_pairs={{0,1},{1,2},{2,3},{3,4},{4,5},{5,6},{6,7},{7,8},{8,9},{9,10},{10,1... | collective-permute-start | bytes 786440 | tf_op jit(solution)/shard_map/ppermute | solution.py:585
  43.9 1.7 %copy-start = (f32[128,6144]{1,0:T(8,128)}, f32[128,6144]{1,0:T(8,128)S(1)}, u32[]{:S(2)}) copy-start(f32[128,6144]{1,0:T(8,128)S(1)} %get-tuple-element.48.hid_in) | copy-start | bytes 9437188
  50.4 16.0 %collective-permute-start.5 = (bf16[128,1024]{1,0:T(8,128)(2,1)S(1)}, bf16[128,1024]{1,0:T(8,128)(2,1)S(1)}, u32[]{:S(2)}, u32[]{:S(2)}) collective-permute-start(bf16[128,1024]{1,0:T(8,128)(2,1)S(1)} %get-tuple-element.46.g_lo.refs_1_), channel_id=1, source_target_pairs={{1,0},{2,1},{3,2},{4,3},{5,4},{6,5},{7,6},{8,7},{9,8},{10,9},{11,1... | collective-permute-start | bytes 786440 | tf_op jit(solution)/shard_map/ppermute | solution.py:585
  55.7 12.9 %collective-permute-start.4 = (bf16[128,1024]{1,0:T(8,128)(2,1)S(1)}, bf16[128,1024]{1,0:T(8,128)(2,1)S(1)}, u32[]{:S(2)}, u32[]{:S(2)}) collective-permute-start(bf16[128,1024]{1,0:T(8,128)(2,1)S(1)} %get-tuple-element.47.g_hi.refs_2_), channel_id=1, source_target_pairs={{0,1},{1,2},{2,3},{3,4},{4,5},{5,6},{6,7},{7,8},{8,9},{9,10},{10,1... | collective-permute-start | bytes 786440 | tf_op jit(solution)/shard_map/ppermute | solution.py:585

commit v4 on v3

--- a/solution.py
+++ b/solution.py
@@ -31,6 +31,7 @@
     parts, dests = out.shape[:2]
     slots = resid.shape[2]
     per = slots // dests
+    pairs = per // 2
     small = [
         pltpu.make_async_copy(index_hbm, index, in_sems.at[parts]),
         pltpu.make_async_copy(count_hbm, count, in_sems.at[parts + 1]),
@@ -43,33 +44,42 @@
         src = resid_hbm.at[:, p * slots : (p + 1) * slots]
         large.append(pltpu.make_async_copy(src, resid.at[p], in_sems.at[p]))
         large[-1].start()
+    width = LANES // pairs
+    row = iota((LANES, slots), 0) & (width - 1)
+    lane, slot = iota((LANES, slots), 0), iota((LANES, slots), 1)
+    mine = ((slot & (per - 1)) >> 1) == (lane >> (width.bit_length() - 1))
+    shift = per.bit_length() - 1
+    fold_to, fold_from = iota((2 * dests, slots), 0), iota((2 * dests, slots), 1)
+    fold = ((fold_from >> shift) * 2 + (fold_from & 1)) == fold_to
+    fold = fold.astype(F32).astype(BF16)
+    own = (iota((dests, slots), 1) >> shift) == iota((dests, slots), 0)
+    own = own.astype(F32).astype(BF16)
+    place = (iota((1, slots), 1) & (per - 1)).astype(F32)
+    total = dests * parts
     for copy in small:
         copy.wait()
     scale = jnp.broadcast_to(weight[...], (LANES, LANES)).T
     scale = jnp.concatenate([scale] * (slots // LANES), axis=1)
-    total = dests * parts
     counts = jnp.broadcast_to(count[...].astype(F32), (8, total)).astype(BF16)
-    row = iota((LANES, slots), 0) & 63
-    lane = iota((dests, 8, LANES), 2)
+    for copy in large:
+        copy.wait()
     sends = []
     for p in range(parts):
         at = slice(p * slots, (p + 1) * slots)
-        spread = iota((total, slots), 1) // per + p * dests == iota((total, slots), 0)
-        used = dot(counts, spread.astype(F32).astype(BF16))[0:1]
+        used = dot(counts[:, p * dests : (p + 1) * dests], own)[0:1]
         cell = index[0:1, at]
         kind = index[1:2, at].astype(F32)
-        valid = (iota((1, slots), 1) % per).astype(F32) < used
+        valid = place < used
         low = ((cell >> 7) & (CHUNK - 1)).astype(F32)
         lat = (cell & (LANES - 1)).astype(F32)
         group = jnp.where(valid, (cell >> 10).astype(F32), UNUSED)
         meta = jnp.where(row == 0, low, jnp.where(row == 1, lat, jnp.where(row == 2, group, kind)))
-        meta = meta.astype(BF16).T.reshape(dests, 2, 8, LANES)
-        first = meta[:, 0].astype(F32)
-        second = meta[:, 1].astype(F32)
-        out[p, :, per : per + 8, :] = jnp.where(lane < 64, first, second).astype(BF16)
-        large[p].wait()
+        meta = jnp.where(mine, meta, 0.0).astype(BF16)
+        meta = lax.dot_general(fold, meta, (((1,), (1,)), ((), ())), preferred_element_type=F32)
+        out[p, :, pairs : pairs + 1] = meta.astype(BF16).reshape(dests, 1, 2, LANES)
         weighted = scale * resid[p].astype(F32)
-        out[p, :, 0:per, :] = weighted.astype(BF16).T.reshape(dests, per, LANES)
+        out[p, :, 0:pairs] = weighted.astype(BF16).T.reshape(dests, pairs, 2, LANES)
+    for p in range(parts):
         dst = out_hbm.at[p * dests : (p + 1) * dests]
         sends.append(pltpu.make_async_copy(out.at[p], dst, out_sems.at[p]))
         sends[-1].start()
@@ -90,13 +100,13 @@
         pack_kernel,
         in_specs=[HBM] * 4,
         out_specs=HBM,
-        out_shape=jax.ShapeDtypeStruct((dests, per + 8, LANES), BF16),
+        out_shape=jax.ShapeDtypeStruct((dests, per // 2 + 1, 2, LANES), BF16),
         scratch_shapes=[
             pltpu.VMEM((parts, channels, slots // parts), BF16),
             pltpu.VMEM(index.shape, jnp.int32),
             pltpu.VMEM(count.shape, jnp.int32),
             pltpu.VMEM(weight.shape, F32),
-            pltpu.VMEM((parts, dests // parts, per + 8, LANES), BF16),
+            pltpu.VMEM((parts, dests // parts, per // 2 + 1, 2, LANES), BF16),
             pltpu.SemaphoreType.DMA((parts + 3,)),
             pltpu.SemaphoreType.DMA((parts,)),
         ],
@@ -111,7 +121,8 @@
     return jnp.concatenate([a, b], axis=0).astype(BF16)
 
 
-def prepare_kernel(jac, dec, enc, conv_w, jac_out, dec_out, enc_out, w_out, rows, tall):
+def prepare_kernel(jac, dec, enc, conv_w, after, jac_out, dec_out, enc_out, w_out, rows, tall):
+    del after
     levels, kinds = jac.shape[:2]
     padded = enc_out.shape[0]
     rows[...] = jnp.zeros_like(rows)
@@ -128,7 +139,7 @@
         w_out[layer] = conv_w[layer].T
 
 
-def prepare(jacobian, decoder, encoder, conv_weight):
+def prepare(jacobian, decoder, encoder, conv_weight, after):
     channels, kinds, levels = jacobian.shape
     layers = conv_weight.shape[0]
     padded = levels + -levels % 16
@@ -136,7 +147,7 @@
     sd = jax.ShapeDtypeStruct
     return pl.pallas_call(
         prepare_kernel,
-        in_specs=[VMEM] * 4,
+        in_specs=[VMEM] * 4 + [ANY],
         out_specs=(VMEM,) * 4,
         out_shape=(
             sd((padded, kinds * channels), BF16),
@@ -148,13 +159,12 @@
             pltpu.VMEM((padded * kinds, channels), F32),
             pltpu.VMEM((256, channels), F32),
         ],
-        compiler_params=params(12),
+        compiler_params=params(20),
         name="prepare",
-    )(jacobian.transpose(2, 1, 0), decoder, encoder.T, conv_w)
-
-
-def gate_edges_kernel(src, after, lo, hi, buf, wide, sems):
-    del after
+    )(jacobian.transpose(2, 1, 0), decoder, encoder.T, conv_w, after)
+
+
+def gate_edges_kernel(src, lo, hi, buf, wide, sems):
     channels, lons, lats = src.shape[1:]
     copies = []
     for k in range(2):
@@ -173,12 +183,12 @@
                     out[k, c : c + 16, r * lats : (r + 1) * lats] = value
 
 
-def gate_edges(gates, after):
+def gate_edges(gates):
     layers, channels, lons, lats = gates.shape
     send = jax.ShapeDtypeStruct((2, channels, DIL * lats), BF16)
     return pl.pallas_call(
         gate_edges_kernel,
-        in_specs=[HBM, ANY],
+        in_specs=[HBM],
         out_specs=(VMEM,) * 2,
         out_shape=(send,) * 2,
         scratch_shapes=[
@@ -188,30 +198,28 @@
         ],
         compiler_params=params(58),
         name="gate_edges",
-    )(gates, after)
+    )(gates)
 
 
 def front_kernel(packed, jac, dec, incr_out, key_out, group_out, grad_out, hid_out, lo_out, hi_out):
-    senders = packed.shape[0]
-    half = senders * 8
-    slots = 2 * half
+    senders, pairs = packed.shape[0], packed.shape[1] - 1
+    part = 2 * senders
+    slots = pairs * part
+    width = LANES // pairs
     levels = jac.shape[0]
     kinds = jac.shape[1] // LANES
-    x = jnp.concatenate(
-        [packed[:, 0:8, :].reshape(half, LANES).T, packed[:, 8:16, :].reshape(half, LANES).T],
-        axis=1,
-    )
-    meta = packed[:, 16:24, :].reshape(half, LANES)
+    x = jnp.concatenate([packed[:, m].reshape(part, LANES).T for m in range(pairs)], axis=1)
+    meta = packed[:, pairs].reshape(part, LANES)
     meta_t = meta.astype(F32).T
 
     def line(q):
-        return jnp.concatenate([meta_t[q : q + 1], meta_t[64 + q : 65 + q]], axis=1)
-
-    def column(q):
-        pick = iota((LANES, LANES), 0)
-        a = dot(meta, (pick == q).astype(F32).astype(BF16))
-        b = dot(meta, (pick == 64 + q).astype(F32).astype(BF16))
-        return jnp.concatenate([a, b], axis=0)
+        rows = [m * width + q for m in range(pairs)]
+        return jnp.concatenate([meta_t[r : r + 1] for r in rows], axis=1)
+
+    def place(m):
+        source = iota((LANES, LANES), 0) - m * width
+        pick = jnp.where(source == 0, float(LANES), jnp.where(source == 1, 1.0, 0.0))
+        return dot(meta, pick.astype(BF16))
 
     group = line(2)
     kind = line(3)
@@ -221,7 +229,8 @@
     )
     incr = dot(jac[...], spread).astype(BF16)
     incr_out[...] = incr
-    key = column(0) * LANES + column(1) - iota((slots, LANES), 1).astype(F32)
+    key = jnp.concatenate([place(m) for m in range(pairs)], axis=0)
+    key = key - iota((slots, LANES), 1).astype(F32)
     key_out[...] = key
     onehot = hot(key)
     last = CHUNK - 1
@@ -244,7 +253,7 @@
 
 
 def front(packed, jac, dec):
-    slots = packed.shape[0] * 16
+    slots = packed.shape[0] * (packed.shape[1] - 1) * 2
     levels = jac.shape[0]
     cols = CHUNK * LANES
     sd = jax.ShapeDtypeStruct
@@ -417,7 +426,7 @@
             pltpu.VMEM((slots, cols), BF16),
         ]
         + gates_scratch(gates),
-        compiler_params=params(44),
+        compiler_params=params(40),
         name="mid",
     )(incr, key, group, hid_edge, g_lo, g_hi, dec, gates, w)
 
@@ -494,7 +503,7 @@
             pltpu.SemaphoreType.DMA((2,)),
         ]
         + gates_scratch(gates),
-        compiler_params=params(46),
+        compiler_params=params(40),
         name="last",
     )(hid_in, field_in, hid_edge, g_lo, g_hi, grad, enc, gates, w)
 
@@ -589,8 +598,9 @@
     dests = lax.axis_size("lat") * lax.axis_size("lon")
     packed = pack(resid, index, count, weight.reshape(1, -1), dests)
     packed = lax.all_to_all(packed, ("lat", "lon"), split_axis=0, concat_axis=0, tiled=True)
-    jac, dec, enc, w = prepare(jacobian, decoder, encoder, conv_weight)
-    gh_lo, gh_hi = halos(*gate_edges(gates, dec))
+    gate_lo, gate_hi = gate_edges(gates)
+    gh_lo, gh_hi = halos(gate_lo, gate_hi)
+    jac, dec, enc, w = prepare(jacobian, decoder, encoder, conv_weight, gate_lo)
     incr, key, group, grad_e, hid_e, g_lo, g_hi = front(packed, jac, dec)
     halo_lo, halo_hi = halos(g_lo, g_hi)
     grad_i, hid_i, field_i, near, end_a, end_b = mid(

time: 71.3 us -> 68.2 us (0.957)
  waiting for transfers between devices: 7.57 us -> 12.9 us
  local copies, waits for them, and re-layouts: 5.78 us -> 0.99 us
  Pallas kernels: 29.4 us -> 26.6 us
  starting transfers between devices: 27.9 us -> 27.1 us
    unnamed x14 -> x10, local copies, waits for them, and re-layouts: 5.78 us -> 0.99 us
    ppermute x6, waiting for transfers between devices: 6.07 us -> 9.79 us  [halos(): return (lax.ppermute(hi, 'lon', up), lax.ppermute(lo, 'lon', down))]
    pallas_call x1, Pallas kernels: 10.8 us -> 7.83 us  [last(): pl.pallas_call(last_kernel, in_specs=[VMEM] * 7 + [HBM, VMEM], out_specs=...]
    all_to_all x1, waiting for transfers between devices: 1.5 us -> 3.15 us  [per_device(): lax.all_to_all(packed, ('lat', 'lon'), split_axis=0, concat_axis=0, tiled...]
    ppermute x6, starting transfers between devices: 16.7 us -> 15.9 us  [halos(): return (lax.ppermute(hi, 'lon', up), lax.ppermute(lo, 'lon', down))]
  transfers between devices with their start and end apart: 7 -> 7, of which waited for: 3 -> 3; matrix products, arithmetic and copies ran while one was open for 0% -> 0% of each run, Pallas kernels for 34% -> 30%
where the time goes in v4:
time: 68.2 us; the launch traced here: 67.9 us
  starting transfers between devices  27.1 us (40%)
  Pallas kernels  26.6 us (39%)
  waiting for transfers between devices  12.9 us (19%)
  local copies, waits for them, and re-layouts  0.99 us (1%)
    ppermute x6, starting transfers between devices, halos(): return (lax.ppermute(hi, 'lon', up), lax.ppermute(lo, 'lon', down))  15.9 us
    all_to_all x1, starting transfers between devices, per_device(): lax.all_to_all(packed, ('lat', 'lon'), split_axis=0, concat_axis=0, tiled...  11.2 us
    ppermute x6, waiting for transfers between devices, halos(): return (lax.ppermute(hi, 'lon', up), lax.ppermute(lo, 'lon', down))  9.79 us
    pallas_call x1, Pallas kernels, last(): pl.pallas_call(last_kernel, in_specs=[VMEM] * 7 + [HBM, VMEM], out_specs=...  7.83 us
    pallas_call x1, Pallas kernels, mid(): pl.pallas_call(mid_kernel, in_specs=[VMEM] * 7 + [HBM, VMEM], out_specs=(...  7.76 us
    all_to_all x1, waiting for transfers between devices, per_device(): lax.all_to_all(packed, ('lat', 'lon'), split_axis=0, concat_axis=0, tiled...  3.15 us
    pallas_call x1, Pallas kernels, pack(): pl.pallas_call(pack_kernel, in_specs=[HBM] * 4, out_specs=HBM, out_shape=...  2.92 us
    pallas_call x1, Pallas kernels, front(): pl.pallas_call(front_kernel, in_specs=[VMEM] * 3, out_specs=(VMEM,) * 7,...  2.61 us
  transfers between devices with their start and end apart: 7, of which 3 were waited for; matrix products, arithmetic and copies ran while one was open for 0% of the time, Pallas kernels for 30%

profile of v4, /device:TPU:0, one launch (start us, length us, event | category | flops | bytes accessed | tf_op | source)
XLA Modules:
  0.0 67.9 jit_solution(10168835637014811122)
XLA Ops:
  0.0 2.9 %pack.1 = bf16[128,9,2,128]{3,2,1,0:T(2,128)(2,1)} custom-call(bf16[128,2048]{1,0:T(8,128)(2,1)} %resid_hbm.1, s32[2,2048]{1,0:T(2,128)} %index_hbm.1, s32[1,128]{1,0:T(1,128)} %count_hbm.1, f32[1,128]{1,0:T(1,128)} %bitcast.7), custom_call_target="tpu_custom_call" | custom-call | tf_op jit(solution)/shard_map/pack/pallas_call | solution.py:99
  2.9 11.2 %all-to-all-start = ((bf16[128,9,2,128]{3,2,1,0:T(2,128)(2,1)}), bf16[128,9,2,128]{3,2,1,0:T(2,128)(2,1)S(1)}, u32[]{:S(2)}, u32[]{:S(2)}) async-start(bf16[128,9,2,128]{3,2,1,0:T(2,128)(2,1)} %pack.1), calls=%async_computation | async-start | bytes 1179648 | tf_op jit(solution)/shard_map/all_to_all | solution.py:600
  14.1 0.0 copy-start
  14.1 0.0 copy-start.1
  14.1 0.0 copy-start.3
  14.2 0.0 copy-start.4
  14.2 2.1 %gate_edges.1 = (bf16[2,128,512]{2,1,0:T(8,128)(2,1)}, bf16[2,128,512]{2,1,0:T(8,128)(2,1)}) custom-call(bf16[4,128,64,128]{3,2,1,0:T(8,128)(2,1)} %gates.3), custom_call_target="tpu_custom_call" | custom-call | tf_op jit(solution)/shard_map/gate_edges/pallas_call | solution.py:189
  16.3 2.5 %collective-permute-start.2 = (bf16[2,128,512]{2,1,0:T(8,128)(2,1)}, bf16[2,128,512]{2,1,0:T(8,128)(2,1)S(1)}, u32[]{:S(2)}, u32[]{:S(2)}) collective-permute-start(bf16[2,128,512]{2,1,0:T(8,128)(2,1)} %get-tuple-element.44), channel_id=1, source_target_pairs={{0,1},{1,2},{2,3},{3,4},{4,5},{5,6},{6,7},{7,8},{8,9},{9,10},{10,1... | collective-permute-start | bytes 786440 | tf_op jit(solution)/shard_map/ppermute | solution.py:594
  18.8 5.3 %collective-permute-start.3 = (bf16[2,128,512]{2,1,0:T(8,128)(2,1)}, bf16[2,128,512]{2,1,0:T(8,128)(2,1)S(1)}, u32[]{:S(2)}, u32[]{:S(2)}) collective-permute-start(bf16[2,128,512]{2,1,0:T(8,128)(2,1)} %get-tuple-element.31.after), channel_id=1, source_target_pairs={{1,0},{2,1},{3,2},{4,3},{5,4},{6,5},{7,6},{8,7},{9,8},{10,9},{11,1... | collective-permute-start | bytes 786440 | tf_op jit(solution)/shard_map/ppermute | solution.py:594
  24.1 0.0 copy-done
  24.1 0.0 copy-done.1
  24.1 0.0 copy-done.3
  24.1 0.0 copy-done.4
  24.1 0.0 copy-start.2
  24.1 1.0 %copy-done.2 = bf16[2,128,512]{2,1,0:T(8,128)(2,1)S(1)} copy-done((bf16[2,128,512]{2,1,0:T(8,128)(2,1)S(1)}, bf16[2,128,512]{2,1,0:T(8,128)(2,1)}, u32[]{:S(2)}) %copy-start.2) | copy-done | bytes 262168
  25.1 0.3 prepare.1
  25.4 3.1 %all-to-all-done.packed = bf16[128,9,2,128]{3,2,1,0:T(2,128)(2,1)S(1)} async-done(((bf16[128,9,2,128]{3,2,1,0:T(2,128)(2,1)}), bf16[128,9,2,128]{3,2,1,0:T(2,128)(2,1)S(1)}, u32[]{:S(2)}, u32[]{:S(2)}) %all-to-all-start) | async-done | bytes 589856 | tf_op jit(solution)/shard_map/all_to_all | solution.py:600
  28.5 2.6 %front.1 = (bf16[144,2048]{1,0:T(8,128)(2,1)S(1)}, f32[2048,128]{1,0:T(8,128)S(1)}, f32[8,2048]{1,0:T(8,128)S(1)}, f32[288,1024]{1,0:T(8,128)S(1)}, f32[2,128,10...) custom-call(bf16[128,9,2,128]{3,2,1,0:T(2,128)(2,1)S(1)} %all-to-all-done.packed, ...), custom_call_target="tpu_custom_call" | custom-call | tf_op jit(solution)/shard_map/front/pallas_call | solution.py:260
  31.1 1.2 %collective-permute-start.1 = (bf16[128,1024]{1,0:T(8,128)(2,1)S(1)}, bf16[128,1024]{1,0:T(8,128)(2,1)S(1)}, u32[]{:S(2)}, u32[]{:S(2)}) collective-permute-start(bf16[128,1024]{1,0:T(8,128)(2,1)S(1)} %get-tuple-element.35.g_lo.refs_1_), channel_id=1, source_target_pairs={{1,0},{2,1},{3,2},{4,3},{5,4},{6,5},{7,6},{8,7},{9,8},{10,9},{11,1... | collective-permute-start | bytes 786440 | tf_op jit(solution)/shard_map/ppermute | solution.py:594
  32.4 2.4 %collective-permute-start = (bf16[128,1024]{1,0:T(8,128)(2,1)S(1)}, bf16[128,1024]{1,0:T(8,128)(2,1)S(1)}, u32[]{:S(2)}, u32[]{:S(2)}) collective-permute-start(bf16[128,1024]{1,0:T(8,128)(2,1)S(1)} %get-tuple-element.36.g_hi.refs_2_), channel_id=1, source_target_pairs={{0,1},{1,2},{2,3},{3,4},{4,5},{5,6},{6,7},{7,8},{8,9},{9,10},{10,1... | collective-permute-start | bytes 786440 | tf_op jit(solution)/shard_map/ppermute | solution.py:594
  34.7 7.8 %mid.1 = (f32[864,1024]{1,0:T(8,128)S(1)}, f32[128,6144]{1,0:T(8,128)S(1)}, bf16[128,6144]{1,0:T(8,128)(2,1)S(1)}, f32[2,128,1024]{2,1,0:T(8,128)S(1)}, bf16[2,1...) custom-call(bf16[144,2048]{1,0:T(8,128)(2,1)S(1)} %get-tuple-element.37.incr, ...), custom_call_target="tpu_custom_call" | custom-call | tf_op jit(solution)/shard_map/mid/pallas_call | solution.py:416
  42.5 0.0 collective-permute-done.2.refs_8_
  42.5 0.0 collective-permute-done.3.refs_9_
  42.5 4.3 %collective-permute-done.1.refs_4_ = bf16[128,1024]{1,0:T(8,128)(2,1)S(1)} collective-permute-done((bf16[128,1024]{1,0:T(8,128)(2,1)S(1)}, bf16[128,1024]{1,0:T(8,128)(2,1)S(1)}, u32[]{:S(2)}, u32[]{:S(2)}) %collective-permute-start.1) | collective-permute-done | bytes 262176 | tf_op jit(solution)/shard_map/ppermute | solution.py:594
  46.9 0.0 collective-permute-done.refs_3_
  46.9 1.0 %edge.1 = (f32[2,128,1024]{2,1,0:T(8,128)S(1)}, bf16[128,1024]{1,0:T(8,128)(2,1)S(1)}, bf16[128,1024]{1,0:T(8,128)(2,1)S(1)}) custom-call(f32[2,128,1024]{2,1,0:T(8,128)S(1)} %get-tuple-element.34.hid_edge.refs_0_, bf16[128,1024]{1,0:T(8,128)(2,1)S(1)} %get-tuple-element.35.g_lo.refs_1_, bf16[128,1024]{1,0:T(8,128)(2,1)S(1)} %get-tuple-element.36.g_hi.refs_2_, ...), custom_call_target="tpu_custom_call" | custom-call | tf_op jit(solution)/shard_map/edge/pallas_call | solution.py:563
  47.9 4.5 %collective-permute-start.5 = (bf16[128,1024]{1,0:T(8,128)(2,1)S(1)}, bf16[128,1024]{1,0:T(8,128)(2,1)S(1)}, u32[]{:S(2)}, u32[]{:S(2)}) collective-permute-start(bf16[128,1024]{1,0:T(8,128)(2,1)S(1)} %get-tuple-element.46.g_lo.refs_1_), channel_id=1, source_target_pairs={{1,0},{2,1},{3,2},{4,3},{5,4},{6,5},{7,6},{8,7},{9,8},{10,9},{11,1... | collective-permute-start | bytes 786440 | tf_op jit(solution)/shard_map/ppermute | solution.py:594
  52.4 0.0 collective-permute-start.4
  52.4 7.8 %last.1 = (f32[137,64,128]{2,1,0:T(8,128)}, f32[2,128,1024]{2,1,0:T(8,128)S(1)}, bf16[2,128,512]{2,1,0:T(8,128)(2,1)S(1)}, bf16[2,128,1024]{2,1,0:T(8,128)(2,1)S(1)}) custom-call(f32[128,6144]{1,0:T(8,128)S(1)} %get-tuple-element.48.hid_in, bf16[128,6144]{1,0:T(8,128)(2,1)S(1)} %get-tuple-element.49.field_in, ...), custom_call_target="tpu_custom_call" | custom-call | tf_op jit(solution)/shard_map/last/pallas_call | solution.py:489
  60.2 0.0 collective-permute-done.5.refs_4_
  60.2 5.4 %collective-permute-done.4.refs_3_ = bf16[128,1024]{1,0:T(8,128)(2,1)S(1)} collective-permute-done((bf16[128,1024]{1,0:T(8,128)(2,1)S(1)}, bf16[128,1024]{1,0:T(8,128)(2,1)S(1)}, u32[]{:S(2)}, u32[]{:S(2)}) %collective-permute-start.4) | collective-permute-done | bytes 262176 | tf_op jit(solution)/shard_map/ppermute | solution.py:594
  65.7 2.1 %edge_last.1 = f32[137,64,128]{2,1,0:T(8,128)} custom-call(f32[2,128,1024]{2,1,0:T(8,128)S(1)} %get-tuple-element.45.hid_edge.refs_0_, bf16[128,1024]{1,0:T(8,128)(2,1)S(1)} %get-tuple-element.46.g_lo.refs_1_, bf16[128,1024]{1,0:T(8,128)(2,1)S(1)} %get-tuple-element.47.g_hi.refs_2_, ...), custom_call_target="tpu_custom_call", output_to_operand_aliasing={{}: (13, {})} | custom-call | tf_op jit(solution)/shard_map/edge_last/pallas_call | solution.py:575
Async XLA Ops:
  2.9 25.6 %all-to-all-start = ((bf16[128,9,2,128]{3,2,1,0:T(2,128)(2,1)}), bf16[128,9,2,128]{3,2,1,0:T(2,128)(2,1)S(1)}, u32[]{:S(2)}, u32[]{:S(2)}) async-start(bf16[128,9,2,128]{3,2,1,0:T(2,128)(2,1)} %pack.1), calls=%async_computation | async-start | bytes 1179648 | tf_op jit(solution)/shard_map/all_to_all | solution.py:600
  14.1 10.0 %copy-start = (bf16[4,3,128,128]{3,2,1,0:T(8,128)(2,1)S(1)}, bf16[4,3,128,128]{3,2,1,0:T(8,128)(2,1)}, u32[]{:S(2)}) copy-start(bf16[4,3,128,128]{3,2,1,0:T(8,128)(2,1)} %param.15) | copy-start | bytes 1179652
  14.1 10.0 %copy-start.1 = (bf16[128,8,137]{0,1,2:T(8,128)(2,1)S(1)}, bf16[128,8,137]{0,1,2:T(8,128)(2,1)}, u32[]{:S(2)}) copy-start(bf16[128,8,137]{0,1,2:T(8,128)(2,1)} %param.13) | copy-start | bytes 841732
  14.1 10.0 %copy-start.3 = (bf16[137,128]{1,0:T(8,128)(2,1)S(1)}, bf16[137,128]{1,0:T(8,128)(2,1)}, u32[]{:S(2)}) copy-start(bf16[137,128]{1,0:T(8,128)(2,1)} %dec.1) | copy-start | bytes 105220
  14.2 10.0 %copy-start.4 = (bf16[128,137]{0,1:T(8,128)(2,1)S(1)}, bf16[128,137]{0,1:T(8,128)(2,1)}, u32[]{:S(2)}) copy-start(bf16[128,137]{0,1:T(8,128)(2,1)} %param.17) | copy-start | bytes 105220
  16.3 26.2 %collective-permute-start.2 = (bf16[2,128,512]{2,1,0:T(8,128)(2,1)}, bf16[2,128,512]{2,1,0:T(8,128)(2,1)S(1)}, u32[]{:S(2)}, u32[]{:S(2)}) collective-permute-start(bf16[2,128,512]{2,1,0:T(8,128)(2,1)} %get-tuple-element.44), channel_id=1, source_target_pairs={{0,1},{1,2},{2,3},{3,4},{4,5},{5,6},{6,7},{7,8},{8,9},{9,10},{10,1... | collective-permute-start | bytes 786440 | tf_op jit(solution)/shard_map/ppermute | solution.py:594
  18.8 23.7 %collective-permute-start.3 = (bf16[2,128,512]{2,1,0:T(8,128)(2,1)}, bf16[2,128,512]{2,1,0:T(8,128)(2,1)S(1)}, u32[]{:S(2)}, u32[]{:S(2)}) collective-permute-start(bf16[2,128,512]{2,1,0:T(8,128)(2,1)} %get-tuple-element.31.after), channel_id=1, source_target_pairs={{1,0},{2,1},{3,2},{4,3},{5,4},{6,5},{7,6},{8,7},{9,8},{10,9},{11,1... | collective-permute-start | bytes 786440 | tf_op jit(solution)/shard_map/ppermute | solution.py:594
  24.1 1.0 %copy-start.2 = (bf16[2,128,512]{2,1,0:T(8,128)(2,1)S(1)}, bf16[2,128,512]{2,1,0:T(8,128)(2,1)}, u32[]{:S(2)}) copy-start(bf16[2,128,512]{2,1,0:T(8,128)(2,1)} %get-tuple-element.31.after) | copy-start | bytes 786436
  31.1 15.7 %collective-permute-start.1 = (bf16[128,1024]{1,0:T(8,128)(2,1)S(1)}, bf16[128,1024]{1,0:T(8,128)(2,1)S(1)}, u32[]{:S(2)}, u32[]{:S(2)}) collective-permute-start(bf16[128,1024]{1,0:T(8,128)(2,1)S(1)} %get-tuple-element.35.g_lo.refs_1_), channel_id=1, source_target_pairs={{1,0},{2,1},{3,2},{4,3},{5,4},{6,5},{7,6},{8,7},{9,8},{10,9},{11,1... | collective-permute-start | bytes 786440 | tf_op jit(solution)/shard_map/ppermute | solution.py:594
  32.4 14.5 %collective-permute-start = (bf16[128,1024]{1,0:T(8,128)(2,1)S(1)}, bf16[128,1024]{1,0:T(8,128)(2,1)S(1)}, u32[]{:S(2)}, u32[]{:S(2)}) collective-permute-start(bf16[128,1024]{1,0:T(8,128)(2,1)S(1)} %get-tuple-element.36.g_hi.refs_2_), channel_id=1, source_target_pairs={{0,1},{1,2},{2,3},{3,4},{4,5},{5,6},{6,7},{7,8},{8,9},{9,10},{10,1... | collective-permute-start | bytes 786440 | tf_op jit(solution)/shard_map/ppermute | solution.py:594
  47.9 12.3 %collective-permute-start.5 = (bf16[128,1024]{1,0:T(8,128)(2,1)S(1)}, bf16[128,1024]{1,0:T(8,128)(2,1)S(1)}, u32[]{:S(2)}, u32[]{:S(2)}) collective-permute-start(bf16[128,1024]{1,0:T(8,128)(2,1)S(1)} %get-tuple-element.46.g_lo.refs_1_), channel_id=1, source_target_pairs={{1,0},{2,1},{3,2},{4,3},{5,4},{6,5},{7,6},{8,7},{9,8},{10,9},{11,1... | collective-permute-start | bytes 786440 | tf_op jit(solution)/shard_map/ppermute | solution.py:594
  52.4 13.3 %collective-permute-start.4 = (bf16[128,1024]{1,0:T(8,128)(2,1)S(1)}, bf16[128,1024]{1,0:T(8,128)(2,1)S(1)}, u32[]{:S(2)}, u32[]{:S(2)}) collective-permute-start(bf16[128,1024]{1,0:T(8,128)(2,1)S(1)} %get-tuple-element.47.g_hi.refs_2_), channel_id=1, source_target_pairs={{0,1},{1,2},{2,3},{3,4},{4,5},{5,6},{6,7},{7,8},{8,9},{9,10},{10,1... | collective-permute-start | bytes 786440 | tf_op jit(solution)/shard_map/ppermute | solution.py:594

commit v5 on v4

--- a/solution.py
+++ b/solution.py
@@ -6,6 +6,7 @@
 from jax.experimental import pallas as pl
 from jax.experimental.pallas import tpu as pltpu
 from jax.sharding import PartitionSpec as P
+
 
 F32 = jnp.float32
 BF16 = jnp.bfloat16
@@ -90,6 +91,16 @@
 HBM = pl.BlockSpec(memory_space=pltpu.HBM)
 VMEM = pl.BlockSpec(memory_space=pltpu.VMEM)
 ANY = pl.BlockSpec(memory_space=pl.ANY)
+SMEM = pl.BlockSpec(memory_space=pltpu.SMEM)
+
+
+def by_side(odd, far_side, body):
+    for parity in range(2):
+        side = parity if far_side else 1 - parity
+
+        @pl.when(odd[0] == parity)
+        def _(side=side):
+            body(side)
 
 
 def pack(resid, index, count, weight, dests):
@@ -164,7 +175,7 @@
     )(jacobian.transpose(2, 1, 0), decoder, encoder.T, conv_w, after)
 
 
-def gate_edges_kernel(src, lo, hi, buf, wide, sems):
+def gate_edges_kernel(odd, src, far, close, both, buf, wide, sems):
     channels, lons, lats = src.shape[1:]
     copies = []
     for k in range(2):
@@ -174,34 +185,44 @@
             copies.append(pltpu.make_async_copy(part, buf.at[k, side], sems.at[k, side]))
             copies[-1].start()
     for k in range(2):
-        for side, out in enumerate((lo, hi)):
+        for side in range(2):
             copies[2 * k + side].wait()
             wide[k, side] = buf[k, side].astype(F32).reshape(channels * CHUNK, lats)
             for r in range(DIL):
                 for c in range(0, channels, 16):
                     value = by_channel(wide.at[k, side], side * DIL + r, CHUNK, c)
-                    out[k, c : c + 16, r * lats : (r + 1) * lats] = value
-
-
-def gate_edges(gates):
-    layers, channels, lons, lats = gates.shape
+                    both[side, k, c : c + 16, r * lats : (r + 1) * lats] = value
+
+    def split(side):
+        far[...] = both[side]
+        close[...] = both[1 - side]
+
+    by_side(odd, True, split)
+
+
+def gate_edges(odd, gates):
+    _, channels, _, lats = gates.shape
     send = jax.ShapeDtypeStruct((2, channels, DIL * lats), BF16)
     return pl.pallas_call(
         gate_edges_kernel,
-        in_specs=[HBM],
+        in_specs=[SMEM, HBM],
         out_specs=(VMEM,) * 2,
         out_shape=(send,) * 2,
         scratch_shapes=[
+            pltpu.VMEM((2, 2, channels, DIL * lats), BF16),
             pltpu.VMEM((2, 2, channels, CHUNK, lats), BF16),
             pltpu.VMEM((2, 2, channels * CHUNK, lats), F32),
             pltpu.SemaphoreType.DMA((2, 2)),
         ],
         compiler_params=params(58),
         name="gate_edges",
-    )(gates)
-
-
-def front_kernel(packed, jac, dec, incr_out, key_out, group_out, grad_out, hid_out, lo_out, hi_out):
+    )(odd, gates)
+
+
+def front_kernel(
+    odd, packed, jac, dec,
+    incr_out, key_out, group_out, grad_out, hid_out, lo_out, hi_out, far_out, close_out,
+):
     senders, pairs = packed.shape[0], packed.shape[1] - 1
     part = 2 * senders
     slots = pairs * part
@@ -245,6 +266,12 @@
         hid_out[side] = hidden
         (lo_out, hi_out)[side][...] = hidden.astype(BF16)
 
+    def split(side):
+        far_out[...] = (lo_out, hi_out)[side][...]
+        close_out[...] = (hi_out, lo_out)[side][...]
+
+    by_side(odd, True, split)
+
 
 def hot(key):
     return jnp.concatenate(
@@ -252,15 +279,15 @@
     )
 
 
-def front(packed, jac, dec):
+def front(odd, packed, jac, dec):
     slots = packed.shape[0] * (packed.shape[1] - 1) * 2
     levels = jac.shape[0]
     cols = CHUNK * LANES
     sd = jax.ShapeDtypeStruct
     return pl.pallas_call(
         front_kernel,
-        in_specs=[VMEM] * 3,
-        out_specs=(VMEM,) * 7,
+        in_specs=[SMEM] + [VMEM] * 3,
+        out_specs=(VMEM,) * 9,
         out_shape=(
             sd((levels, slots), BF16),
             sd((slots, LANES), F32),
@@ -269,10 +296,12 @@
             sd((2, LANES, cols), F32),
             sd((LANES, cols), BF16),
             sd((LANES, cols), BF16),
+            sd((LANES, cols), BF16),
+            sd((LANES, cols), BF16),
         ),
         compiler_params=params(28),
         name="front",
-    )(packed, jac, dec)
+    )(odd, packed, jac, dec)
 
 
 def conv(weight, taps):
@@ -357,7 +386,6 @@
 ):
     load = load_gates(gates, 3, bufs, sems)
     cols = CHUNK * LANES
-    step = DIL * LANES
     levels = incr.shape[0]
     channels, total = hid.shape
     inner = total // cols - 2
@@ -453,7 +481,6 @@
     out, near_out, ends_a, ends_b, hid, gb, tiles, sems, bufs, wide, gate_sems,
 ):
     load = load_gates(gates, 1, bufs, gate_sems)
-    cols = CHUNK * LANES
     channels, total = hid.shape
     levels = enc.shape[0]
     copies = []
@@ -508,121 +535,160 @@
     )(hid_in, field_in, hid_edge, g_lo, g_hi, grad, enc, gates, w)
 
 
-def edge_values(which, hid, g_lo, g_hi, halo_lo, halo_hi, near, gate_a, gate_b, ah_lo, ah_hi, w):
+def edge_value(which, side, hid, g_lo, g_hi, halo, near, gate_a, gate_b, gate_halo, w):
     cols = CHUNK * LANES
     step = DIL * LANES
     wa, wb = w.at[2 * which + 1], w.at[2 * which]
-    result = []
-    for side in range(2):
-        if side == 0:
-            field = jnp.concatenate([halo_lo[...], g_lo[...]], axis=1)
-            old = jnp.concatenate([halo_lo[:, step:].astype(F32), hid[0, :, :step]], axis=1)
-            gate = jnp.concatenate([ah_lo[which], gate_a[0]], axis=1)
-        else:
-            field = jnp.concatenate([g_hi[...], halo_hi[...]], axis=1)
-            old = jnp.concatenate([hid[1, :, step:], halo_hi[:, :step].astype(F32)], axis=1)
-            gate = jnp.concatenate([gate_a[1], ah_hi[which]], axis=1)
-        back = conv(wa, [field[:, d : d + cols] for d in (2 * step, step, 0)])
-        new = old + gate.astype(F32) * back
-        pieces = (new, near[0]) if side == 0 else (near[1], new)
-        joined = jnp.concatenate(pieces, axis=1)
-        field = joined.astype(BF16)
-        back = conv(wb, [field[:, d : d + cols] for d in (2 * step, step, 0)])
-        result.append(joined[:, step : step + cols] + gate_b[side].astype(F32) * back)
-    return result
-
-
-def edge_kernel(which, *refs):
-    ins, (hid_out, lo_out, hi_out) = refs[:11], refs[11:]
-    lo, hi = edge_values(which, *ins)
-    hid_out[0] = lo
-    hid_out[1] = hi
-    lo_out[...] = lo.astype(BF16)
-    hi_out[...] = hi.astype(BF16)
-
-
-def edge_last_kernel(which, *refs):
-    ins, (grad, enc, _), (out, tiles, sems) = refs[:11], refs[11:14], refs[14:]
+    if side == 0:
+        field = jnp.concatenate([halo[...], g_lo[...]], axis=1)
+        old = jnp.concatenate([halo[:, step:].astype(F32), hid[0, :, :step]], axis=1)
+        gate = jnp.concatenate([gate_halo[which], gate_a[0]], axis=1)
+    else:
+        field = jnp.concatenate([g_hi[...], halo[...]], axis=1)
+        old = jnp.concatenate([hid[1, :, step:], halo[:, :step].astype(F32)], axis=1)
+        gate = jnp.concatenate([gate_a[1], gate_halo[which]], axis=1)
+    back = conv(wa, [field[:, d : d + cols] for d in (2 * step, step, 0)])
+    new = old + gate.astype(F32) * back
+    joined = jnp.concatenate((new, near[0]) if side == 0 else (near[1], new), axis=1)
+    field = joined.astype(BF16)
+    back = conv(wb, [field[:, d : d + cols] for d in (2 * step, step, 0)])
+    return joined[:, step : step + cols] + gate_b[side].astype(F32) * back
+
+
+def edge_far_kernel(which, odd, *refs):
+    ins, (hid_out, send) = refs[:9], refs[9:]
+
+    def body(side):
+        value = edge_value(which, side, *ins)
+        hid_out[...] = value
+        send[...] = value.astype(BF16)
+
+    by_side(odd, True, body)
+
+
+def edge_close_kernel(which, odd, *refs):
+    ins, (far_hid, far_g), (hid_out, lo_out, hi_out, send) = refs[:9], refs[9:11], refs[11:]
+
+    def body(side):
+        value = edge_value(which, side, *ins)
+        hid_out[side] = value
+        send[...] = value.astype(BF16)
+        (lo_out, hi_out)[side][...] = value.astype(BF16)
+        hid_out[1 - side] = far_hid[...]
+        (hi_out, lo_out)[side][...] = far_g[...]
+
+    by_side(odd, False, body)
+
+
+def edge_last_kernel(which, far_side, odd, *refs):
+    ins, (grad, enc, _), (out, tile, sem) = refs[:9], refs[9:12], refs[12:]
     levels = enc.shape[0]
-    values = edge_values(which, *ins)
     chunks = out.shape[1] // CHUNK
-    copies = []
-    for side in range(2):
-        part = grad[side * levels : (side + 1) * levels, :]
-        emit(enc[...], part, values[side], tiles.at[side])
-        copy = send_tile(tiles.at[side], out, side * (chunks - 1), sems.at[side])
+
+    def body(side):
+        value = edge_value(which, side, *ins)
+        emit(enc[...], grad[side * levels : (side + 1) * levels, :], value, tile)
+        copy = send_tile(tile, out, side * (chunks - 1), sem)
         copy.start()
-        copies.append(copy)
-    for copy in copies:
         copy.wait()
 
-
-def edge(which, *args):
+    by_side(odd, far_side, body)
+
+
+def edge_far(which, *args):
     sd = jax.ShapeDtypeStruct
-    hid, g_lo = args[:2]
-    return pl.pallas_call(
-        functools.partial(edge_kernel, which),
-        in_specs=[VMEM] * 11,
-        out_specs=(VMEM,) * 3,
-        out_shape=(sd(hid.shape, F32), sd(g_lo.shape, BF16), sd(g_lo.shape, BF16)),
+    g_lo = args[2]
+    return pl.pallas_call(
+        functools.partial(edge_far_kernel, which),
+        in_specs=[SMEM] + [VMEM] * 9,
+        out_specs=(VMEM,) * 2,
+        out_shape=(sd(g_lo.shape, F32), sd(g_lo.shape, BF16)),
         compiler_params=params(18),
-        name="edge",
+        name="edge_far",
     )(*args)
 
 
-def edge_last(which, *args):
-    enc, state = args[12:]
-    return pl.pallas_call(
-        functools.partial(edge_last_kernel, which),
-        in_specs=[VMEM] * 13 + [HBM],
+def edge_close(which, *args):
+    sd = jax.ShapeDtypeStruct
+    hid, g_lo = args[1:3]
+    return pl.pallas_call(
+        functools.partial(edge_close_kernel, which),
+        in_specs=[SMEM] + [VMEM] * 11,
+        out_specs=(VMEM,) * 4,
+        out_shape=(sd(hid.shape, F32),) + (sd(g_lo.shape, BF16),) * 3,
+        compiler_params=params(18),
+        name="edge_close",
+    )(*args)
+
+
+def edge_last(which, far_side, *args):
+    enc, state = args[-2:]
+    return pl.pallas_call(
+        functools.partial(edge_last_kernel, which, far_side),
+        in_specs=[SMEM] + [VMEM] * 11 + [HBM],
         out_specs=HBM,
         out_shape=jax.ShapeDtypeStruct(state.shape, F32),
         scratch_shapes=[
-            pltpu.VMEM((2, enc.shape[0] * CHUNK, LANES), F32),
-            pltpu.SemaphoreType.DMA((2,)),
+            pltpu.VMEM((enc.shape[0] * CHUNK, LANES), F32),
+            pltpu.SemaphoreType.DMA,
         ],
-        input_output_aliases={13: 0},
+        input_output_aliases={12: 0},
         compiler_params=params(18),
         name="edge_last",
     )(*args)
 
 
-def halos(lo, hi):
+def swap(value, first):
     count = lax.axis_size("lon")
-    up = [(i, (i + 1) % count) for i in range(count)]
-    down = [(b, a) for a, b in up]
-    return lax.ppermute(hi, "lon", up), lax.ppermute(lo, "lon", down)
-
-
-def per_device(resid, index, count, weight, jacobian, decoder, conv_weight, gates, encoder):
+    pairs = []
+    for i in range(first, first + count, 2):
+        low, high = i % count, (i + 1) % count
+        pairs += [(low, high), (high, low)]
+    return lax.ppermute(value, "lon", pairs)
+
+
+def program(resid, index, count, weight, jacobian, decoder, conv_weight, gates, encoder):
     dests = lax.axis_size("lat") * lax.axis_size("lon")
+    odd = (lax.axis_index("lon") % 2).astype(jnp.int32).reshape(1)
     packed = pack(resid, index, count, weight.reshape(1, -1), dests)
     packed = lax.all_to_all(packed, ("lat", "lon"), split_axis=0, concat_axis=0, tiled=True)
-    gate_lo, gate_hi = gate_edges(gates)
-    gh_lo, gh_hi = halos(gate_lo, gate_hi)
-    jac, dec, enc, w = prepare(jacobian, decoder, encoder, conv_weight, gate_lo)
-    incr, key, group, grad_e, hid_e, g_lo, g_hi = front(packed, jac, dec)
-    halo_lo, halo_hi = halos(g_lo, g_hi)
+    gate_far, gate_close = gate_edges(odd, gates)
+    gate_far_halo = swap(gate_far, 1)
+    gate_close_halo = swap(gate_close, 0)
+    jac, dec, enc, w = prepare(jacobian, decoder, encoder, conv_weight, gate_far)
+    incr, key, group, grad_e, hid_e, g_lo, g_hi, far, close = front(odd, packed, jac, dec)
+    far = swap(far, 1)
+    close = swap(close, 0)
     grad_i, hid_i, field_i, near, end_a, end_b = mid(
         incr, key, group, hid_e, g_lo, g_hi, dec, gates, w
     )
-    hid_e, g_lo, g_hi = edge(
-        1, hid_e, g_lo, g_hi, halo_lo, halo_hi, near, end_a, end_b, gh_lo, gh_hi, w
-    )
-    halo_lo, halo_hi = halos(g_lo, g_hi)
+    far_hid, far_g = edge_far(1, odd, hid_e, g_lo, g_hi, far, near, end_a, end_b, gate_far_halo, w)
+    far = swap(far_g, 1)
+    hid_e, g_lo, g_hi, close = edge_close(
+        1, odd, hid_e, g_lo, g_hi, close, near, end_a, end_b, gate_close_halo, w, far_hid, far_g
+    )
+    close = swap(close, 0)
     out_shape = (jacobian.shape[2],) + gates.shape[2:]
     state, near, end_a, end_b = last(
         hid_i, field_i, hid_e, g_lo, g_hi, grad_i, enc, gates, w, out_shape
     )
-    return edge_last(
-        0, hid_e, g_lo, g_hi, halo_lo, halo_hi, near, end_a, end_b, gh_lo, gh_hi, w,
-        grad_e, enc, state,
-    )
+    halves = ((FAR_FIRST, far, gate_far_halo), (not FAR_FIRST, close, gate_close_halo))
+    if not FAR_FIRST:
+        halves = ((False, close, gate_close_halo), (True, far, gate_far_halo))
+    for far_side, halo, gate_halo in halves:
+        state = edge_last(
+            0, far_side, odd, hid_e, g_lo, g_hi, halo, near, end_a, end_b, gate_halo, w,
+            grad_e, enc, state,
+        )
+    return state
+
+
+FAR_FIRST = True
 
 
 def solution(mesh):
     return jax.shard_map(
-        per_device,
+        program,
         mesh=mesh,
         in_specs=(
             P(None, ("lat", "lon")),

time: 68.2 us -> 72.6 us (1.065)
  starting transfers between devices: 27.1 us -> 30.2 us
  Pallas kernels: 26.6 us -> 27.9 us
    ppermute x6, starting transfers between devices: 15.9 us -> 19.1 us  [swap(): return lax.ppermute(value, 'lon', pairs)]
    pallas_call x4 -> x6, Pallas kernels: 7.84 us -> 9.17 us  [the longest x2 3.15 us: edge_last(): pl.pallas_call(functools.partial(edge_last_kernel, which, far_side), in_s...]
  transfers between devices with their start and end apart: 7 -> 7, of which waited for: 3 -> 3; matrix products, arithmetic and copies ran while one was open for 0% -> 0% of each run, Pallas kernels for 30% -> 33%
where the time goes in v5:
time: 72.6 us; the launch traced here: 71.8 us
  starting transfers between devices  30.2 us (42%)
  Pallas kernels  27.9 us (38%)
  waiting for transfers between devices  12.3 us (17%)
  local copies, waits for them, and re-layouts  0.99 us (1%)
    ppermute x6, starting transfers between devices, swap(): return lax.ppermute(value, 'lon', pairs)  19.1 us
    all_to_all x1, starting transfers between devices, program(): lax.all_to_all(packed, ('lat', 'lon'), split_axis=0, concat_axis=0, tiled...  11.2 us
    ppermute x6, waiting for transfers between devices, swap(): return lax.ppermute(value, 'lon', pairs)  9.13 us
    pallas_call x1, Pallas kernels, mid(): pl.pallas_call(mid_kernel, in_specs=[VMEM] * 7 + [HBM, VMEM], out_specs=(...  7.79 us
    pallas_call x1, Pallas kernels, last(): pl.pallas_call(last_kernel, in_specs=[VMEM] * 7 + [HBM, VMEM], out_specs=...  7.71 us
    all_to_all x1, waiting for transfers between devices, program(): lax.all_to_all(packed, ('lat', 'lon'), split_axis=0, concat_axis=0, tiled...  3.19 us
    pallas_call x2, Pallas kernels, edge_last(): pl.pallas_call(functools.partial(edge_last_kernel, which, far_side), in_s...  3.15 us
    pallas_call x1, Pallas kernels, pack(): pl.pallas_call(pack_kernel, in_specs=[HBM] * 4, out_specs=HBM, out_shape=...  2.92 us
  transfers between devices with their start and end apart: 7, of which 3 were waited for; matrix products, arithmetic and copies ran while one was open for 0% of the time, Pallas kernels for 33%

profile of v5, /device:TPU:0, one launch (start us, length us, event | category | flops | bytes accessed | tf_op | source)
XLA Modules:
  0.0 71.8 jit_solution(402318033694810418)
XLA Ops:
  0.0 2.9 %pack.1 = bf16[128,9,2,128]{3,2,1,0:T(2,128)(2,1)} custom-call(bf16[128,2048]{1,0:T(8,128)(2,1)} %resid_hbm.1, s32[2,2048]{1,0:T(2,128)} %index_hbm.1, s32[1,128]{1,0:T(1,128)} %count_hbm.1, f32[1,128]{1,0:T(1,128)} %bitcast.8), custom_call_target="tpu_custom_call" | custom-call | tf_op jit(solution)/shard_map/pack/pallas_call | solution.py:110
  2.9 11.2 %all-to-all-start = ((bf16[128,9,2,128]{3,2,1,0:T(2,128)(2,1)}), bf16[128,9,2,128]{3,2,1,0:T(2,128)(2,1)S(1)}, u32[]{:S(2)}, u32[]{:S(2)}) async-start(bf16[128,9,2,128]{3,2,1,0:T(2,128)(2,1)} %pack.1), calls=%async_computation | async-start | bytes 1179648 | tf_op jit(solution)/shard_map/all_to_all | solution.py:654
  14.1 0.0 copy-start
  14.1 0.0 copy-start.1
  14.1 0.0 copy-start.3
  14.2 0.0 copy-start.4
  14.2 2.2 %gate_edges.1 = (bf16[2,128,512]{2,1,0:T(8,128)(2,1)}, bf16[2,128,512]{2,1,0:T(8,128)(2,1)}) custom-call(s32[1]{0:T(128)} %bitcast.odd, bf16[4,128,64,128]{3,2,1,0:T(8,128)(2,1)} %gates.3), custom_call_target="tpu_custom_call" | custom-call | tf_op jit(solution)/shard_map/gate_edges/pallas_call | solution.py:206
  16.4 7.6 %collective-permute-start.3 = (bf16[2,128,512]{2,1,0:T(8,128)(2,1)}, bf16[2,128,512]{2,1,0:T(8,128)(2,1)S(1)}, u32[]{:S(2)}, u32[]{:S(2)}) collective-permute-start(bf16[2,128,512]{2,1,0:T(8,128)(2,1)} %get-tuple-element.36.after), channel_id=1, source_target_pairs={{1,2},{2,1},{3,4},{4,3},{5,6},{6,5},{7,8},{8,7},{9,10},{10,9},{11,... | collective-permute-start | bytes 786440 | tf_op jit(solution)/shard_map/ppermute | solution.py:647
  24.0 0.0 copy-done
  24.0 0.0 copy-done.1
  24.0 0.0 copy-done.3
  24.0 0.0 copy-done.4
  24.0 0.0 copy-start.2
  24.0 1.0 %copy-done.2 = bf16[2,128,512]{2,1,0:T(8,128)(2,1)S(1)} copy-done((bf16[2,128,512]{2,1,0:T(8,128)(2,1)S(1)}, bf16[2,128,512]{2,1,0:T(8,128)(2,1)}, u32[]{:S(2)}) %copy-start.2) | copy-done | bytes 262168
  25.0 0.3 prepare.1
  25.3 3.2 %all-to-all-done.packed = bf16[128,9,2,128]{3,2,1,0:T(2,128)(2,1)S(1)} async-done(((bf16[128,9,2,128]{3,2,1,0:T(2,128)(2,1)}), bf16[128,9,2,128]{3,2,1,0:T(2,128)(2,1)S(1)}, u32[]{:S(2)}, u32[]{:S(2)}) %all-to-all-start) | async-done | bytes 589856 | tf_op jit(solution)/shard_map/all_to_all | solution.py:654
  28.5 2.6 %front.1 = (bf16[144,2048]{1,0:T(8,128)(2,1)S(1)}, f32[2048,128]{1,0:T(8,128)S(1)}, f32[8,2048]{1,0:T(8,128)S(1)}, f32[288,1024]{1,0:T(8,128)S(1)}, f32[2,128,10...) custom-call(s32[1]{0:T(128)} %bitcast.odd, ...), custom_call_target="tpu_custom_call" | custom-call | tf_op jit(solution)/shard_map/front/pallas_call | solution.py:287
  31.1 1.3 %collective-permute-start.2 = (bf16[128,1024]{1,0:T(8,128)(2,1)S(1)}, bf16[128,1024]{1,0:T(8,128)(2,1)S(1)}, u32[]{:S(2)}, u32[]{:S(2)}) collective-permute-start(bf16[128,1024]{1,0:T(8,128)(2,1)S(1)} %get-tuple-element.51), channel_id=1, source_target_pairs={{1,2},{2,1},{3,4},{4,3},{5,6},{6,5},{7,8},{8,7},{9,10},{10,9},{11,... | collective-permute-start | bytes 786440 | tf_op jit(solution)/shard_map/ppermute | solution.py:647
  32.4 1.7 %collective-permute-start.1 = (bf16[2,128,512]{2,1,0:T(8,128)(2,1)}, bf16[2,128,512]{2,1,0:T(8,128)(2,1)S(1)}, u32[]{:S(2)}, u32[]{:S(2)}) collective-permute-start(bf16[2,128,512]{2,1,0:T(8,128)(2,1)} %get-tuple-element.50), channel_id=1, source_target_pairs={{0,1},{1,0},{2,3},{3,2},{4,5},{5,4},{6,7},{7,6},{8,9},{9,8},{10,11... | collective-permute-start | bytes 786440 | tf_op jit(solution)/shard_map/ppermute | solution.py:647
  34.1 1.8 %collective-permute-start = (bf16[128,1024]{1,0:T(8,128)(2,1)S(1)}, bf16[128,1024]{1,0:T(8,128)(2,1)S(1)}, u32[]{:S(2)}, u32[]{:S(2)}) collective-permute-start(bf16[128,1024]{1,0:T(8,128)(2,1)S(1)} %get-tuple-element.42), channel_id=1, source_target_pairs={{0,1},{1,0},{2,3},{3,2},{4,5},{5,4},{6,7},{7,6},{8,9},{9,8},{10,11... | collective-permute-start | bytes 786440 | tf_op jit(solution)/shard_map/ppermute | solution.py:647
  36.0 7.8 %mid.1 = (f32[864,1024]{1,0:T(8,128)S(1)}, f32[128,6144]{1,0:T(8,128)S(1)}, bf16[128,6144]{1,0:T(8,128)(2,1)S(1)}, f32[2,128,1024]{2,1,0:T(8,128)S(1)}, bf16[2,1...) custom-call(bf16[144,2048]{1,0:T(8,128)(2,1)S(1)} %get-tuple-element.43.incr, ...), custom_call_target="tpu_custom_call" | custom-call | tf_op jit(solution)/shard_map/mid/pallas_call | solution.py:444
  43.8 0.0 collective-permute-done.3.refs_7_
  43.8 1.8 %collective-permute-done.2.refs_3_ = bf16[128,1024]{1,0:T(8,128)(2,1)S(1)} collective-permute-done((bf16[128,1024]{1,0:T(8,128)(2,1)S(1)}, bf16[128,1024]{1,0:T(8,128)(2,1)S(1)}, u32[]{:S(2)}, u32[]{:S(2)}) %collective-permute-start.2) | collective-permute-done | bytes 262176 | tf_op jit(solution)/shard_map/ppermute | solution.py:647
  45.6 0.6 edge_far.1
  46.2 4.9 %collective-permute-start.5 = (bf16[128,1024]{1,0:T(8,128)(2,1)S(1)}, bf16[128,1024]{1,0:T(8,128)(2,1)S(1)}, u32[]{:S(2)}, u32[]{:S(2)}) collective-permute-start(bf16[128,1024]{1,0:T(8,128)(2,1)S(1)} %get-tuple-element.53.refs_10_), channel_id=1, source_target_pairs={{1,2},{2,1},{3,4},{4,3},{5,6},{6,5},{7,8},{8,7},{9,10},{10,9},{11,... | collective-permute-start | bytes 786440 | tf_op jit(solution)/shard_map/ppermute | solution.py:647
  51.1 0.0 collective-permute-done.1.refs_7_
  51.1 7.3 %collective-permute-done.refs_3_ = bf16[128,1024]{1,0:T(8,128)(2,1)S(1)} collective-permute-done((bf16[128,1024]{1,0:T(8,128)(2,1)S(1)}, bf16[128,1024]{1,0:T(8,128)(2,1)S(1)}, u32[]{:S(2)}, u32[]{:S(2)}) %collective-permute-start) | collective-permute-done | bytes 262176 | tf_op jit(solution)/shard_map/ppermute | solution.py:647
  58.4 0.6 edge_close.1
  59.0 1.7 %collective-permute-start.4 = (bf16[128,1024]{1,0:T(8,128)(2,1)S(1)}, bf16[128,1024]{1,0:T(8,128)(2,1)S(1)}, u32[]{:S(2)}, u32[]{:S(2)}) collective-permute-start(bf16[128,1024]{1,0:T(8,128)(2,1)S(1)} %get-tuple-element.57), channel_id=1, source_target_pairs={{0,1},{1,0},{2,3},{3,2},{4,5},{5,4},{6,7},{7,6},{8,9},{9,8},{10,11... | collective-permute-start | bytes 786440 | tf_op jit(solution)/shard_map/ppermute | solution.py:647
  60.7 7.7 %last.1 = (f32[137,64,128]{2,1,0:T(8,128)}, f32[2,128,1024]{2,1,0:T(8,128)S(1)}, bf16[2,128,512]{2,1,0:T(8,128)(2,1)S(1)}, bf16[2,128,1024]{2,1,0:T(8,128)(2,1)S(1)}) custom-call(f32[128,6144]{1,0:T(8,128)S(1)} %get-tuple-element.58.hid_in, bf16[128,6144]{1,0:T(8,128)(2,1)S(1)} %get-tuple-element.59.field_in, ...), custom_call_target="tpu_custom_call" | custom-call | tf_op jit(solution)/shard_map/last/pallas_call | solution.py:516
  68.4 0.0 collective-permute-done.5.refs_3_
  68.4 1.6 %edge_last.2.refs_11_ = f32[137,64,128]{2,1,0:T(8,128)} custom-call(s32[1]{0:T(128)} %bitcast.odd, f32[2,128,1024]{2,1,0:T(8,128)S(1)} %get-tuple-element.54.hid_edge.refs_0_, bf16[128,1024]{1,0:T(8,128)(2,1)S(1)} %get-tuple-element.55.g_lo.refs_1_, bf16[128,1024]{1,0:T(8,128)(2,1)S(1)} %get-tuple-element.56.g_hi.refs_2_, ...), custom_call_target="tpu_custom_call", output_to_operand_aliasing={{}: (12, {})} | custom-call | tf_op jit(solution)/shard_map/edge_last/pallas_call | solution.py:626
  70.0 0.0 collective-permute-done.4.refs_3_
  70.0 1.6 %edge_last.3 = f32[137,64,128]{2,1,0:T(8,128)} custom-call(s32[1]{0:T(128)} %bitcast.odd, f32[2,128,1024]{2,1,0:T(8,128)S(1)} %get-tuple-element.54.hid_edge.refs_0_, bf16[128,1024]{1,0:T(8,128)(2,1)S(1)} %get-tuple-element.55.g_lo.refs_1_, bf16[128,1024]{1,0:T(8,128)(2,1)S(1)} %get-tuple-element.56.g_hi.refs_2_, ...), custom_call_target="tpu_custom_call", output_to_operand_aliasing={{}: (12, {})} | custom-call | tf_op jit(solution)/shard_map/edge_last/pallas_call | solution.py:626
Async XLA Ops:
  2.9 25.5 %all-to-all-start = ((bf16[128,9,2,128]{3,2,1,0:T(2,128)(2,1)}), bf16[128,9,2,128]{3,2,1,0:T(2,128)(2,1)S(1)}, u32[]{:S(2)}, u32[]{:S(2)}) async-start(bf16[128,9,2,128]{3,2,1,0:T(2,128)(2,1)} %pack.1), calls=%async_computation | async-start | bytes 1179648 | tf_op jit(solution)/shard_map/all_to_all | solution.py:654
  14.1 9.9 %copy-start = (bf16[4,3,128,128]{3,2,1,0:T(8,128)(2,1)S(1)}, bf16[4,3,128,128]{3,2,1,0:T(8,128)(2,1)}, u32[]{:S(2)}) copy-start(bf16[4,3,128,128]{3,2,1,0:T(8,128)(2,1)} %param.15) | copy-start | bytes 1179652
  14.1 9.9 %copy-start.1 = (bf16[128,8,137]{0,1,2:T(8,128)(2,1)S(1)}, bf16[128,8,137]{0,1,2:T(8,128)(2,1)}, u32[]{:S(2)}) copy-start(bf16[128,8,137]{0,1,2:T(8,128)(2,1)} %param.13) | copy-start | bytes 841732
  14.1 9.9 %copy-start.3 = (bf16[137,128]{1,0:T(8,128)(2,1)S(1)}, bf16[137,128]{1,0:T(8,128)(2,1)}, u32[]{:S(2)}) copy-start(bf16[137,128]{1,0:T(8,128)(2,1)} %dec.1) | copy-start | bytes 105220
  14.2 9.9 %copy-start.4 = (bf16[128,137]{0,1:T(8,128)(2,1)S(1)}, bf16[128,137]{0,1:T(8,128)(2,1)}, u32[]{:S(2)}) copy-start(bf16[128,137]{0,1:T(8,128)(2,1)} %param.17) | copy-start | bytes 105220
  16.4 27.3 %collective-permute-start.3 = (bf16[2,128,512]{2,1,0:T(8,128)(2,1)}, bf16[2,128,512]{2,1,0:T(8,128)(2,1)S(1)}, u32[]{:S(2)}, u32[]{:S(2)}) collective-permute-start(bf16[2,128,512]{2,1,0:T(8,128)(2,1)} %get-tuple-element.36.after), channel_id=1, source_target_pairs={{1,2},{2,1},{3,4},{4,3},{5,6},{6,5},{7,8},{8,7},{9,10},{10,9},{11,... | collective-permute-start | bytes 786440 | tf_op jit(solution)/shard_map/ppermute | solution.py:647
  24.0 1.0 %copy-start.2 = (bf16[2,128,512]{2,1,0:T(8,128)(2,1)S(1)}, bf16[2,128,512]{2,1,0:T(8,128)(2,1)}, u32[]{:S(2)}) copy-start(bf16[2,128,512]{2,1,0:T(8,128)(2,1)} %get-tuple-element.36.after) | copy-start | bytes 786436
  31.1 14.5 %collective-permute-start.2 = (bf16[128,1024]{1,0:T(8,128)(2,1)S(1)}, bf16[128,1024]{1,0:T(8,128)(2,1)S(1)}, u32[]{:S(2)}, u32[]{:S(2)}) collective-permute-start(bf16[128,1024]{1,0:T(8,128)(2,1)S(1)} %get-tuple-element.51), channel_id=1, source_target_pairs={{1,2},{2,1},{3,4},{4,3},{5,6},{6,5},{7,8},{8,7},{9,10},{10,9},{11,... | collective-permute-start | bytes 786440 | tf_op jit(solution)/shard_map/ppermute | solution.py:647
  32.4 18.6 %collective-permute-start.1 = (bf16[2,128,512]{2,1,0:T(8,128)(2,1)}, bf16[2,128,512]{2,1,0:T(8,128)(2,1)S(1)}, u32[]{:S(2)}, u32[]{:S(2)}) collective-permute-start(bf16[2,128,512]{2,1,0:T(8,128)(2,1)} %get-tuple-element.50), channel_id=1, source_target_pairs={{0,1},{1,0},{2,3},{3,2},{4,5},{5,4},{6,7},{7,6},{8,9},{9,8},{10,11... | collective-permute-start | bytes 786440 | tf_op jit(solution)/shard_map/ppermute | solution.py:647
  34.1 24.2 %collective-permute-start = (bf16[128,1024]{1,0:T(8,128)(2,1)S(1)}, bf16[128,1024]{1,0:T(8,128)(2,1)S(1)}, u32[]{:S(2)}, u32[]{:S(2)}) collective-permute-start(bf16[128,1024]{1,0:T(8,128)(2,1)S(1)} %get-tuple-element.42), channel_id=1, source_target_pairs={{0,1},{1,0},{2,3},{3,2},{4,5},{5,4},{6,7},{7,6},{8,9},{9,8},{10,11... | collective-permute-start | bytes 786440 | tf_op jit(solution)/shard_map/ppermute | solution.py:647
  46.2 22.2 %collective-permute-start.5 = (bf16[128,1024]{1,0:T(8,128)(2,1)S(1)}, bf16[128,1024]{1,0:T(8,128)(2,1)S(1)}, u32[]{:S(2)}, u32[]{:S(2)}) collective-permute-start(bf16[128,1024]{1,0:T(8,128)(2,1)S(1)} %get-tuple-element.53.refs_10_), channel_id=1, source_target_pairs={{1,2},{2,1},{3,4},{4,3},{5,6},{6,5},{7,8},{8,7},{9,10},{10,9},{11,... | collective-permute-start | bytes 786440 | tf_op jit(solution)/shard_map/ppermute | solution.py:647
  59.0 11.1 %collective-permute-start.4 = (bf16[128,1024]{1,0:T(8,128)(2,1)S(1)}, bf16[128,1024]{1,0:T(8,128)(2,1)S(1)}, u32[]{:S(2)}, u32[]{:S(2)}) collective-permute-start(bf16[128,1024]{1,0:T(8,128)(2,1)S(1)} %get-tuple-element.57), channel_id=1, source_target_pairs={{0,1},{1,0},{2,3},{3,2},{4,5},{5,4},{6,7},{7,6},{8,9},{9,8},{10,11... | collective-permute-start | bytes 786440 | tf_op jit(solution)/shard_map/ppermute | solution.py:647
